TPU v7x, 256 devices: a whole 4x4x8 slice. The times are simulated.
256 devices in a mesh: expert: 8 (over z), dp: 32 (over y, x, core).
Axes of the slice: x: 4, y: 4, z: 8, core: 2. Of those that a mesh axis runs over, the one named last changes fastest.
Arguments:
- row_acts: bfloat16 [8, 32768, 2048], P('expert', 'dp'), may hold values from -6 to 6
- row_grads: bfloat16 [8, 32768, 768], P('expert', 'dp'), may hold values from -6 to 6
- grad_factor: bfloat16 [8, 768, 768], P('expert', None, 'dp'), may hold values from -0.21875 to 0.21875
- value_factor: bfloat16 [8, 2048, 768], P('expert', None, 'dp'), may hold values from -0.125 to 0.125
- counts: int32 [8, 32], P('expert', 'dp'), may hold values from 128 to 1024, as said below
- row_token: int32 [8, 32768], P('expert', 'dp'), may hold values from 0 to 2047, as said below
Outputs:
- influence: float32 [65536, 24], P(('expert', 'dp'))
Inputs may be any that keep to these rules, and one draw needn't show every extreme that they name: counts[e, b] slots at the start of each block of 1024 slots are live; some block has all 1024 live. `row_token`: within one block of 1024 slots of one expert the ids are distinct, dead slots included.
All inputs are finite; a program needn't handle non-finite values.
Results may differ from a plain program's by a relative error of at most 0.0003.
Values may be sent and summed in bfloat16 or wider, within the bound.
No kernel may reach another device: no remote copies, remote signals or barrier semaphores. Data moves between devices by JAX's collectives and lax.ppermute only.
A program may use at most 64 MiB of HBM per device.

v0:
```python
import jax
import jax.numpy as jnp
from jax import lax
from jax.sharding import PartitionSpec as P

MODEL = 2048
MOE_FF = 768
RANK = 32
QUERIES = 24
TOK_DEV = 256


epsilon = 1e-06


def local(row_acts, row_grads, grad_factor, value_factor, counts, row_token):
    activ = row_acts[0]
    gradient = row_grads[0]
    acts_proj = jnp.dot(
        activ,
        lax.all_gather(value_factor[0], "dp", axis=1, tiled=True),
        preferred_element_type=jnp.float32,
    )
    grads_proj = jnp.dot(
        gradient,
        lax.all_gather(grad_factor[0], "dp", axis=1, tiled=True),
        preferred_element_type=jnp.float32,
    )
    columns_all = acts_proj.shape[1]
    column_ids = lax.broadcasted_iota(jnp.int32, (columns_all, QUERIES), 0) // RANK
    query_ids = lax.broadcasted_iota(jnp.int32, (columns_all, QUERIES), 1)
    grouping = (column_ids == query_ids).astype(jnp.float32)
    scores = jnp.dot(acts_proj * grads_proj, grouping, precision=lax.Precision.HIGHEST)
    slots = activ.shape[0]
    live = lax.broadcasted_iota(jnp.int32, (slots,), 0) < counts[0, 0]
    norms = jnp.sum(jnp.square(activ.astype(jnp.float32)), 1) * jnp.sum(
        jnp.square(gradient.astype(jnp.float32)), 1
    )
    shard_tokens = TOK_DEV * lax.axis_size("expert")
    owner_grid = lax.broadcasted_iota(jnp.int32, (slots, shard_tokens), 1)
    onehot = ((row_token[0][:, None] == owner_grid) & live[:, None]).astype(jnp.float32)
    contract = (((0,), (0,)), ((), ()))
    dense = lax.dot_general(onehot, scores, contract, precision=lax.Precision.HIGHEST)
    dense_norm = lax.dot_general(onehot, norms[:, None], contract, precision=lax.Precision.HIGHEST)[
        :, 0
    ]
    summed, summed_norm = lax.psum((dense, dense_norm), "expert")
    first = lax.axis_index("expert") * TOK_DEV
    totals = lax.dynamic_slice_in_dim(summed, first, TOK_DEV, 0)
    norm_sum = lax.dynamic_slice_in_dim(summed_norm, first, TOK_DEV, 0)
    factor = lax.rsqrt(norm_sum / (MODEL * MOE_FF) + epsilon) / jnp.sqrt(jnp.float32(RANK))
    return totals * factor[:, None]


def solution(mesh):
    return jax.shard_map(
        local,
        mesh=mesh,
        in_specs=(
            P("expert", "dp", None),
            P("expert", "dp", None),
            P("expert", None, "dp"),
            P("expert", None, "dp"),
            P("expert", "dp"),
            P("expert", "dp"),
        ),
        out_specs=P(("expert", "dp"), None),
        check_vma=False,
    )
```

profile of v0, /device:TPU:1, one launch (start us, length us, event | category | flops | bytes accessed | tf_op | source)
XLA Modules:
  0.0 200.8 jit_solution(17010396526934770541)
XLA Ops:
  6.5 0.0 all-gather.7.cloned.1.call-start
  6.5 0.7 all-gather.7.cloned.1.call-update
  7.3 0.0 all-gather.5.cloned.1.call-start
  7.3 0.7 all-gather.5.cloned.1.call-update
  8.0 0.0 all-reduce.2.cloned.1.call-start
  8.7 1.8 multiply_reduce_fusion.1
  10.5 3.1 %multiply_reduce_fusion = f32[1024]{0:T(1024)S(1)} fusion(bf16[1,1024,2048]{2,1,0:T(8,128)(2,1)} %param.6), kind=kLoop, calls=%fused_computation | loop fusion | flops 6290432 | bytes 4198400 | tf_op jit(solution)/shard_map/reduce_sum | solution.py:36
  13.6 48.6 %all-gather.7.cloned.1.call-done = bf16[1,768,768]{1,2,0:T(8,128)(2,1)} async-done(((bf16[1,768,24]{1,2,0:T(8,128)(2,1)}), bf16[1,768,768]{1,2,0:T(8,128)(2,1)}) %all-gather.7.cloned.1.call-update) | async-done | bytes 1179664 | tf_op jit(solution)/shard_map/all_gather | solution.py:26
  62.2 3.2 %fusion.14 = f32[1024,768]{1,0:T(8,128)S(1)} fusion(bf16[1,1024,768]{2,1,0:T(8,128)(2,1)} %param.7, bf16[1,768,768]{1,2,0:T(8,128)(2,1)} %all-gather.7.cloned.1.call-done), kind=kOutput, calls=%fused_computation.15 | convolution fusion | flops 1207959552 | bytes 5898240 | tf_op jit(solution)/shard_map/dot_general | solution.py:24
  65.4 48.9 %all-gather.5.cloned.1.call-done = bf16[1,2048,768]{1,2,0:T(8,128)(2,1)} async-done(((bf16[1,2048,24]{1,2,0:T(8,128)(2,1)}), bf16[1,2048,768]{1,2,0:T(8,128)(2,1)}) %all-gather.5.cloned.1.call-update) | async-done | bytes 3145744 | tf_op jit(solution)/shard_map/all_gather | solution.py:21
  114.2 6.2 %fusion.5 = f32[1024,768]{1,0:T(8,128)S(1)} fusion(bf16[1,1024,2048]{2,1,0:T(8,128)(2,1)} %param.6, bf16[1,2048,768]{1,2,0:T(8,128)(2,1)} %all-gather.5.cloned.1.call-done), kind=kOutput, calls=%fused_computation.5 | convolution fusion | flops 3221225472 | bytes 10485760 | tf_op jit(solution)/shard_map/dot_general | solution.py:19
  120.4 0.0 copy-start
  120.5 1.8 fusion.12
  122.3 0.0 copy-done
  122.3 3.7 %fusion.3 = f32[2048,24]{0,1:T(8,128)} fusion(f32[1024,24]{1,0:T(8,128)S(1)} %fusion.12, s32[1024]{0:T(1024)S(1)} %bitcast.23, pred[1024]{0:T(1024)(128)(4,1)S(1)} %iota_compare_fusion.3), kind=kOutput, calls=%fused_computation.4 | convolution fusion | flops 608174080 | bytes 300032 | tf_op jit(solution)/shard_map/dot_general | solution.py:43
  126.0 0.0 all-reduce.2.cloned.1.call-update
  126.0 3.0 %fusion.1 = f32[1,2048]{1,0:T(1,128)S(1)} fusion(f32[1024,1]{0,1:T(1,128)S(1)} %bitcast.22, s32[1024]{0:T(1024)S(1)} %bitcast.24, pred[1024]{0:T(1024)(128)(4,1)S(1)} %iota_compare_fusion.3), kind=kOutput, calls=%fused_computation.3 | convolution fusion | flops 29360128 | bytes 17408 | tf_op jit(solution)/shard_map/dot_general | solution.py:44
  129.1 14.1 %psum.15 = f32[2048]{0:T(1024)S(1)} all-reduce(f32[2048]{0:T(1024)S(1)} %bitcast.21), channel_id=1, replica_groups=mesh['expert'=8,'dp'=32] {'expert'}, use_global_device_ids=true, to_apply=%region_3.4 | all-reduce | flops 2048 | bytes 16384 | tf_op jit(solution)/shard_map/psum | solution.py:47
  143.1 0.1 rsqrt_multiply_fusion
  143.2 49.7 %all-reduce.2.cloned.1.call-done = f32[2048,24]{0,1:T(8,128)} async-done(((f32[2048,24]{0,1:T(8,128)}), f32[2048,24]{0,1:T(8,128)}) %all-reduce.2.cloned.1.call-update) | async-done | bytes 196624 | tf_op jit(solution)/shard_map/psum | solution.py:47
  192.9 1.3 dynamic-slice_multiply_fusion
  (4 shorter events, 0.0 us)
Async XLA Ops:
  6.5 55.7 %all-gather.7.cloned.1.call-start = ((), (), s32[]{:S(2)}) async-start(), calls=%async_computation.2 | async-start | bytes 1216512 | tf_op jit(solution)/shard_map/all_gather | solution.py:26
  7.3 107.0 %all-gather.5.cloned.1.call-start = ((), (), s32[]{:S(2)}) async-start(), calls=%async_computation.1 | async-start | bytes 3244032 | tf_op jit(solution)/shard_map/all_gather | solution.py:21
  8.0 184.9 %all-reduce.2.cloned.1.call-start = ((), (), s32[]{:S(2)}) async-start(), calls=%async_computation | async-start | bytes 393216 | tf_op jit(solution)/shard_map/psum | solution.py:47
  120.4 1.8 copy-start
Sparse Core Ops, SparseCore 0:
  10.0 52.1 all-gather.6
  64.8 49.4 all-gather.4
  126.2 66.6 all-reduce.1
where the time goes:
time: 205 us; the launch traced here: 201 us
  waiting for transfers between devices  149 us (73%)
  matrix products  17.9 us (9%)
  blocking collectives  14.1 us (7%)
  between operations  13.8 us (7%)
  other arithmetic  6.31 us (3%)
    psum x1, waiting for transfers between devices, local(): summed, summed_norm = lax.psum((dense, dense_norm), 'expert')  49.7 us
    all_gather x1, waiting for transfers between devices, local(): lax.all_gather(value_factor[0], 'dp', axis=1, tiled=True)  48.9 us
    all_gather x1, waiting for transfers between devices, local(): lax.all_gather(grad_factor[0], 'dp', axis=1, tiled=True)  48.6 us
    psum x1, blocking collectives, local(): summed, summed_norm = lax.psum((dense, dense_norm), 'expert')  14.1 us
    dot_general x1, matrix products, local(): jnp.dot(activ, lax.all_gather(value_factor[0], 'dp', axis=1, tiled=True),...  6.2 us
  transfers between devices with their start and end apart: 3, of which 3 were waited for; matrix products, arithmetic and copies ran while one was open for 6% of the time, Pallas kernels for 0%

commit v1 on v0

v1 whole, which is shorter than its diff:
```python
import jax
import jax.numpy as jnp
from jax import lax
from jax.sharding import PartitionSpec as P

MODEL = 2048
MOE_FF = 768
RANK = 32
QUERIES = 24
TOK_DEV = 256
SIDE = 4
OFFSETS = (0, -1, 1, 2)

epsilon = 1e-06


def place(y, x, core):
    return ((y % SIDE) * SIDE + x % SIDE) * 2 + core


def pairs(step):
    return [
        (place(y, x, core), place(*step(y, x, core)))
        for y in range(SIDE)
        for x in range(SIDE)
        for core in range(2)
    ]


def first_axis(shift):
    return pairs(lambda y, x, core: (y, x + shift, 0) if core == 0 else (y + shift, x, 1))


def second_axis(shift):
    return pairs(lambda y, x, core: (y + shift, x, 0) if core == 0 else (y, x + shift, 1))


SIBLING = pairs(lambda y, x, core: (y, x, 1 - core))


def slot_queries(per_device):
    me = lax.axis_index("dp")
    my_core, my_x, my_y = me % 2, (me // 2) % SIDE, me // (2 * SIDE)
    offsets = jnp.array(OFFSETS, jnp.int32)
    second = offsets[:, None, None, None]
    core = jnp.stack([my_core, 1 - my_core])[None, :, None, None]
    first = offsets[None, None, :, None]
    x = (my_x + jnp.where(core == 0, first, second)) % SIDE
    y = (my_y + jnp.where(core == 0, second, first)) % SIDE
    lane = lax.broadcasted_iota(jnp.int32, (1, 1, 1, per_device), 3)
    column = ((y * SIDE + x) * 2 + core) * per_device + lane
    return column.reshape(-1) // RANK


def gather(shard):
    send = lambda value, table: lax.ppermute(value, "dp", table)
    line = [shard] + [send(shard, first_axis(-d)) for d in OFFSETS[1:]]
    line = jnp.concatenate(line, 0)
    mine = [line] + [send(line, second_axis(-d)) for d in OFFSETS[1:]]
    theirs = [send(block, SIBLING) for block in mine]
    return jnp.concatenate([block for pair in zip(mine, theirs) for block in pair], 0)


def local(row_acts, row_grads, grad_factor, value_factor, counts, row_token):
    activ = row_acts[0]
    gradient = row_grads[0]
    shard = jnp.concatenate([value_factor[0].T, grad_factor[0].T], 1)
    factors = gather(shard)
    contract = (((1,), (1,)), ((), ()))
    acts_proj = lax.dot_general(
        factors[:, :MODEL], activ, contract, preferred_element_type=jnp.float32
    )
    grads_proj = lax.dot_general(
        factors[:, MODEL:], gradient, contract, preferred_element_type=jnp.float32
    )
    queries = slot_queries(shard.shape[0])
    query_ids = lax.broadcasted_iota(jnp.int32, (QUERIES, queries.shape[0]), 0)
    grouping = (query_ids == queries[None, :]).astype(jnp.float32)
    scores = jnp.dot(grouping, acts_proj * grads_proj, precision=lax.Precision.HIGHEST)
    slots = activ.shape[0]
    live = lax.broadcasted_iota(jnp.int32, (slots,), 0) < counts[0, 0]
    norms = jnp.sum(jnp.square(activ.astype(jnp.float32)), 1) * jnp.sum(
        jnp.square(gradient.astype(jnp.float32)), 1
    )
    experts = lax.axis_size("expert")
    shard_tokens = TOK_DEV * experts
    owner_grid = lax.broadcasted_iota(jnp.int32, (slots, shard_tokens), 1)
    onehot = ((row_token[0][:, None] == owner_grid) & live[:, None]).astype(jnp.float32)
    table = jnp.concatenate([scores, norms[None, :]], 0)
    dense = jnp.dot(table, onehot, precision=lax.Precision.HIGHEST)
    dense = dense.reshape(QUERIES + 1, experts, TOK_DEV).transpose(1, 0, 2)
    summed = lax.all_to_all(dense, "expert", 0, 0).sum(0)
    totals, norm_sum = summed[:QUERIES], summed[QUERIES]
    factor = lax.rsqrt(norm_sum / (MODEL * MOE_FF) + epsilon) / jnp.sqrt(jnp.float32(RANK))
    return (totals * factor[None, :]).T


def solution(mesh):
    return jax.shard_map(
        local,
        mesh=mesh,
        in_specs=(
            P("expert", "dp", None),
            P("expert", "dp", None),
            P("expert", None, "dp"),
            P("expert", None, "dp"),
            P("expert", "dp"),
            P("expert", "dp"),
        ),
        out_specs=P(("expert", "dp"), None),
        check_vma=False,
    )
```

time: 205 us -> 63.6 us (0.31); the launches traced: 201 us -> 63.3 us
  waiting for transfers between devices: 149 us -> 13.9 us
  between operations: 13.8 us -> 0.9 us
  starting transfers between devices: 0.08 us -> 12.5 us
  matrix products: 17.9 us -> 9.48 us
  blocking collectives: 14.1 us -> 18.3 us
    all_gather x2 -> x0, waiting for transfers between devices: 97.5 us -> none  [the longest x1 48.9 us: local(): lax.all_gather(value_factor[0], 'dp', axis=1, tiled=True)]
    psum x1 -> x0, waiting for transfers between devices: 49.7 us -> none  [local(): summed, summed_norm = lax.psum((dense, dense_norm), 'expert')]
    all_to_all x0 -> x1, blocking collectives: none -> 18.3 us  [local(): summed = lax.all_to_all(dense, 'expert', 0, 0).sum(0)]
    psum x1 -> x0, blocking collectives: 14.1 us -> none  [local(): summed, summed_norm = lax.psum((dense, dense_norm), 'expert')]
    ppermute x0 -> x10, waiting for transfers between devices: none -> 13.9 us  [gather(): send = lambda value, table: lax.ppermute(value, 'dp', table)]
    ppermute x0 -> x10, starting transfers between devices: none -> 12.5 us  [gather(): send = lambda value, table: lax.ppermute(value, 'dp', table)]
    dot_general x5 -> x4, matrix products: 17.9 us -> 9.48 us  [the longest x1 3.43 us: local(): lax.dot_general(factors[:, :MODEL], activ, contract, preferred_element_ty...]
  transfers between devices with their start and end apart: 3 -> 10, of which waited for: 3 -> 4; matrix products, arithmetic and copies ran while one was open for 6% -> 8% of each run, Pallas kernels for 0% -> 0%
where the time goes in v1:
time: 63.6 us; the launch traced here: 63.3 us
  blocking collectives  18.3 us (29%)
  waiting for transfers between devices  13.9 us (22%)
  starting transfers between devices  12.5 us (20%)
  matrix products  9.48 us (15%)
  other arithmetic  6.98 us (11%)
  local copies, waits for them, and re-layouts  1.34 us (2%)
  between operations  0.9 us (1%)
    all_to_all x1, blocking collectives, local(): summed = lax.all_to_all(dense, 'expert', 0, 0).sum(0)  18.3 us
    ppermute x10, waiting for transfers between devices, gather(): send = lambda value, table: lax.ppermute(value, 'dp', table)  13.9 us
    ppermute x10, starting transfers between devices, gather(): send = lambda value, table: lax.ppermute(value, 'dp', table)  12.5 us
    dot_general x1, matrix products, local(): lax.dot_general(factors[:, :MODEL], activ, contract, preferred_element_ty...  3.43 us
    dot_general x1, matrix products, local(): dense = jnp.dot(table, onehot, precision=lax.Precision.HIGHEST)  3.41 us
    reduce_sum x1, other arithmetic, local(): jnp.sum(jnp.square(activ.astype(jnp.float32)), 1)  3.22 us
    concatenate x1, other arithmetic, local(): shard = jnp.concatenate([value_factor[0].T, grad_factor[0].T], 1)  1.7 us
    dot_general x1, matrix products, local(): lax.dot_general(factors[:, MODEL:], gradient, contract, preferred_element...  1.41 us
  transfers between devices with their start and end apart: 10, of which 4 were waited for; matrix products, arithmetic and copies ran while one was open for 8% of the time, Pallas kernels for 0%

profile of v1, /device:TPU:1, one launch (start us, length us, event | category | flops | bytes accessed | tf_op | source)
XLA Modules:
  0.0 63.3 jit_solution(16753584526728430209)
XLA Ops:
  0.0 1.7 %pad_maximum_fusion.1 = (bf16[24,2816]{1,0:T(8,128)(2,1)S(1)}, bf16[768,2816]{1,0:T(8,128)(2,1)}) fusion(bf16[24,768]{1,0:T(8,128)(2,1)} %bitcast.34, bf16[24,2048]{1,0:T(8,128)(2,1)} %bitcast.31), kind=kLoop, calls=%fused_computation.17 | loop fusion | flops 270335 | bytes 405504 | tf_op jit(solution)/shard_map/concatenate | solution.py:67
  1.7 2.1 %collective-permute-start = (bf16[24,2816]{1,0:T(8,128)(2,1)S(1)}, bf16[24,2816]{1,0:T(8,128)(2,1)S(1)}, u32[]{:S(2)}, u32[]{:S(2)}) collective-permute-start(bf16[24,2816]{1,0:T(8,128)(2,1)S(1)} %get-tuple-element.7), channel_id=1, source_target_pairs={{0,2},{1,9},{2,4},{3,11},{4,6},{5,13},{6,0},{7,15},{8,10},{9,17},{... | collective-permute-start | bytes 405512 | tf_op jit(solution)/shard_map/ppermute | solution.py:56
  3.8 1.4 %collective-permute-start.1 = (bf16[24,2816]{1,0:T(8,128)(2,1)S(1)}, bf16[24,2816]{1,0:T(8,128)(2,1)S(1)}, u32[]{:S(2)}, u32[]{:S(2)}) collective-permute-start(bf16[24,2816]{1,0:T(8,128)(2,1)S(1)} %get-tuple-element.7), channel_id=1, source_target_pairs={{0,6},{1,25},{2,0},{3,27},{4,2},{5,29},{6,4},{7,31},{8,14},{9,1},{... | collective-permute-start | bytes 405512 | tf_op jit(solution)/shard_map/ppermute | solution.py:56
  5.3 1.6 %collective-permute-start.2 = (bf16[24,2816]{1,0:T(8,128)(2,1)S(1)}, bf16[24,2816]{1,0:T(8,128)(2,1)S(1)}, u32[]{:S(2)}, u32[]{:S(2)}) collective-permute-start(bf16[24,2816]{1,0:T(8,128)(2,1)S(1)} %get-tuple-element.7), channel_id=1, source_target_pairs={{0,4},{1,17},{2,6},{3,19},{4,0},{5,21},{6,2},{7,23},{8,12},{9,25},... | collective-permute-start | bytes 405512 | tf_op jit(solution)/shard_map/ppermute | solution.py:56
  7.0 0.8 %add_multiply_fusion = s32[4,2,4]{2,1,0:T(2,128)S(1)} fusion(pred[2]{0:T(512)(128)(4,1)S(1)} %get-tuple-element.5, s32[2]{0:T(128)S(1)} %get-tuple-element.6, s32[]{:T(128)S(6)} %select_n.70, s32[4]{0:T(128)} %constant.92.clone, s32[]{:T(128)S(6)} %select_n.65), kind=kLoop, calls=%fused_computation.54 | loop fusion | flops 992 | bytes 162 | tf_op jit(solution)/shard_map/mul | solution.py:51
  7.9 0.1 add.119
  8.0 3.2 %multiply_reduce_fusion = f32[1024]{0:T(1024)S(1)} fusion(bf16[1,1024,2048]{2,1,0:T(8,128)(2,1)} %param.7), kind=kLoop, calls=%fused_computation.1 | loop fusion | flops 6290432 | bytes 4198400 | tf_op jit(solution)/shard_map/reduce_sum | solution.py:82
  11.3 0.4 multiply_reduce_fusion.1
  12.4 2.4 %collective-permute-start.3 = (bf16[96,2816]{1,0:T(8,128)(2,1)S(1)}, bf16[96,2816]{1,0:T(8,128)(2,1)S(1)}, u32[]{:S(2)}, u32[]{:S(2)}) collective-permute-start(bf16[96,2816]{1,0:T(8,128)(2,1)S(1)} %pad_maximum_fusion), channel_id=1, source_target_pairs={{0,1},{1,0},{2,3},{3,2},{4,5},{5,4},{6,7},{7,6},{8,9},{9,8},{10,11... | collective-permute-start | bytes 1622024 | tf_op jit(solution)/shard_map/ppermute | solution.py:56
  14.8 2.7 %collective-permute-start.6 = (bf16[96,2816]{1,0:T(8,128)(2,1)S(1)}, bf16[96,2816]{1,0:T(8,128)(2,1)S(1)}, u32[]{:S(2)}, u32[]{:S(2)}) collective-permute-start(bf16[96,2816]{1,0:T(8,128)(2,1)S(1)} %pad_maximum_fusion), channel_id=1, source_target_pairs={{0,24},{1,7},{2,26},{3,1},{4,28},{5,3},{6,30},{7,5},{8,0},{9,15},{... | collective-permute-start | bytes 1622024 | tf_op jit(solution)/shard_map/ppermute | solution.py:56
  17.5 1.0 %collective-permute-start.8 = (bf16[96,2816]{1,0:T(8,128)(2,1)S(1)}, bf16[96,2816]{1,0:T(8,128)(2,1)S(1)}, u32[]{:S(2)}, u32[]{:S(2)}) collective-permute-start(bf16[96,2816]{1,0:T(8,128)(2,1)S(1)} %pad_maximum_fusion), channel_id=1, source_target_pairs={{0,16},{1,5},{2,18},{3,7},{4,20},{5,1},{6,22},{7,3},{8,24},{9,13},... | collective-permute-start | bytes 1622024 | tf_op jit(solution)/shard_map/ppermute | solution.py:56
  18.5 11.8 %collective-permute-done.4 = bf16[96,2816]{1,0:T(8,128)(2,1)S(1)} collective-permute-done((bf16[96,2816]{1,0:T(8,128)(2,1)S(1)}, bf16[96,2816]{1,0:T(8,128)(2,1)S(1)}, u32[]{:S(2)}, u32[]{:S(2)}) %collective-permute-start.4) | collective-permute-done | bytes 540704 | tf_op jit(solution)/shard_map/ppermute | solution.py:56
  30.4 0.5 collective-permute-start.7
  30.9 0.7 %collective-permute-start.9 = (bf16[96,2816]{1,0:T(8,128)(2,1)S(1)}, bf16[96,2816]{1,0:T(8,128)(2,1)S(1)}, u32[]{:S(2)}, u32[]{:S(2)}) collective-permute-start(bf16[96,2816]{1,0:T(8,128)(2,1)S(1)} %collective-permute-done.8), channel_id=1, source_target_pairs={{0,1},{1,0},{2,3},{3,2},{4,5},{5,4},{6,7},{7,6},{8,9},{9,8},{10,11... | collective-permute-start | bytes 1622024 | tf_op jit(solution)/shard_map/ppermute | solution.py:56
  31.6 0.7 %collective-permute-done.5 = bf16[96,2816]{1,0:T(8,128)(2,1)S(1)} collective-permute-done((bf16[96,2816]{1,0:T(8,128)(2,1)S(1)}, bf16[96,2816]{1,0:T(8,128)(2,1)S(1)}, u32[]{:S(2)}, u32[]{:S(2)}) %collective-permute-start.5) | collective-permute-done | bytes 540704 | tf_op jit(solution)/shard_map/ppermute | solution.py:56
  32.4 0.7 %collective-permute-done.7 = bf16[96,2816]{1,0:T(8,128)(2,1)S(1)} collective-permute-done((bf16[96,2816]{1,0:T(8,128)(2,1)S(1)}, bf16[96,2816]{1,0:T(8,128)(2,1)S(1)}, u32[]{:S(2)}, u32[]{:S(2)}) %collective-permute-start.7) | collective-permute-done | bytes 540704 | tf_op jit(solution)/shard_map/ppermute | solution.py:56
  33.1 0.7 %collective-permute-done.9 = bf16[96,2816]{1,0:T(8,128)(2,1)S(1)} collective-permute-done((bf16[96,2816]{1,0:T(8,128)(2,1)S(1)}, bf16[96,2816]{1,0:T(8,128)(2,1)S(1)}, u32[]{:S(2)}, u32[]{:S(2)}) %collective-permute-start.9) | collective-permute-done | bytes 540704 | tf_op jit(solution)/shard_map/ppermute | solution.py:56
  33.9 1.4 %fusion.10 = f32[768,1024]{1,0:T(8,128)S(1)} fusion(bf16[1,1024,768]{2,1,0:T(8,128)(2,1)S(1)} %copy-done.1, bf16[768,2816]{1,0:T(8,128)(2,1)S(1)} %constant_dynamic-update-slice_fusion), kind=kOutput, calls=%fused_computation.12 | convolution fusion | flops 1207959552 | bytes 5898240 | tf_op jit(solution)/shard_map/dot_general | solution.py:73
  35.3 0.8 %copy-done = bf16[1,1024,2048]{2,1,0:T(8,128)(2,1)S(1)} copy-done((bf16[1,1024,2048]{2,1,0:T(8,128)(2,1)S(1)}, bf16[1,1024,2048]{2,1,0:T(8,128)(2,1)}, u32[]{:S(2)}) %copy-start) | copy-done | bytes 4194328
  36.1 3.4 %fusion.3 = f32[768,1024]{1,0:T(8,128)S(1)} fusion(bf16[1,1024,2048]{2,1,0:T(8,128)(2,1)S(1)} %copy-done, bf16[768,2816]{1,0:T(8,128)(2,1)S(1)} %constant_dynamic-update-slice_fusion), kind=kOutput, calls=%fused_computation.4 | convolution fusion | flops 3221225472 | bytes 10485760 | tf_op jit(solution)/shard_map/dot_general | solution.py:70
  39.5 1.2 %fusion.8 = f32[24,1024]{1,0:T(8,128)S(1)} fusion(f32[768,1024]{1,0:T(8,128)S(1)} %fusion.3, f32[768,1024]{1,0:T(8,128)S(1)} %fusion.10, s32[768]{0:T(1024)S(1)} %add_select_fusion), kind=kOutput, calls=%fused_computation.10 | convolution fusion | flops 227297280 | bytes 6392832 | tf_op jit(solution)/shard_map/dot_general | solution.py:79
  40.8 3.4 %fusion.1 = f32[25,2048]{1,0:T(8,128)S(1)} fusion(s32[1024]{0:T(1024)S(1)} %bitcast.38, pred[1024]{0:T(1024)(128)(4,1)S(1)} %iota_compare_fusion.3, f32[1,1024]{1,0:T(1,128)S(1)} %bitcast.36, f32[24,1024]{1,0:T(8,128)S(1)} %fusion.8), kind=kOutput, calls=%fused_computation.3 | convolution fusion | flops 633365504 | bytes 312320 | tf_op jit(solution)/shard_map/dot_general | solution.py:90
  44.4 18.3 %all_to_all.5 = f32[8,25,256]{2,1,0:T(8,128)S(1)} all-to-all(f32[8,25,256]{2,1,0:T(8,128)S(1)} %bitcast.29), channel_id=1, replica_groups=mesh['expert'=8,'dp'=32] {'expert'}, dimensions={0} | all-to-all | bytes 409600 | tf_op jit(solution)/shard_map/all_to_all | solution.py:92
  62.7 0.6 fusion.17
  (40 shorter events, 0.8 us)
Async XLA Ops:
  0.0 12.3 %copy-start.2 = (bf16[1,2048,24]{1,2,0:T(8,128)(2,1)S(1)}, bf16[1,2048,24]{1,2,0:T(8,128)(2,1)}, u32[]{:S(2)}) copy-start(bf16[1,2048,24]{1,2,0:T(8,128)(2,1)} %param.10) | copy-start | bytes 294916
  0.0 12.4 %copy-start.3 = (bf16[1,768,24]{1,2,0:T(8,128)(2,1)S(1)}, bf16[1,768,24]{1,2,0:T(8,128)(2,1)}, u32[]{:S(2)}) copy-start(bf16[1,768,24]{1,2,0:T(8,128)(2,1)} %param.9) | copy-start | bytes 110596
  0.0 11.2 %copy-start.1 = (bf16[1,1024,768]{2,1,0:T(8,128)(2,1)S(1)}, bf16[1,1024,768]{2,1,0:T(8,128)(2,1)}, u32[]{:S(2)}) copy-start(bf16[1,1024,768]{2,1,0:T(8,128)(2,1)} %param.8) | copy-start | bytes 4718596
  1.7 10.6 %collective-permute-start = (bf16[24,2816]{1,0:T(8,128)(2,1)S(1)}, bf16[24,2816]{1,0:T(8,128)(2,1)S(1)}, u32[]{:S(2)}, u32[]{:S(2)}) collective-permute-start(bf16[24,2816]{1,0:T(8,128)(2,1)S(1)} %get-tuple-element.7), channel_id=1, source_target_pairs={{0,2},{1,9},{2,4},{3,11},{4,6},{5,13},{6,0},{7,15},{8,10},{9,17},{... | collective-permute-start | bytes 405512 | tf_op jit(solution)/shard_map/ppermute | solution.py:56
  3.8 8.5 %collective-permute-start.1 = (bf16[24,2816]{1,0:T(8,128)(2,1)S(1)}, bf16[24,2816]{1,0:T(8,128)(2,1)S(1)}, u32[]{:S(2)}, u32[]{:S(2)}) collective-permute-start(bf16[24,2816]{1,0:T(8,128)(2,1)S(1)} %get-tuple-element.7), channel_id=1, source_target_pairs={{0,6},{1,25},{2,0},{3,27},{4,2},{5,29},{6,4},{7,31},{8,14},{9,1},{... | collective-permute-start | bytes 405512 | tf_op jit(solution)/shard_map/ppermute | solution.py:56
  5.3 7.1 %collective-permute-start.2 = (bf16[24,2816]{1,0:T(8,128)(2,1)S(1)}, bf16[24,2816]{1,0:T(8,128)(2,1)S(1)}, u32[]{:S(2)}, u32[]{:S(2)}) collective-permute-start(bf16[24,2816]{1,0:T(8,128)(2,1)S(1)} %get-tuple-element.7), channel_id=1, source_target_pairs={{0,4},{1,17},{2,6},{3,19},{4,0},{5,21},{6,2},{7,23},{8,12},{9,25},... | collective-permute-start | bytes 405512 | tf_op jit(solution)/shard_map/ppermute | solution.py:56
  8.0 10.5 %copy-start.4 = (bf16[768,2816]{1,0:T(8,128)(2,1)S(1)}, bf16[768,2816]{1,0:T(8,128)(2,1)}, u32[]{:S(2)}) copy-start(bf16[768,2816]{1,0:T(8,128)(2,1)} %get-tuple-element.8) | copy-start | bytes 12976132
  12.4 19.1 %collective-permute-start.3 = (bf16[96,2816]{1,0:T(8,128)(2,1)S(1)}, bf16[96,2816]{1,0:T(8,128)(2,1)S(1)}, u32[]{:S(2)}, u32[]{:S(2)}) collective-permute-start(bf16[96,2816]{1,0:T(8,128)(2,1)S(1)} %pad_maximum_fusion), channel_id=1, source_target_pairs={{0,1},{1,0},{2,3},{3,2},{4,5},{5,4},{6,7},{7,6},{8,9},{9,8},{10,11... | collective-permute-start | bytes 1622024 | tf_op jit(solution)/shard_map/ppermute | solution.py:56
  14.8 15.5 %collective-permute-start.4 = (bf16[96,2816]{1,0:T(8,128)(2,1)S(1)}, bf16[96,2816]{1,0:T(8,128)(2,1)S(1)}, u32[]{:S(2)}, u32[]{:S(2)}) collective-permute-start(bf16[96,2816]{1,0:T(8,128)(2,1)S(1)} %pad_maximum_fusion), channel_id=1, source_target_pairs={{0,8},{1,3},{2,10},{3,5},{4,12},{5,7},{6,14},{7,1},{8,16},{9,11},{... | collective-permute-start | bytes 1622024 | tf_op jit(solution)/shard_map/ppermute | solution.py:56
  14.8 15.5 %collective-permute-start.6 = (bf16[96,2816]{1,0:T(8,128)(2,1)S(1)}, bf16[96,2816]{1,0:T(8,128)(2,1)S(1)}, u32[]{:S(2)}, u32[]{:S(2)}) collective-permute-start(bf16[96,2816]{1,0:T(8,128)(2,1)S(1)} %pad_maximum_fusion), channel_id=1, source_target_pairs={{0,24},{1,7},{2,26},{3,1},{4,28},{5,3},{6,30},{7,5},{8,0},{9,15},{... | collective-permute-start | bytes 1622024 | tf_op jit(solution)/shard_map/ppermute | solution.py:56
  17.5 13.4 %collective-permute-start.8 = (bf16[96,2816]{1,0:T(8,128)(2,1)S(1)}, bf16[96,2816]{1,0:T(8,128)(2,1)S(1)}, u32[]{:S(2)}, u32[]{:S(2)}) collective-permute-start(bf16[96,2816]{1,0:T(8,128)(2,1)S(1)} %pad_maximum_fusion), channel_id=1, source_target_pairs={{0,16},{1,5},{2,18},{3,7},{4,20},{5,1},{6,22},{7,3},{8,24},{9,13},... | collective-permute-start | bytes 1622024 | tf_op jit(solution)/shard_map/ppermute | solution.py:56
  30.4 1.9 %collective-permute-start.5 = (bf16[96,2816]{1,0:T(8,128)(2,1)S(1)}, bf16[96,2816]{1,0:T(8,128)(2,1)S(1)}, u32[]{:S(2)}, u32[]{:S(2)}) collective-permute-start(bf16[96,2816]{1,0:T(8,128)(2,1)S(1)} %collective-permute-done.4), channel_id=1, source_target_pairs={{0,1},{1,0},{2,3},{3,2},{4,5},{5,4},{6,7},{7,6},{8,9},{9,8},{10,11... | collective-permute-start | bytes 1622024 | tf_op jit(solution)/shard_map/ppermute | solution.py:56
  30.4 2.7 %collective-permute-start.7 = (bf16[96,2816]{1,0:T(8,128)(2,1)S(1)}, bf16[96,2816]{1,0:T(8,128)(2,1)S(1)}, u32[]{:S(2)}, u32[]{:S(2)}) collective-permute-start(bf16[96,2816]{1,0:T(8,128)(2,1)S(1)} %collective-permute-done.6), channel_id=1, source_target_pairs={{0,1},{1,0},{2,3},{3,2},{4,5},{5,4},{6,7},{7,6},{8,9},{9,8},{10,11... | collective-permute-start | bytes 1622024 | tf_op jit(solution)/shard_map/ppermute | solution.py:56
  30.9 3.0 %collective-permute-start.9 = (bf16[96,2816]{1,0:T(8,128)(2,1)S(1)}, bf16[96,2816]{1,0:T(8,128)(2,1)S(1)}, u32[]{:S(2)}, u32[]{:S(2)}) collective-permute-start(bf16[96,2816]{1,0:T(8,128)(2,1)S(1)} %collective-permute-done.8), channel_id=1, source_target_pairs={{0,1},{1,0},{2,3},{3,2},{4,5},{5,4},{6,7},{7,6},{8,9},{9,8},{10,11... | collective-permute-start | bytes 1622024 | tf_op jit(solution)/shard_map/ppermute | solution.py:56
  33.9 2.2 %copy-start = (bf16[1,1024,2048]{2,1,0:T(8,128)(2,1)S(1)}, bf16[1,1024,2048]{2,1,0:T(8,128)(2,1)}, u32[]{:S(2)}) copy-start(bf16[1,1024,2048]{2,1,0:T(8,128)(2,1)} %param.7) | copy-start | bytes 12582916
  39.5 1.2 %copy-start.5 = (s32[1,1024]{1,0:T(1,128)S(1)}, s32[1,1024]{1,0:T(1,128)}, u32[]{:S(2)}) copy-start(s32[1,1024]{1,0:T(1,128)} %param.12) | copy-start | bytes 12292

commit v2 on v1

v2 whole, which is shorter than its diff:
```python
import functools

import jax
import jax.numpy as jnp
from jax import lax
from jax.experimental import pallas as pl
from jax.experimental.pallas import tpu as pltpu
from jax.sharding import PartitionSpec as P

MODEL = 2048
MOE_FF = 768
RANK = 32
QUERIES = 24
TOK_DEV = 256
SIDE = 4
OFFSETS = (0, -1, 1, 2)
ROW_TILE = 256

epsilon = 1e-06

CONTRACT_LAST = (((1,), (1,)), ((), ()))
VMEM = pl.BlockSpec(memory_space=pltpu.VMEM)


def place(y, x, core):
    return ((y % SIDE) * SIDE + x % SIDE) * 2 + core


def pairs(step):
    return [
        (place(y, x, core), place(*step(y, x, core)))
        for y in range(SIDE)
        for x in range(SIDE)
        for core in range(2)
    ]


def first_axis(shift):
    return pairs(lambda y, x, core: (y, x + shift, 0) if core == 0 else (y + shift, x, 1))


def second_axis(shift):
    return pairs(lambda y, x, core: (y + shift, x, 0) if core == 0 else (y, x + shift, 1))


SIBLING = pairs(lambda y, x, core: (y, x, 1 - core))


def send(value, table):
    return lax.ppermute(value, "dp", table)


def slot_queries(per_device):
    me = lax.axis_index("dp")
    core, my_x, my_y = me % 2, (me // 2) % SIDE, me // (2 * SIDE)
    slots = SIDE * SIDE * per_device
    slot = lax.broadcasted_iota(jnp.int32, (QUERIES, slots), 1)
    piece = slot // per_device
    offset = lambda i: jnp.where(i == 1, SIDE - 1, jnp.where(i == 0, 0, i - 1))
    first, second = offset(piece % SIDE), offset(piece // SIDE)
    x = (my_x + jnp.where(core == 0, first, second)) % SIDE
    y = (my_y + jnp.where(core == 0, second, first)) % SIDE
    column = ((y * SIDE + x) * 2 + core) * per_device + slot % per_device
    return column // RANK


def split(value, terms):
    parts = []
    for _ in range(terms):
        part = value.astype(jnp.bfloat16)
        parts.append(part)
        value = value - part.astype(jnp.float32)
    return parts


def scores_kernel(acts, grads, w0, w1, w2, w3, grouping, out, factors):
    width = w0.shape[0]
    for i, w in enumerate((w0, w1, w2, w3)):
        factors[i * width : (i + 1) * width, :] = w[...]
    dot = functools.partial(
        lax.dot_general, dimension_numbers=CONTRACT_LAST, preferred_element_type=jnp.float32
    )
    for start in range(0, acts.shape[0], ROW_TILE):
        rows = slice(start, start + ROW_TILE)
        product = dot(factors[:, :MODEL], acts[rows, :]) * dot(factors[:, MODEL:], grads[rows, :])
        high, low = split(product, 2)
        out[:, rows] = jnp.dot(
            grouping[...], high, preferred_element_type=jnp.float32
        ) + jnp.dot(grouping[...], low, preferred_element_type=jnp.float32)


def row_scores(acts, grads, pieces, grouping):
    rows = acts.shape[0]
    slots = 4 * pieces[0].shape[0]
    return pl.pallas_call(
        scores_kernel,
        out_shape=jax.ShapeDtypeStruct((QUERIES, rows), jnp.float32),
        in_specs=[VMEM] * 7,
        out_specs=VMEM,
        scratch_shapes=[pltpu.VMEM((slots, MODEL + MOE_FF), jnp.bfloat16)],
        compiler_params=pltpu.CompilerParams(vmem_limit_bytes=24 << 20),
        cost_estimate=pl.CostEstimate(
            flops=2 * rows * slots * (MODEL + MOE_FF), bytes_accessed=8 << 20, transcendentals=0
        ),
        name="row_scores",
    )(acts, grads, *pieces, grouping)


def owners_kernel(tokens, norms, onehot, dense):
    owner = lax.broadcasted_iota(jnp.int32, (TOK_DEV, tokens.shape[1]), 0)
    high, middle, low = split(norms[...], 3)
    for start in range(0, onehot.shape[0], TOK_DEV):
        hot = (owner + start == tokens[...]).astype(jnp.float32).astype(jnp.bfloat16)
        onehot[start : start + TOK_DEV, :] = hot
        part = [
            lax.dot_general(
                jnp.broadcast_to(term, (8, term.shape[1])),
                hot,
                CONTRACT_LAST,
                preferred_element_type=jnp.float32,
            )
            for term in (high, middle, low)
        ]
        dense[:, start : start + TOK_DEV] = part[0] + part[1] + part[2]


def owners(tokens, norms, shard_tokens):
    rows = tokens.shape[1]
    return pl.pallas_call(
        owners_kernel,
        out_shape=(
            jax.ShapeDtypeStruct((shard_tokens, rows), jnp.bfloat16),
            jax.ShapeDtypeStruct((8, shard_tokens), jnp.float32),
        ),
        in_specs=[VMEM] * 2,
        out_specs=(VMEM, VMEM),
        compiler_params=pltpu.CompilerParams(vmem_limit_bytes=16 << 20),
        cost_estimate=pl.CostEstimate(
            flops=2 * rows * shard_tokens * 128, bytes_accessed=8 << 20, transcendentals=0
        ),
        name="owners",
    )(tokens, norms)


def scatter_kernel(mine, theirs, onehot, dense_norm, out):
    table = jnp.concatenate(split(mine[...] + theirs[...], 3), 0)
    for i in range(out.shape[0]):
        owned = slice(i * TOK_DEV, (i + 1) * TOK_DEV)
        part = lax.dot_general(
            table, onehot[owned, :], CONTRACT_LAST, preferred_element_type=jnp.float32
        )
        out[i, :QUERIES, :] = (
            part[:QUERIES] + part[QUERIES : 2 * QUERIES] + part[2 * QUERIES :]
        )
        out[i, QUERIES:, :] = dense_norm[:1, owned]


def scatter(mine, theirs, onehot, dense_norm):
    shard_tokens = onehot.shape[0]
    return pl.pallas_call(
        scatter_kernel,
        out_shape=jax.ShapeDtypeStruct(
            (shard_tokens // TOK_DEV, QUERIES + 1, TOK_DEV), jnp.float32
        ),
        in_specs=[VMEM] * 4,
        out_specs=VMEM,
        compiler_params=pltpu.CompilerParams(vmem_limit_bytes=16 << 20),
        name="scatter",
    )(mine, theirs, onehot, dense_norm)


def local(row_acts, row_grads, grad_factor, value_factor, counts, row_token):
    acts, grads = row_acts[0], row_grads[0]
    experts = lax.axis_size("expert")
    shard = jnp.concatenate([value_factor[0].T, grad_factor[0].T], 1)
    line = [shard] + [send(shard, first_axis(-d)) for d in OFFSETS[1:]]
    their_acts, their_grads = send(acts, SIBLING), send(grads, SIBLING)
    line = jnp.concatenate(line, 0)
    line, late_acts, late_grads, tokens = lax.optimization_barrier((line, acts, grads, row_token))
    pieces = [line] + [send(line, second_axis(-d)) for d in OFFSETS[1:]]
    slots = acts.shape[0]
    live = lax.broadcasted_iota(jnp.int32, (1, slots), 1) < counts[0, 0]
    norms = jnp.sum(jnp.square(late_acts.astype(jnp.float32)), 1) * jnp.sum(
        jnp.square(late_grads.astype(jnp.float32)), 1
    )
    onehot, dense_norm = owners(
        jnp.where(live, tokens, -1), norms[None, :], TOK_DEV * experts
    )
    queries = slot_queries(shard.shape[0])
    query_ids = lax.broadcasted_iota(jnp.int32, queries.shape, 0)
    grouping = (query_ids == queries).astype(jnp.bfloat16)
    for_them = row_scores(their_acts, their_grads, pieces, grouping)
    theirs = send(for_them, SIBLING)
    mine = row_scores(acts, grads, pieces, grouping)
    dense = scatter(mine, theirs, onehot, dense_norm)
    summed = lax.all_to_all(dense, "expert", 0, 0).sum(0)
    totals, norm_sum = summed[:QUERIES], summed[QUERIES]
    factor = lax.rsqrt(norm_sum / (MODEL * MOE_FF) + epsilon) / jnp.sqrt(jnp.float32(RANK))
    return (totals * factor[None, :]).T


def solution(mesh):
    return jax.shard_map(
        local,
        mesh=mesh,
        in_specs=(
            P("expert", "dp", None),
            P("expert", "dp", None),
            P("expert", None, "dp"),
            P("expert", None, "dp"),
            P("expert", "dp"),
            P("expert", "dp"),
        ),
        out_specs=P(("expert", "dp"), None),
        check_vma=False,
    )
```

time: 63.6 us -> 64.6 us (1.016)
  Pallas kernels: 0 us -> 15.8 us
  matrix products: 9.48 us -> 0 us
  waiting for transfers between devices: 13.9 us -> 9.72 us
  blocking collectives: 18.3 us -> 19.8 us
  local copies, waits for them, and re-layouts: 1.34 us -> 0.3 us
  other arithmetic: 6.98 us -> 6.06 us
  starting transfers between devices: 12.5 us -> 11.8 us
    pallas_call x0 -> x4, Pallas kernels: none -> 15.8 us  [the longest x2 10.8 us: row_scores(): pl.pallas_call(scores_kernel, out_shape=jax.ShapeDtypeStruct((QUERIES, ro...]
    dot_general x4 -> x0, matrix products: 9.48 us -> none  [the longest x1 3.43 us: local(): lax.dot_general(factors[:, :MODEL], activ, contract, preferred_element_ty...]
    ppermute x10 -> x9, waiting for transfers between devices: 13.9 us -> 9.72 us  [send(): return lax.ppermute(value, 'dp', table)]
    all_to_all x1, blocking collectives: 18.3 us -> 19.8 us  [local(): summed = lax.all_to_all(dense, 'expert', 0, 0).sum(0)]
    concatenate x1, other arithmetic: 0.05 us -> 0.95 us  [local(): line = jnp.concatenate(line, 0)]
    unnamed x22 -> x6, local copies, waits for them, and re-layouts: 1.13 us -> 0.3 us
    mul x2 -> x1, other arithmetic: 0.82 us -> 0.01 us  [local(): jnp.sum(jnp.square(late_acts.astype(jnp.float32)), 1)]
    concatenate x1, other arithmetic: 1.7 us -> 0.92 us  [local(): shard = jnp.concatenate([value_factor[0].T, grad_factor[0].T], 1)]
  transfers between devices with their start and end apart: 10 -> 9, of which waited for: 4 -> 4; matrix products, arithmetic and copies ran while one was open for 8% -> 8% of each run, Pallas kernels for 0% -> 12%
where the time goes in v2:
time: 64.6 us; the launch traced here: 64.3 us
  blocking collectives  19.8 us (31%)
  Pallas kernels  15.8 us (24%)
  starting transfers between devices  11.8 us (18%)
  waiting for transfers between devices  9.72 us (15%)
  other arithmetic  6.06 us (9%)
  between operations  0.79 us (1%)
    all_to_all x1, blocking collectives, local(): summed = lax.all_to_all(dense, 'expert', 0, 0).sum(0)  19.8 us
    ppermute x9, starting transfers between devices, send(): return lax.ppermute(value, 'dp', table)  11.8 us
    pallas_call x2, Pallas kernels, row_scores(): pl.pallas_call(scores_kernel, out_shape=jax.ShapeDtypeStruct((QUERIES, ro...  10.8 us
    ppermute x9, waiting for transfers between devices, send(): return lax.ppermute(value, 'dp', table)  9.72 us
    pallas_call x1, Pallas kernels, owners(): pl.pallas_call(owners_kernel, out_shape=(jax.ShapeDtypeStruct((shard_toke...  3.57 us
    reduce_sum x1, other arithmetic, local(): jnp.sum(jnp.square(late_acts.astype(jnp.float32)), 1)  3.07 us
    pallas_call x1, Pallas kernels, scatter(): pl.pallas_call(scatter_kernel, out_shape=jax.ShapeDtypeStruct((shard_toke...  1.41 us
  transfers between devices with their start and end apart: 9, of which 4 were waited for; matrix products, arithmetic and copies ran while one was open for 8% of the time, Pallas kernels for 12%

profile of v2, /device:TPU:1, one launch (start us, length us, event | category | flops | bytes accessed | tf_op | source)
XLA Modules:
  0.0 64.3 jit_solution(6254078142681486449)
XLA Ops:
  0.0 3.2 %collective-permute-start.6 = (bf16[1024,2048]{1,0:T(8,128)(2,1)}, bf16[1024,2048]{1,0:T(8,128)(2,1)}, u32[]{:S(2)}, u32[]{:S(2)}) collective-permute-start(bf16[1024,2048]{1,0:T(8,128)(2,1)} %bitcast.14), channel_id=1, source_target_pairs={{0,1},{1,0},{2,3},{3,2},{4,5},{5,4},{6,7},{7,6},{8,9},{9,8},{10,11... | collective-permute-start | bytes 12582920 | tf_op jit(solution)/shard_map/ppermute | solution.py:50
  3.2 0.9 %pad_maximum_fusion.1 = bf16[24,2816]{1,0:T(8,128)(2,1)S(1)} fusion(bf16[24,768]{1,0:T(8,128)(2,1)} %bitcast.23, bf16[24,2048]{1,0:T(8,128)(2,1)} %bitcast.21), kind=kLoop, calls=%fused_computation.3 | loop fusion | flops 270336 | bytes 270336 | tf_op jit(solution)/shard_map/concatenate | solution.py:175
  4.2 0.1 collective-permute-start
  4.3 2.7 %collective-permute-start.1 = (bf16[24,2816]{1,0:T(8,128)(2,1)S(1)}, bf16[24,2816]{1,0:T(8,128)(2,1)S(1)}, u32[]{:S(2)}, u32[]{:S(2)}) collective-permute-start(bf16[24,2816]{1,0:T(8,128)(2,1)S(1)} %pad_maximum_fusion.1), channel_id=1, source_target_pairs={{0,6},{1,25},{2,0},{3,27},{4,2},{5,29},{6,4},{7,31},{8,14},{9,1},{... | collective-permute-start | bytes 405512 | tf_op jit(solution)/shard_map/ppermute | solution.py:50
  6.9 0.6 collective-permute-start.7
  8.3 0.1 fusion.15.grouping
  8.3 1.3 %collective-permute-done = bf16[24,2816]{1,0:T(8,128)(2,1)S(1)} collective-permute-done((bf16[24,2816]{1,0:T(8,128)(2,1)S(1)}, bf16[24,2816]{1,0:T(8,128)(2,1)S(1)}, u32[]{:S(2)}, u32[]{:S(2)}) %collective-permute-start) | collective-permute-done | bytes 135200 | tf_op jit(solution)/shard_map/ppermute | solution.py:50
  9.6 0.7 %collective-permute-done.1 = bf16[24,2816]{1,0:T(8,128)(2,1)S(1)} collective-permute-done((bf16[24,2816]{1,0:T(8,128)(2,1)S(1)}, bf16[24,2816]{1,0:T(8,128)(2,1)S(1)}, u32[]{:S(2)}, u32[]{:S(2)}) %collective-permute-start.1) | collective-permute-done | bytes 135200 | tf_op jit(solution)/shard_map/ppermute | solution.py:50
  10.3 2.3 %collective-permute-done.2 = bf16[24,2816]{1,0:T(8,128)(2,1)S(1)} collective-permute-done((bf16[24,2816]{1,0:T(8,128)(2,1)S(1)}, bf16[24,2816]{1,0:T(8,128)(2,1)S(1)}, u32[]{:S(2)}, u32[]{:S(2)}) %collective-permute-start.2) | collective-permute-done | bytes 135200 | tf_op jit(solution)/shard_map/ppermute | solution.py:50
  12.6 1.0 %pad_maximum_fusion.w0 = bf16[96,2816]{1,0:T(8,128)(2,1)S(1)} fusion(bf16[24,2816]{1,0:T(8,128)(2,1)S(1)} %collective-permute-done.2, bf16[24,2816]{1,0:T(8,128)(2,1)S(1)} %collective-permute-done.1, bf16[24,2816]{1,0:T(8,128)(2,1)S(1)} %collective-permute-done, bf16[24,768]{1,0:T(8,128)(2,1)} %bitcast.24, bf16[24,2048]{1,0:T(8,128)(2,1)} %bitcast.22), kind=kLoop, calls=%fused_computation.2 | loop fusion | flops 2703360 | bytes 1081344 | tf_op jit(solution)/shard_map/concatenate | solution.py:178
  13.6 0.1 collective-permute-start.3
  13.6 2.7 %collective-permute-start.4 = (bf16[96,2816]{1,0:T(8,128)(2,1)S(1)}, bf16[96,2816]{1,0:T(8,128)(2,1)S(1)}, u32[]{:S(2)}, u32[]{:S(2)}) collective-permute-start(bf16[96,2816]{1,0:T(8,128)(2,1)S(1)} %pad_maximum_fusion.w0), channel_id=1, source_target_pairs={{0,24},{1,7},{2,26},{3,1},{4,28},{5,3},{6,30},{7,5},{8,0},{9,15},{... | collective-permute-start | bytes 1622024 | tf_op jit(solution)/shard_map/ppermute | solution.py:50
  16.3 3.1 %multiply_reduce_fusion = f32[1024]{0:T(1024)S(1)} fusion(bf16[1024,2048]{1,0:T(8,128)(2,1)} %bitcast.15), kind=kLoop, calls=%fused_computation | loop fusion | flops 6290432 | bytes 4198400 | tf_op jit(solution)/shard_map/reduce_sum | solution.py:183
  19.4 0.0 copy-start.2
  19.4 0.4 multiply_reduce_fusion.1
  19.8 0.3 copy-done.2
  20.1 3.6 %owners.1 = (bf16[2048,1024]{1,0:T(8,128)(2,1)S(1)}, f32[8,2048]{1,0:T(8,128)S(1)}) custom-call(s32[1,1024]{1,0:T(1,128)S(1)} %compare_select_fusion.tokens, f32[1,1024]{1,0:T(1,128)S(1)} %bitcast.20), custom_call_target="tpu_custom_call" | custom-call | flops 536870912 | bytes 8388608 | tf_op jit(solution)/shard_map/owners/pallas_call | solution.py:129
  23.7 5.5 %collective-permute-done.3.w1 = bf16[96,2816]{1,0:T(8,128)(2,1)S(1)} collective-permute-done((bf16[96,2816]{1,0:T(8,128)(2,1)S(1)}, bf16[96,2816]{1,0:T(8,128)(2,1)S(1)}, u32[]{:S(2)}, u32[]{:S(2)}) %collective-permute-start.3) | collective-permute-done | bytes 540704 | tf_op jit(solution)/shard_map/ppermute | solution.py:50
  29.2 6.5 %row_scores.3 = f32[24,1024]{1,0:T(8,128)S(1)} custom-call(bf16[1024,2048]{1,0:T(8,128)(2,1)} %collective-permute-done.6.acts, bf16[1024,768]{1,0:T(8,128)(2,1)S(1)} %collective-permute-done.7.grads, bf16[96,2816]{1,0:T(8,128)(2,1)S(1)} %pad_maximum_fusion.w0, bf16[96,2816]{1,0:T(8,128)(2,1)S(1)} %collective-permute-done.3.w1, ...), custom_call_target="tpu_custom_call" | custom-call | flops 2214592512 | bytes 8388608 | tf_op jit(solution)/shard_map/row_scores/pallas_call | solution.py:95
  35.7 2.4 %collective-permute-start.8 = (f32[24,1024]{1,0:T(8,128)S(1)}, f32[24,1024]{1,0:T(8,128)S(1)}, u32[]{:S(2)}, u32[]{:S(2)}) collective-permute-start(f32[24,1024]{1,0:T(8,128)S(1)} %row_scores.3), channel_id=1, source_target_pairs={{0,1},{1,0},{2,3},{3,2},{4,5},{5,4},{6,7},{7,6},{8,9},{9,8},{10,11... | collective-permute-start | bytes 294920 | tf_op jit(solution)/shard_map/ppermute | solution.py:50
  38.1 4.3 %row_scores.2.mine = f32[24,1024]{1,0:T(8,128)S(1)} custom-call(bf16[1024,2048]{1,0:T(8,128)(2,1)S(1)} %bitcast.16, bf16[1024,768]{1,0:T(8,128)(2,1)S(1)} %bitcast.19, bf16[96,2816]{1,0:T(8,128)(2,1)S(1)} %pad_maximum_fusion.w0, bf16[96,2816]{1,0:T(8,128)(2,1)S(1)} %collective-permute-done.3.w1, bf16[96,2816]{1,0:T(8,128)(2,1)S(1)} %collective-permute-done.4.w2, ...), custom_call_target="tpu_custom_call" | custom-call | flops 2214592512 | bytes 8388608 | tf_op jit(solution)/shard_map/row_scores/pallas_call | solution.py:95
  42.4 1.4 %scatter.1 = f32[8,25,256]{2,1,0:T(8,128)S(1)} custom-call(f32[24,1024]{1,0:T(8,128)S(1)} %row_scores.2.mine, f32[24,1024]{1,0:T(8,128)S(1)} %collective-permute-done.8.theirs, bf16[2048,1024]{1,0:T(8,128)(2,1)S(1)} %get-tuple-element.15.onehot, f32[8,2048]{1,0:T(8,128)S(1)} %get-tuple-element.16.dense_norm), custom_call_target="tpu_custom_call" | custom-call | tf_op jit(solution)/shard_map/scatter/pallas_call | solution.py:160
  43.8 19.8 %all_to_all.5 = f32[8,25,256]{2,1,0:T(8,128)S(1)} all-to-all(f32[8,25,256]{2,1,0:T(8,128)S(1)} %scatter.1), channel_id=1, replica_groups=mesh['expert'=8,'dp'=32] {'expert'}, dimensions={0} | all-to-all | bytes 409600 | tf_op jit(solution)/shard_map/all_to_all | solution.py:196
  63.7 0.6 fusion.16
  (18 shorter events, 0.1 us)
Async XLA Ops:
  0.0 29.2 %collective-permute-start.6 = (bf16[1024,2048]{1,0:T(8,128)(2,1)}, bf16[1024,2048]{1,0:T(8,128)(2,1)}, u32[]{:S(2)}, u32[]{:S(2)}) collective-permute-start(bf16[1024,2048]{1,0:T(8,128)(2,1)} %bitcast.14), channel_id=1, source_target_pairs={{0,1},{1,0},{2,3},{3,2},{4,5},{5,4},{6,7},{7,6},{8,9},{9,8},{10,11... | collective-permute-start | bytes 12582920 | tf_op jit(solution)/shard_map/ppermute | solution.py:50
  4.2 5.4 %collective-permute-start = (bf16[24,2816]{1,0:T(8,128)(2,1)S(1)}, bf16[24,2816]{1,0:T(8,128)(2,1)S(1)}, u32[]{:S(2)}, u32[]{:S(2)}) collective-permute-start(bf16[24,2816]{1,0:T(8,128)(2,1)S(1)} %pad_maximum_fusion.1), channel_id=1, source_target_pairs={{0,2},{1,9},{2,4},{3,11},{4,6},{5,13},{6,0},{7,15},{8,10},{9,17},{... | collective-permute-start | bytes 405512 | tf_op jit(solution)/shard_map/ppermute | solution.py:50
  4.3 6.1 %collective-permute-start.1 = (bf16[24,2816]{1,0:T(8,128)(2,1)S(1)}, bf16[24,2816]{1,0:T(8,128)(2,1)S(1)}, u32[]{:S(2)}, u32[]{:S(2)}) collective-permute-start(bf16[24,2816]{1,0:T(8,128)(2,1)S(1)} %pad_maximum_fusion.1), channel_id=1, source_target_pairs={{0,6},{1,25},{2,0},{3,27},{4,2},{5,29},{6,4},{7,31},{8,14},{9,1},{... | collective-permute-start | bytes 405512 | tf_op jit(solution)/shard_map/ppermute | solution.py:50
  6.9 5.7 %collective-permute-start.2 = (bf16[24,2816]{1,0:T(8,128)(2,1)S(1)}, bf16[24,2816]{1,0:T(8,128)(2,1)S(1)}, u32[]{:S(2)}, u32[]{:S(2)}) collective-permute-start(bf16[24,2816]{1,0:T(8,128)(2,1)S(1)} %pad_maximum_fusion.1), channel_id=1, source_target_pairs={{0,4},{1,17},{2,6},{3,19},{4,0},{5,21},{6,2},{7,23},{8,12},{9,25},... | collective-permute-start | bytes 405512 | tf_op jit(solution)/shard_map/ppermute | solution.py:50
  6.9 22.2 %collective-permute-start.7 = (bf16[1024,768]{1,0:T(8,128)(2,1)}, bf16[1024,768]{1,0:T(8,128)(2,1)S(1)}, u32[]{:S(2)}, u32[]{:S(2)}) collective-permute-start(bf16[1024,768]{1,0:T(8,128)(2,1)} %bitcast.17), channel_id=1, source_target_pairs={{0,1},{1,0},{2,3},{3,2},{4,5},{5,4},{6,7},{7,6},{8,9},{9,8},{10,11... | collective-permute-start | bytes 4718600 | tf_op jit(solution)/shard_map/ppermute | solution.py:50
  13.5 5.8 %copy-start.1 = (bf16[1,1024,768]{2,1,0:T(8,128)(2,1)S(1)}, bf16[1,1024,768]{2,1,0:T(8,128)(2,1)}, u32[]{:S(2)}) copy-start(bf16[1,1024,768]{2,1,0:T(8,128)(2,1)} %param.7) | copy-start | bytes 4718596
  13.6 15.6 %collective-permute-start.3 = (bf16[96,2816]{1,0:T(8,128)(2,1)S(1)}, bf16[96,2816]{1,0:T(8,128)(2,1)S(1)}, u32[]{:S(2)}, u32[]{:S(2)}) collective-permute-start(bf16[96,2816]{1,0:T(8,128)(2,1)S(1)} %pad_maximum_fusion.w0), channel_id=1, source_target_pairs={{0,8},{1,3},{2,10},{3,5},{4,12},{5,7},{6,14},{7,1},{8,16},{9,11},{... | collective-permute-start | bytes 1622024 | tf_op jit(solution)/shard_map/ppermute | solution.py:50
  13.6 15.5 %collective-permute-start.4 = (bf16[96,2816]{1,0:T(8,128)(2,1)S(1)}, bf16[96,2816]{1,0:T(8,128)(2,1)S(1)}, u32[]{:S(2)}, u32[]{:S(2)}) collective-permute-start(bf16[96,2816]{1,0:T(8,128)(2,1)S(1)} %pad_maximum_fusion.w0), channel_id=1, source_target_pairs={{0,24},{1,7},{2,26},{3,1},{4,28},{5,3},{6,30},{7,5},{8,0},{9,15},{... | collective-permute-start | bytes 1622024 | tf_op jit(solution)/shard_map/ppermute | solution.py:50
  16.3 12.8 %collective-permute-start.5 = (bf16[96,2816]{1,0:T(8,128)(2,1)S(1)}, bf16[96,2816]{1,0:T(8,128)(2,1)S(1)}, u32[]{:S(2)}, u32[]{:S(2)}) collective-permute-start(bf16[96,2816]{1,0:T(8,128)(2,1)S(1)} %pad_maximum_fusion.w0), channel_id=1, source_target_pairs={{0,16},{1,5},{2,18},{3,7},{4,20},{5,1},{6,22},{7,3},{8,24},{9,13},... | collective-permute-start | bytes 1622024 | tf_op jit(solution)/shard_map/ppermute | solution.py:50
  19.4 0.7 %copy-start.2 = (s32[1,1024]{1,0:T(1,128)S(1)}, s32[1,1024]{1,0:T(1,128)}, u32[]{:S(2)}) copy-start(s32[1,1024]{1,0:T(1,128)} %param.11) | copy-start | bytes 12292
  23.7 14.4 %copy-start = (bf16[1,1024,2048]{2,1,0:T(8,128)(2,1)S(1)}, bf16[1,1024,2048]{2,1,0:T(8,128)(2,1)}, u32[]{:S(2)}) copy-start(bf16[1,1024,2048]{2,1,0:T(8,128)(2,1)} %param.6) | copy-start | bytes 12582916
  35.7 6.8 %collective-permute-start.8 = (f32[24,1024]{1,0:T(8,128)S(1)}, f32[24,1024]{1,0:T(8,128)S(1)}, u32[]{:S(2)}, u32[]{:S(2)}) collective-permute-start(f32[24,1024]{1,0:T(8,128)S(1)} %row_scores.3), channel_id=1, source_target_pairs={{0,1},{1,0},{2,3},{3,2},{4,5},{5,4},{6,7},{7,6},{8,9},{9,8},{10,11... | collective-permute-start | bytes 294920 | tf_op jit(solution)/shard_map/ppermute | solution.py:50

commit v3 on v2

--- a/solution.py
+++ b/solution.py
@@ -14,7 +14,7 @@
 TOK_DEV = 256
 SIDE = 4
 OFFSETS = (0, -1, 1, 2)
-ROW_TILE = 256
+HALF = TOK_DEV // 2
 
 epsilon = 1e-06
 
@@ -52,16 +52,17 @@
 
 def slot_queries(per_device):
     me = lax.axis_index("dp")
-    core, my_x, my_y = me % 2, (me // 2) % SIDE, me // (2 * SIDE)
+    core, my_x, my_y = me & 1, (me >> 1) & (SIDE - 1), me >> 3
     slots = SIDE * SIDE * per_device
     slot = lax.broadcasted_iota(jnp.int32, (QUERIES, slots), 1)
-    piece = slot // per_device
+    piece = (slot * (65536 // per_device + 1)) >> 16
     offset = lambda i: jnp.where(i == 1, SIDE - 1, jnp.where(i == 0, 0, i - 1))
-    first, second = offset(piece % SIDE), offset(piece // SIDE)
-    x = (my_x + jnp.where(core == 0, first, second)) % SIDE
-    y = (my_y + jnp.where(core == 0, second, first)) % SIDE
-    column = ((y * SIDE + x) * 2 + core) * per_device + slot % per_device
-    return column // RANK
+    first, second = offset(piece & (SIDE - 1)), offset(piece >> 2)
+    swapped = (first - second) * core
+    x = (my_x + first - swapped) & (SIDE - 1)
+    y = (my_y + second + swapped) & (SIDE - 1)
+    column = ((y * SIDE + x) * 2 + core) * per_device + slot - piece * per_device
+    return column >> 5
 
 
 def split(value, terms):
@@ -73,6 +74,24 @@
     return parts
 
 
+def line_kernel(own, before, after, across, out):
+    width = own.shape[0]
+    for i, shard in enumerate((own, before, after, across)):
+        out[i * width : (i + 1) * width, :] = shard[...]
+
+
+def join(shards):
+    width, depth = shards[0].shape
+    return pl.pallas_call(
+        line_kernel,
+        out_shape=jax.ShapeDtypeStruct((len(shards) * width, depth), shards[0].dtype),
+        in_specs=[VMEM] * len(shards),
+        out_specs=VMEM,
+        compiler_params=pltpu.CompilerParams(vmem_limit_bytes=1 << 20),
+        name="line",
+    )(*shards)
+
+
 def scores_kernel(acts, grads, w0, w1, w2, w3, grouping, out, factors):
     width = w0.shape[0]
     for i, w in enumerate((w0, w1, w2, w3)):
@@ -80,13 +99,11 @@
     dot = functools.partial(
         lax.dot_general, dimension_numbers=CONTRACT_LAST, preferred_element_type=jnp.float32
     )
-    for start in range(0, acts.shape[0], ROW_TILE):
-        rows = slice(start, start + ROW_TILE)
-        product = dot(factors[:, :MODEL], acts[rows, :]) * dot(factors[:, MODEL:], grads[rows, :])
-        high, low = split(product, 2)
-        out[:, rows] = jnp.dot(
-            grouping[...], high, preferred_element_type=jnp.float32
-        ) + jnp.dot(grouping[...], low, preferred_element_type=jnp.float32)
+    product = dot(factors[:, :MODEL], acts[...]) * dot(factors[:, MODEL:], grads[...])
+    high, low = split(product, 2)
+    out[...] = jnp.dot(grouping[...], high, preferred_element_type=jnp.float32) + jnp.dot(
+        grouping[...], low, preferred_element_type=jnp.float32
+    )
 
 
 def row_scores(acts, grads, pieces, grouping):
@@ -98,7 +115,7 @@
         in_specs=[VMEM] * 7,
         out_specs=VMEM,
         scratch_shapes=[pltpu.VMEM((slots, MODEL + MOE_FF), jnp.bfloat16)],
-        compiler_params=pltpu.CompilerParams(vmem_limit_bytes=24 << 20),
+        compiler_params=pltpu.CompilerParams(vmem_limit_bytes=4 << 20),
         cost_estimate=pl.CostEstimate(
             flops=2 * rows * slots * (MODEL + MOE_FF), bytes_accessed=8 << 20, transcendentals=0
         ),
@@ -106,7 +123,10 @@
     )(acts, grads, *pieces, grouping)
 
 
-def owners_kernel(tokens, norms, onehot, dense):
+def owners_kernel(tokens, norms, onehot, dense, grouping):
+    queries = slot_queries(grouping.shape[1] // (SIDE * SIDE))
+    query_ids = lax.broadcasted_iota(jnp.int32, queries.shape, 0)
+    grouping[...] = (query_ids == queries).astype(jnp.float32).astype(jnp.bfloat16)
     owner = lax.broadcasted_iota(jnp.int32, (TOK_DEV, tokens.shape[1]), 0)
     high, middle, low = split(norms[...], 3)
     for start in range(0, onehot.shape[0], TOK_DEV):
@@ -124,17 +144,18 @@
         dense[:, start : start + TOK_DEV] = part[0] + part[1] + part[2]
 
 
-def owners(tokens, norms, shard_tokens):
+def owners(tokens, norms, shard_tokens, slots):
     rows = tokens.shape[1]
     return pl.pallas_call(
         owners_kernel,
         out_shape=(
             jax.ShapeDtypeStruct((shard_tokens, rows), jnp.bfloat16),
             jax.ShapeDtypeStruct((8, shard_tokens), jnp.float32),
+            jax.ShapeDtypeStruct((QUERIES, slots), jnp.bfloat16),
         ),
         in_specs=[VMEM] * 2,
-        out_specs=(VMEM, VMEM),
-        compiler_params=pltpu.CompilerParams(vmem_limit_bytes=16 << 20),
+        out_specs=(VMEM, VMEM, VMEM),
+        compiler_params=pltpu.CompilerParams(vmem_limit_bytes=3 << 20),
         cost_estimate=pl.CostEstimate(
             flops=2 * rows * shard_tokens * 128, bytes_accessed=8 << 20, transcendentals=0
         ),
@@ -149,10 +170,13 @@
         part = lax.dot_general(
             table, onehot[owned, :], CONTRACT_LAST, preferred_element_type=jnp.float32
         )
-        out[i, :QUERIES, :] = (
-            part[:QUERIES] + part[QUERIES : 2 * QUERIES] + part[2 * QUERIES :]
-        )
-        out[i, QUERIES:, :] = dense_norm[:1, owned]
+        part = part[:QUERIES] + part[QUERIES : 2 * QUERIES] + part[2 * QUERIES :]
+        for half in range(2):
+            lanes = slice(half * HALF, (half + 1) * HALF)
+            out[i, half * QUERIES : (half + 1) * QUERIES, :] = part[:, lanes]
+            out[i, 2 * QUERIES + half : 2 * QUERIES + half + 1, :] = dense_norm[
+                :1, i * TOK_DEV + half * HALF : i * TOK_DEV + (half + 1) * HALF
+            ]
 
 
 def scatter(mine, theirs, onehot, dense_norm):
@@ -160,11 +184,11 @@
     return pl.pallas_call(
         scatter_kernel,
         out_shape=jax.ShapeDtypeStruct(
-            (shard_tokens // TOK_DEV, QUERIES + 1, TOK_DEV), jnp.float32
+            (shard_tokens // TOK_DEV, 2 * QUERIES + 2, HALF), jnp.float32
         ),
         in_specs=[VMEM] * 4,
         out_specs=VMEM,
-        compiler_params=pltpu.CompilerParams(vmem_limit_bytes=16 << 20),
+        compiler_params=pltpu.CompilerParams(vmem_limit_bytes=2 << 20),
         name="scatter",
     )(mine, theirs, onehot, dense_norm)
 
@@ -175,28 +199,28 @@
     shard = jnp.concatenate([value_factor[0].T, grad_factor[0].T], 1)
     line = [shard] + [send(shard, first_axis(-d)) for d in OFFSETS[1:]]
     their_acts, their_grads = send(acts, SIBLING), send(grads, SIBLING)
-    line = jnp.concatenate(line, 0)
-    line, late_acts, late_grads, tokens = lax.optimization_barrier((line, acts, grads, row_token))
+    line = join(line)
+    line, tokens = lax.optimization_barrier((line, row_token))
     pieces = [line] + [send(line, second_axis(-d)) for d in OFFSETS[1:]]
     slots = acts.shape[0]
     live = lax.broadcasted_iota(jnp.int32, (1, slots), 1) < counts[0, 0]
-    norms = jnp.sum(jnp.square(late_acts.astype(jnp.float32)), 1) * jnp.sum(
-        jnp.square(late_grads.astype(jnp.float32)), 1
-    )
-    onehot, dense_norm = owners(
-        jnp.where(live, tokens, -1), norms[None, :], TOK_DEV * experts
-    )
-    queries = slot_queries(shard.shape[0])
-    query_ids = lax.broadcasted_iota(jnp.int32, queries.shape, 0)
-    grouping = (query_ids == queries).astype(jnp.bfloat16)
+    norms = jnp.sum(jnp.square(acts.astype(jnp.float32)), 1) * jnp.sum(
+        jnp.square(grads.astype(jnp.float32)), 1
+    )
+    onehot, dense_norm, grouping = owners(
+        jnp.where(live, tokens, -1),
+        norms[None, :],
+        TOK_DEV * experts,
+        SIDE * SIDE * shard.shape[0],
+    )
     for_them = row_scores(their_acts, their_grads, pieces, grouping)
     theirs = send(for_them, SIBLING)
     mine = row_scores(acts, grads, pieces, grouping)
     dense = scatter(mine, theirs, onehot, dense_norm)
     summed = lax.all_to_all(dense, "expert", 0, 0).sum(0)
-    totals, norm_sum = summed[:QUERIES], summed[QUERIES]
+    totals, norm_sum = summed[: 2 * QUERIES].reshape(2, QUERIES, HALF), summed[2 * QUERIES :]
     factor = lax.rsqrt(norm_sum / (MODEL * MOE_FF) + epsilon) / jnp.sqrt(jnp.float32(RANK))
-    return (totals * factor[None, :]).T
+    return (totals * factor[:, None, :]).transpose(0, 2, 1).reshape(TOK_DEV, QUERIES)
 
 
 def solution(mesh):

time: 64.6 us -> 58.1 us (0.90)
  Pallas kernels: 15.8 us -> 10.4 us
  starting transfers between devices: 11.8 us -> 13.3 us
  other arithmetic: 6.06 us -> 5.02 us
  waiting for transfers between devices: 9.72 us -> 8.84 us
    pallas_call x2, Pallas kernels: 10.8 us -> 5.36 us  [row_scores(): pl.pallas_call(scores_kernel, out_shape=jax.ShapeDtypeStruct((QUERIES, ro...]
    ppermute x9, starting transfers between devices: 11.8 us -> 13.3 us  [send(): return lax.ppermute(value, 'dp', table)]
    concatenate x1 -> x0, other arithmetic: 0.95 us -> none  [local(): line = jnp.concatenate(line, 0)]
    ppermute x9, waiting for transfers between devices: 9.72 us -> 8.84 us  [send(): return lax.ppermute(value, 'dp', table)]
  transfers between devices with their start and end apart: 9 -> 9, of which waited for: 4 -> 5; matrix products, arithmetic and copies ran while one was open for 8% -> 8% of each run, Pallas kernels for 12% -> 11%
where the time goes in v3:
time: 58.1 us; the launch traced here: 57.9 us
  blocking collectives  19.6 us (34%)
  starting transfers between devices  13.3 us (23%)
  Pallas kernels  10.4 us (18%)
  waiting for transfers between devices  8.84 us (15%)
  other arithmetic  5.02 us (9%)
  between operations  0.74 us (1%)
    all_to_all x1, blocking collectives, local(): summed = lax.all_to_all(dense, 'expert', 0, 0).sum(0)  19.6 us
    ppermute x9, starting transfers between devices, send(): return lax.ppermute(value, 'dp', table)  13.3 us
    ppermute x9, waiting for transfers between devices, send(): return lax.ppermute(value, 'dp', table)  8.84 us
    pallas_call x2, Pallas kernels, row_scores(): pl.pallas_call(scores_kernel, out_shape=jax.ShapeDtypeStruct((QUERIES, ro...  5.36 us
    pallas_call x1, Pallas kernels, owners(): pl.pallas_call(owners_kernel, out_shape=(jax.ShapeDtypeStruct((shard_toke...  3.56 us
    reduce_sum x1, other arithmetic, local(): jnp.sum(jnp.square(acts.astype(jnp.float32)), 1)  3.07 us
    pallas_call x1, Pallas kernels, scatter(): pl.pallas_call(scatter_kernel, out_shape=jax.ShapeDtypeStruct((shard_toke...  1.42 us
  transfers between devices with their start and end apart: 9, of which 5 were waited for; matrix products, arithmetic and copies ran while one was open for 8% of the time, Pallas kernels for 11%

profile of v3, /device:TPU:1, one launch (start us, length us, event | category | flops | bytes accessed | tf_op | source)
XLA Modules:
  0.0 57.9 jit_solution(7932382100186014644)
XLA Ops:
  0.0 3.2 %collective-permute-start.6 = (bf16[1024,2048]{1,0:T(8,128)(2,1)}, bf16[1024,2048]{1,0:T(8,128)(2,1)S(1)}, u32[]{:S(2)}, u32[]{:S(2)}) collective-permute-start(bf16[1024,2048]{1,0:T(8,128)(2,1)} %bitcast.20), channel_id=1, source_target_pairs={{0,1},{1,0},{2,3},{3,2},{4,5},{5,4},{6,7},{7,6},{8,9},{9,8},{10,11... | collective-permute-start | bytes 12582920 | tf_op jit(solution)/shard_map/ppermute | solution.py:50
  3.2 0.0 collective-permute-start.7
  3.2 0.9 %pad_maximum_fusion.own = bf16[24,2816]{1,0:T(8,128)(2,1)S(1)} fusion(bf16[24,768]{1,0:T(8,128)(2,1)} %bitcast.27, bf16[24,2048]{1,0:T(8,128)(2,1)} %bitcast.25), kind=kLoop, calls=%fused_computation.2 | loop fusion | flops 270336 | bytes 270336 | tf_op jit(solution)/shard_map/concatenate | solution.py:199
  4.2 1.4 %collective-permute-start.2 = (bf16[24,2816]{1,0:T(8,128)(2,1)S(1)}, bf16[24,2816]{1,0:T(8,128)(2,1)S(1)}, u32[]{:S(2)}, u32[]{:S(2)}) collective-permute-start(bf16[24,2816]{1,0:T(8,128)(2,1)S(1)} %pad_maximum_fusion.own), channel_id=1, source_target_pairs={{0,4},{1,17},{2,6},{3,19},{4,0},{5,21},{6,2},{7,23},{8,12},{9,25},... | collective-permute-start | bytes 405512 | tf_op jit(solution)/shard_map/ppermute | solution.py:50
  5.5 0.8 %collective-permute-start.1 = (bf16[24,2816]{1,0:T(8,128)(2,1)S(1)}, bf16[24,2816]{1,0:T(8,128)(2,1)S(1)}, u32[]{:S(2)}, u32[]{:S(2)}) collective-permute-start(bf16[24,2816]{1,0:T(8,128)(2,1)S(1)} %pad_maximum_fusion.own), channel_id=1, source_target_pairs={{0,6},{1,25},{2,0},{3,27},{4,2},{5,29},{6,4},{7,31},{8,14},{9,1},{... | collective-permute-start | bytes 405512 | tf_op jit(solution)/shard_map/ppermute | solution.py:50
  6.3 0.7 %collective-permute-start = (bf16[24,2816]{1,0:T(8,128)(2,1)S(1)}, bf16[24,2816]{1,0:T(8,128)(2,1)S(1)}, u32[]{:S(2)}, u32[]{:S(2)}) collective-permute-start(bf16[24,2816]{1,0:T(8,128)(2,1)S(1)} %pad_maximum_fusion.own), channel_id=1, source_target_pairs={{0,2},{1,9},{2,4},{3,11},{4,6},{5,13},{6,0},{7,15},{8,10},{9,17},{... | collective-permute-start | bytes 405512 | tf_op jit(solution)/shard_map/ppermute | solution.py:50
  7.0 2.9 %collective-permute-done.2.across = bf16[24,2816]{1,0:T(8,128)(2,1)S(1)} collective-permute-done((bf16[24,2816]{1,0:T(8,128)(2,1)S(1)}, bf16[24,2816]{1,0:T(8,128)(2,1)S(1)}, u32[]{:S(2)}, u32[]{:S(2)}) %collective-permute-start.2) | collective-permute-done | bytes 135200 | tf_op jit(solution)/shard_map/ppermute | solution.py:50
  9.9 0.1 collective-permute-done.1.after
  10.1 1.6 %collective-permute-done.before = bf16[24,2816]{1,0:T(8,128)(2,1)S(1)} collective-permute-done((bf16[24,2816]{1,0:T(8,128)(2,1)S(1)}, bf16[24,2816]{1,0:T(8,128)(2,1)S(1)}, u32[]{:S(2)}, u32[]{:S(2)}) %collective-permute-start) | collective-permute-done | bytes 135200 | tf_op jit(solution)/shard_map/ppermute | solution.py:50
  11.7 2.5 %collective-permute-start.5 = (bf16[96,2816]{1,0:T(8,128)(2,1)S(1)}, bf16[96,2816]{1,0:T(8,128)(2,1)S(1)}, u32[]{:S(2)}, u32[]{:S(2)}) collective-permute-start(bf16[96,2816]{1,0:T(8,128)(2,1)S(1)} %line.1.w0), channel_id=1, source_target_pairs={{0,16},{1,5},{2,18},{3,7},{4,20},{5,1},{6,22},{7,3},{8,24},{9,13},... | collective-permute-start | bytes 1622024 | tf_op jit(solution)/shard_map/ppermute | solution.py:50
  14.3 0.9 %collective-permute-start.4 = (bf16[96,2816]{1,0:T(8,128)(2,1)S(1)}, bf16[96,2816]{1,0:T(8,128)(2,1)S(1)}, u32[]{:S(2)}, u32[]{:S(2)}) collective-permute-start(bf16[96,2816]{1,0:T(8,128)(2,1)S(1)} %line.1.w0), channel_id=1, source_target_pairs={{0,24},{1,7},{2,26},{3,1},{4,28},{5,3},{6,30},{7,5},{8,0},{9,15},{... | collective-permute-start | bytes 1622024 | tf_op jit(solution)/shard_map/ppermute | solution.py:50
  15.1 0.6 %collective-permute-start.3 = (bf16[96,2816]{1,0:T(8,128)(2,1)S(1)}, bf16[96,2816]{1,0:T(8,128)(2,1)S(1)}, u32[]{:S(2)}, u32[]{:S(2)}) collective-permute-start(bf16[96,2816]{1,0:T(8,128)(2,1)S(1)} %line.1.w0), channel_id=1, source_target_pairs={{0,8},{1,3},{2,10},{3,5},{4,12},{5,7},{6,14},{7,1},{8,16},{9,11},{... | collective-permute-start | bytes 1622024 | tf_op jit(solution)/shard_map/ppermute | solution.py:50
  15.7 3.1 %multiply_reduce_fusion = f32[1024]{0:T(1024)S(1)} fusion(bf16[1,1024,2048]{2,1,0:T(8,128)(2,1)} %param.6), kind=kLoop, calls=%fused_computation | loop fusion | flops 6290432 | bytes 4198400 | tf_op jit(solution)/shard_map/reduce_sum | solution.py:207
  19.5 0.4 multiply_reduce_fusion.1
  19.9 3.6 %owners.1 = (bf16[2048,1024]{1,0:T(8,128)(2,1)S(1)}, f32[8,2048]{1,0:T(8,128)S(1)}, bf16[24,384]{1,0:T(8,128)(2,1)S(1)}) custom-call(s32[1,1024]{1,0:T(1,128)S(1)} %compare_select_fusion.tokens, f32[1,1024]{1,0:T(1,128)S(1)} %bitcast.24), custom_call_target="tpu_custom_call" | custom-call | flops 536870912 | bytes 8388608 | tf_op jit(solution)/shard_map/owners/pallas_call | solution.py:149
  23.5 4.0 %collective-permute-done.4.w2 = bf16[96,2816]{1,0:T(8,128)(2,1)S(1)} collective-permute-done((bf16[96,2816]{1,0:T(8,128)(2,1)S(1)}, bf16[96,2816]{1,0:T(8,128)(2,1)S(1)}, u32[]{:S(2)}, u32[]{:S(2)}) %collective-permute-start.4) | collective-permute-done | bytes 540704 | tf_op jit(solution)/shard_map/ppermute | solution.py:50
  27.4 0.2 collective-permute-done.3.w1
  27.6 0.0 collective-permute-done.7.grads
  27.6 2.7 %row_scores.3 = f32[24,1024]{1,0:T(8,128)S(1)} custom-call(bf16[1024,2048]{1,0:T(8,128)(2,1)S(1)} %collective-permute-done.6.acts, bf16[1024,768]{1,0:T(8,128)(2,1)S(1)} %collective-permute-done.7.grads, bf16[96,2816]{1,0:T(8,128)(2,1)S(1)} %line.1.w0, bf16[96,2816]{1,0:T(8,128)(2,1)S(1)} %collective-permute-done.3.w1, ...), custom_call_target="tpu_custom_call" | custom-call | flops 2214592512 | bytes 8388608 | tf_op jit(solution)/shard_map/row_scores/pallas_call | solution.py:112
  30.3 3.2 %collective-permute-start.8 = (f32[24,1024]{1,0:T(8,128)S(1)}, f32[24,1024]{1,0:T(8,128)S(1)}, u32[]{:S(2)}, u32[]{:S(2)}) collective-permute-start(f32[24,1024]{1,0:T(8,128)S(1)} %row_scores.3), channel_id=1, source_target_pairs={{0,1},{1,0},{2,3},{3,2},{4,5},{5,4},{6,7},{7,6},{8,9},{9,8},{10,11... | collective-permute-start | bytes 294920 | tf_op jit(solution)/shard_map/ppermute | solution.py:50
  33.5 2.7 %row_scores.2.mine = f32[24,1024]{1,0:T(8,128)S(1)} custom-call(bf16[1024,2048]{1,0:T(8,128)(2,1)S(1)} %bitcast.21, bf16[1024,768]{1,0:T(8,128)(2,1)S(1)} %bitcast.23, bf16[96,2816]{1,0:T(8,128)(2,1)S(1)} %line.1.w0, bf16[96,2816]{1,0:T(8,128)(2,1)S(1)} %collective-permute-done.3.w1, bf16[96,2816]{1,0:T(8,128)(2,1)S(1)} %collective-permute-done.4.w2, ...), custom_call_target="tpu_custom_call" | custom-call | flops 2214592512 | bytes 8388608 | tf_op jit(solution)/shard_map/row_scores/pallas_call | solution.py:112
  36.2 1.4 %scatter.1 = f32[8,50,128]{2,1,0:T(8,128)S(1)} custom-call(f32[24,1024]{1,0:T(8,128)S(1)} %row_scores.2.mine, f32[24,1024]{1,0:T(8,128)S(1)} %collective-permute-done.8.theirs, bf16[2048,1024]{1,0:T(8,128)(2,1)S(1)} %get-tuple-element.13.onehot, f32[8,2048]{1,0:T(8,128)S(1)} %get-tuple-element.14.dense_norm), custom_call_target="tpu_custom_call" | custom-call | tf_op jit(solution)/shard_map/scatter/pallas_call | solution.py:184
  37.6 19.6 %all_to_all.5 = f32[8,50,128]{2,1,0:T(8,128)S(1)} all-to-all(f32[8,50,128]{2,1,0:T(8,128)S(1)} %scatter.1), channel_id=1, replica_groups=mesh['expert'=8,'dp'=32] {'expert'}, dimensions={0} | all-to-all | bytes 409600 | tf_op jit(solution)/shard_map/all_to_all | solution.py:220
  57.3 0.6 %copy_bitcast_fusion = f32[256,24]{0,1:T(8,128)} fusion(f32[2,24,128]{2,1,0:T(8,128)S(1)} %bitcast.26, f32[2,128]{1,0:T(2,128)S(1)} %fusion.2), kind=kLoop, calls=%fused_computation.3 | loop fusion | flops 6144 | bytes 50176 | tf_op jit(solution)/shard_map/reshape | solution.py:223
  (15 shorter events, 0.1 us)
Async XLA Ops:
  0.0 19.5 %copy-start.1 = (bf16[1,1024,768]{2,1,0:T(8,128)(2,1)S(1)}, bf16[1,1024,768]{2,1,0:T(8,128)(2,1)}, u32[]{:S(2)}) copy-start(bf16[1,1024,768]{2,1,0:T(8,128)(2,1)} %param.7) | copy-start | bytes 4718596
  0.0 19.9 %copy-start.2 = (s32[1,1024]{1,0:T(1,128)S(1)}, s32[1,1024]{1,0:T(1,128)}, u32[]{:S(2)}) copy-start(s32[1,1024]{1,0:T(1,128)} %param.11) | copy-start | bytes 12292
  0.0 27.6 %collective-permute-start.6 = (bf16[1024,2048]{1,0:T(8,128)(2,1)}, bf16[1024,2048]{1,0:T(8,128)(2,1)S(1)}, u32[]{:S(2)}, u32[]{:S(2)}) collective-permute-start(bf16[1024,2048]{1,0:T(8,128)(2,1)} %bitcast.20), channel_id=1, source_target_pairs={{0,1},{1,0},{2,3},{3,2},{4,5},{5,4},{6,7},{7,6},{8,9},{9,8},{10,11... | collective-permute-start | bytes 12582920 | tf_op jit(solution)/shard_map/ppermute | solution.py:50
  3.2 24.4 %collective-permute-start.7 = (bf16[1024,768]{1,0:T(8,128)(2,1)}, bf16[1024,768]{1,0:T(8,128)(2,1)S(1)}, u32[]{:S(2)}, u32[]{:S(2)}) collective-permute-start(bf16[1024,768]{1,0:T(8,128)(2,1)} %bitcast.22), channel_id=1, source_target_pairs={{0,1},{1,0},{2,3},{3,2},{4,5},{5,4},{6,7},{7,6},{8,9},{9,8},{10,11... | collective-permute-start | bytes 4718600 | tf_op jit(solution)/shard_map/ppermute | solution.py:50
  4.2 5.7 %collective-permute-start.2 = (bf16[24,2816]{1,0:T(8,128)(2,1)S(1)}, bf16[24,2816]{1,0:T(8,128)(2,1)S(1)}, u32[]{:S(2)}, u32[]{:S(2)}) collective-permute-start(bf16[24,2816]{1,0:T(8,128)(2,1)S(1)} %pad_maximum_fusion.own), channel_id=1, source_target_pairs={{0,4},{1,17},{2,6},{3,19},{4,0},{5,21},{6,2},{7,23},{8,12},{9,25},... | collective-permute-start | bytes 405512 | tf_op jit(solution)/shard_map/ppermute | solution.py:50
  5.5 4.5 %collective-permute-start.1 = (bf16[24,2816]{1,0:T(8,128)(2,1)S(1)}, bf16[24,2816]{1,0:T(8,128)(2,1)S(1)}, u32[]{:S(2)}, u32[]{:S(2)}) collective-permute-start(bf16[24,2816]{1,0:T(8,128)(2,1)S(1)} %pad_maximum_fusion.own), channel_id=1, source_target_pairs={{0,6},{1,25},{2,0},{3,27},{4,2},{5,29},{6,4},{7,31},{8,14},{9,1},{... | collective-permute-start | bytes 405512 | tf_op jit(solution)/shard_map/ppermute | solution.py:50
  6.3 5.4 %collective-permute-start = (bf16[24,2816]{1,0:T(8,128)(2,1)S(1)}, bf16[24,2816]{1,0:T(8,128)(2,1)S(1)}, u32[]{:S(2)}, u32[]{:S(2)}) collective-permute-start(bf16[24,2816]{1,0:T(8,128)(2,1)S(1)} %pad_maximum_fusion.own), channel_id=1, source_target_pairs={{0,2},{1,9},{2,4},{3,11},{4,6},{5,13},{6,0},{7,15},{8,10},{9,17},{... | collective-permute-start | bytes 405512 | tf_op jit(solution)/shard_map/ppermute | solution.py:50
  11.7 11.7 %collective-permute-start.5 = (bf16[96,2816]{1,0:T(8,128)(2,1)S(1)}, bf16[96,2816]{1,0:T(8,128)(2,1)S(1)}, u32[]{:S(2)}, u32[]{:S(2)}) collective-permute-start(bf16[96,2816]{1,0:T(8,128)(2,1)S(1)} %line.1.w0), channel_id=1, source_target_pairs={{0,16},{1,5},{2,18},{3,7},{4,20},{5,1},{6,22},{7,3},{8,24},{9,13},... | collective-permute-start | bytes 1622024 | tf_op jit(solution)/shard_map/ppermute | solution.py:50
  14.3 13.2 %collective-permute-start.4 = (bf16[96,2816]{1,0:T(8,128)(2,1)S(1)}, bf16[96,2816]{1,0:T(8,128)(2,1)S(1)}, u32[]{:S(2)}, u32[]{:S(2)}) collective-permute-start(bf16[96,2816]{1,0:T(8,128)(2,1)S(1)} %line.1.w0), channel_id=1, source_target_pairs={{0,24},{1,7},{2,26},{3,1},{4,28},{5,3},{6,30},{7,5},{8,0},{9,15},{... | collective-permute-start | bytes 1622024 | tf_op jit(solution)/shard_map/ppermute | solution.py:50
  15.1 12.5 %collective-permute-start.3 = (bf16[96,2816]{1,0:T(8,128)(2,1)S(1)}, bf16[96,2816]{1,0:T(8,128)(2,1)S(1)}, u32[]{:S(2)}, u32[]{:S(2)}) collective-permute-start(bf16[96,2816]{1,0:T(8,128)(2,1)S(1)} %line.1.w0), channel_id=1, source_target_pairs={{0,8},{1,3},{2,10},{3,5},{4,12},{5,7},{6,14},{7,1},{8,16},{9,11},{... | collective-permute-start | bytes 1622024 | tf_op jit(solution)/shard_map/ppermute | solution.py:50
  23.4 10.1 %copy-start = (bf16[1,1024,2048]{2,1,0:T(8,128)(2,1)S(1)}, bf16[1,1024,2048]{2,1,0:T(8,128)(2,1)}, u32[]{:S(2)}) copy-start(bf16[1,1024,2048]{2,1,0:T(8,128)(2,1)} %param.6) | copy-start | bytes 12582916
  30.3 5.9 %collective-permute-start.8 = (f32[24,1024]{1,0:T(8,128)S(1)}, f32[24,1024]{1,0:T(8,128)S(1)}, u32[]{:S(2)}, u32[]{:S(2)}) collective-permute-start(f32[24,1024]{1,0:T(8,128)S(1)} %row_scores.3), channel_id=1, source_target_pairs={{0,1},{1,0},{2,3},{3,2},{4,5},{5,4},{6,7},{7,6},{8,9},{9,8},{10,11... | collective-permute-start | bytes 294920 | tf_op jit(solution)/shard_map/ppermute | solution.py:50

commit v4 on v3

--- a/solution.py
+++ b/solution.py
@@ -13,7 +13,8 @@
 QUERIES = 24
 TOK_DEV = 256
 SIDE = 4
-OFFSETS = (0, -1, 1, 2)
+FIRST = (0, -1, 1, 2)
+SECOND = (0, 2, -1, 1)
 HALF = TOK_DEV // 2
 
 epsilon = 1e-06
@@ -50,14 +51,20 @@
     return lax.ppermute(value, "dp", table)
 
 
-def slot_queries(per_device):
+def offset(index, table):
+    value = jnp.full_like(index, table[-1])
+    for i, shift in enumerate(table[:-1]):
+        value = jnp.where(index == i, shift, value)
+    return value
+
+
+def slot_queries(shape, start):
+    per_device = shape[1] // (2 * SIDE)
     me = lax.axis_index("dp")
     core, my_x, my_y = me & 1, (me >> 1) & (SIDE - 1), me >> 3
-    slots = SIDE * SIDE * per_device
-    slot = lax.broadcasted_iota(jnp.int32, (QUERIES, slots), 1)
+    slot = lax.broadcasted_iota(jnp.int32, shape, 1) + start * SIDE * per_device
     piece = (slot * (65536 // per_device + 1)) >> 16
-    offset = lambda i: jnp.where(i == 1, SIDE - 1, jnp.where(i == 0, 0, i - 1))
-    first, second = offset(piece & (SIDE - 1)), offset(piece >> 2)
+    first, second = offset(piece & (SIDE - 1), FIRST), offset(piece >> 2, SECOND)
     swapped = (first - second) * core
     x = (my_x + first - swapped) & (SIDE - 1)
     y = (my_y + second + swapped) & (SIDE - 1)
@@ -92,56 +99,55 @@
     )(*shards)
 
 
-def scores_kernel(acts, grads, w0, w1, w2, w3, grouping, out, factors):
+def scores_kernel(acts, grads, w0, w1, grouping, *rest):
+    *base, out, factors = rest
     width = w0.shape[0]
-    for i, w in enumerate((w0, w1, w2, w3)):
-        factors[i * width : (i + 1) * width, :] = w[...]
+    factors[:width, :] = w0[...]
+    factors[width:, :] = w1[...]
     dot = functools.partial(
         lax.dot_general, dimension_numbers=CONTRACT_LAST, preferred_element_type=jnp.float32
     )
     product = dot(factors[:, :MODEL], acts[...]) * dot(factors[:, MODEL:], grads[...])
     high, low = split(product, 2)
-    out[...] = jnp.dot(grouping[...], high, preferred_element_type=jnp.float32) + jnp.dot(
+    scores = jnp.dot(grouping[...], high, preferred_element_type=jnp.float32) + jnp.dot(
         grouping[...], low, preferred_element_type=jnp.float32
     )
-
-
-def row_scores(acts, grads, pieces, grouping):
+    out[...] = scores + base[0][...] if base else scores
+
+
+def row_scores(acts, grads, pieces, grouping, *base):
     rows = acts.shape[0]
-    slots = 4 * pieces[0].shape[0]
+    slots = 2 * pieces[0].shape[0]
     return pl.pallas_call(
         scores_kernel,
         out_shape=jax.ShapeDtypeStruct((QUERIES, rows), jnp.float32),
-        in_specs=[VMEM] * 7,
+        in_specs=[VMEM] * (5 + len(base)),
         out_specs=VMEM,
         scratch_shapes=[pltpu.VMEM((slots, MODEL + MOE_FF), jnp.bfloat16)],
         compiler_params=pltpu.CompilerParams(vmem_limit_bytes=4 << 20),
         cost_estimate=pl.CostEstimate(
-            flops=2 * rows * slots * (MODEL + MOE_FF), bytes_accessed=8 << 20, transcendentals=0
-        ),
-        name="row_scores",
-    )(acts, grads, *pieces, grouping)
-
-
-def owners_kernel(tokens, norms, onehot, dense, grouping):
-    queries = slot_queries(grouping.shape[1] // (SIDE * SIDE))
-    query_ids = lax.broadcasted_iota(jnp.int32, queries.shape, 0)
-    grouping[...] = (query_ids == queries).astype(jnp.float32).astype(jnp.bfloat16)
+            flops=2 * rows * slots * (MODEL + MOE_FF), bytes_accessed=7 << 20, transcendentals=0
+        ),
+        name="late_scores" if base else "early_scores",
+    )(acts, grads, *pieces, grouping, *base)
+
+
+def owners_kernel(tokens, norms, onehot, dense, early, late):
+    for i, grouping in enumerate((early, late)):
+        queries = slot_queries(grouping.shape, 2 * i)
+        query_ids = lax.broadcasted_iota(jnp.int32, grouping.shape, 0)
+        grouping[...] = (query_ids == queries).astype(jnp.float32).astype(jnp.bfloat16)
     owner = lax.broadcasted_iota(jnp.int32, (TOK_DEV, tokens.shape[1]), 0)
+    row = lax.broadcasted_iota(jnp.int32, (8, tokens.shape[1]), 0)
     high, middle, low = split(norms[...], 3)
+    terms = jnp.where(row == 0, high, jnp.where(row == 1, middle, low))
     for start in range(0, onehot.shape[0], TOK_DEV):
         hot = (owner + start == tokens[...]).astype(jnp.float32).astype(jnp.bfloat16)
         onehot[start : start + TOK_DEV, :] = hot
-        part = [
-            lax.dot_general(
-                jnp.broadcast_to(term, (8, term.shape[1])),
-                hot,
-                CONTRACT_LAST,
-                preferred_element_type=jnp.float32,
-            )
-            for term in (high, middle, low)
-        ]
-        dense[:, start : start + TOK_DEV] = part[0] + part[1] + part[2]
+        part = lax.dot_general(
+            terms, hot, CONTRACT_LAST, preferred_element_type=jnp.float32
+        )
+        dense[:, start : start + TOK_DEV] = part[:1] + part[1:2] + part[2:3]
 
 
 def owners(tokens, norms, shard_tokens, slots):
@@ -150,11 +156,12 @@
         owners_kernel,
         out_shape=(
             jax.ShapeDtypeStruct((shard_tokens, rows), jnp.bfloat16),
-            jax.ShapeDtypeStruct((8, shard_tokens), jnp.float32),
-            jax.ShapeDtypeStruct((QUERIES, slots), jnp.bfloat16),
+            jax.ShapeDtypeStruct((1, shard_tokens), jnp.float32),
+            jax.ShapeDtypeStruct((QUERIES, slots // 2), jnp.bfloat16),
+            jax.ShapeDtypeStruct((QUERIES, slots // 2), jnp.bfloat16),
         ),
         in_specs=[VMEM] * 2,
-        out_specs=(VMEM, VMEM, VMEM),
+        out_specs=(VMEM,) * 4,
         compiler_params=pltpu.CompilerParams(vmem_limit_bytes=3 << 20),
         cost_estimate=pl.CostEstimate(
             flops=2 * rows * shard_tokens * 128, bytes_accessed=8 << 20, transcendentals=0
@@ -175,7 +182,7 @@
             lanes = slice(half * HALF, (half + 1) * HALF)
             out[i, half * QUERIES : (half + 1) * QUERIES, :] = part[:, lanes]
             out[i, 2 * QUERIES + half : 2 * QUERIES + half + 1, :] = dense_norm[
-                :1, i * TOK_DEV + half * HALF : i * TOK_DEV + (half + 1) * HALF
+                :, i * TOK_DEV + half * HALF : i * TOK_DEV + (half + 1) * HALF
             ]
 
 
@@ -197,25 +204,28 @@
     acts, grads = row_acts[0], row_grads[0]
     experts = lax.axis_size("expert")
     shard = jnp.concatenate([value_factor[0].T, grad_factor[0].T], 1)
-    line = [shard] + [send(shard, first_axis(-d)) for d in OFFSETS[1:]]
+    line = [shard] + [send(shard, first_axis(-d)) for d in FIRST[1:]]
     their_acts, their_grads = send(acts, SIBLING), send(grads, SIBLING)
+    norms = jnp.sum(jnp.square(acts.astype(jnp.float32)), 1) * jnp.sum(
+        jnp.square(grads.astype(jnp.float32)), 1
+    )
+    line[-1], norms = lax.optimization_barrier((line[-1], norms))
     line = join(line)
     line, tokens = lax.optimization_barrier((line, row_token))
-    pieces = [line] + [send(line, second_axis(-d)) for d in OFFSETS[1:]]
+    pieces = [line] + [send(line, second_axis(-d)) for d in SECOND[1:]]
     slots = acts.shape[0]
     live = lax.broadcasted_iota(jnp.int32, (1, slots), 1) < counts[0, 0]
-    norms = jnp.sum(jnp.square(acts.astype(jnp.float32)), 1) * jnp.sum(
-        jnp.square(grads.astype(jnp.float32)), 1
-    )
-    onehot, dense_norm, grouping = owners(
+    onehot, dense_norm, early, late = owners(
         jnp.where(live, tokens, -1),
         norms[None, :],
         TOK_DEV * experts,
         SIDE * SIDE * shard.shape[0],
     )
-    for_them = row_scores(their_acts, their_grads, pieces, grouping)
+    for_them = row_scores(their_acts, their_grads, pieces[:2], early)
+    mine = row_scores(acts, grads, pieces[:2], early)
+    for_them = row_scores(their_acts, their_grads, pieces[2:], late, for_them)
     theirs = send(for_them, SIBLING)
-    mine = row_scores(acts, grads, pieces, grouping)
+    mine = row_scores(acts, grads, pieces[2:], late, mine)
     dense = scatter(mine, theirs, onehot, dense_norm)
     summed = lax.all_to_all(dense, "expert", 0, 0).sum(0)
     totals, norm_sum = summed[: 2 * QUERIES].reshape(2, QUERIES, HALF), summed[2 * QUERIES :]

time: 58.1 us -> 57.2 us (0.985)
  waiting for transfers between devices: 8.84 us -> 6.6 us
  Pallas kernels: 10.4 us -> 11.7 us
    pallas_call x2 -> x4, Pallas kernels: 5.36 us -> 8.83 us  [row_scores(): pl.pallas_call(scores_kernel, out_shape=jax.ShapeDtypeStruct((QUERIES, ro...]
    ppermute x9, waiting for transfers between devices: 8.84 us -> 6.6 us  [send(): return lax.ppermute(value, 'dp', table)]
    pallas_call x1, Pallas kernels: 3.56 us -> 1.39 us  [owners(): pl.pallas_call(owners_kernel, out_shape=(jax.ShapeDtypeStruct((shard_toke...]
  transfers between devices with their start and end apart: 9 -> 9, of which waited for: 5 -> 4; matrix products, arithmetic and copies ran while one was open for 8% -> 8% of each run, Pallas kernels for 11% -> 14%
where the time goes in v4:
time: 57.2 us; the launch traced here: 57 us
  blocking collectives  19.6 us (34%)
  starting transfers between devices  13.3 us (23%)
  Pallas kernels  11.7 us (20%)
  waiting for transfers between devices  6.6 us (12%)
  other arithmetic  5.02 us (9%)
  between operations  0.78 us (1%)
    all_to_all x1, blocking collectives, local(): summed = lax.all_to_all(dense, 'expert', 0, 0).sum(0)  19.6 us
    ppermute x9, starting transfers between devices, send(): return lax.ppermute(value, 'dp', table)  13.3 us
    pallas_call x4, Pallas kernels, row_scores(): pl.pallas_call(scores_kernel, out_shape=jax.ShapeDtypeStruct((QUERIES, ro...  8.83 us
    ppermute x9, waiting for transfers between devices, send(): return lax.ppermute(value, 'dp', table)  6.6 us
    reduce_sum x1, other arithmetic, local(): jnp.sum(jnp.square(acts.astype(jnp.float32)), 1)  3.07 us
    pallas_call x1, Pallas kernels, scatter(): pl.pallas_call(scatter_kernel, out_shape=jax.ShapeDtypeStruct((shard_toke...  1.4 us
    pallas_call x1, Pallas kernels, owners(): pl.pallas_call(owners_kernel, out_shape=(jax.ShapeDtypeStruct((shard_toke...  1.39 us
  transfers between devices with their start and end apart: 9, of which 4 were waited for; matrix products, arithmetic and copies ran while one was open for 8% of the time, Pallas kernels for 14%

profile of v4, /device:TPU:1, one launch (start us, length us, event | category | flops | bytes accessed | tf_op | source)
XLA Modules:
  0.0 57.0 jit_solution(1039186934597282527)
XLA Ops:
  0.0 3.2 %collective-permute-start.6 = (bf16[1024,2048]{1,0:T(8,128)(2,1)}, bf16[1024,2048]{1,0:T(8,128)(2,1)S(1)}, u32[]{:S(2)}, u32[]{:S(2)}) collective-permute-start(bf16[1024,2048]{1,0:T(8,128)(2,1)} %bitcast.20), channel_id=1, source_target_pairs={{0,1},{1,0},{2,3},{3,2},{4,5},{5,4},{6,7},{7,6},{8,9},{9,8},{10,11... | collective-permute-start | bytes 12582920 | tf_op jit(solution)/shard_map/ppermute | solution.py:51
  3.2 0.9 %pad_maximum_fusion.own = bf16[24,2816]{1,0:T(8,128)(2,1)S(1)} fusion(bf16[24,768]{1,0:T(8,128)(2,1)} %bitcast.29, bf16[24,2048]{1,0:T(8,128)(2,1)} %bitcast.27), kind=kLoop, calls=%fused_computation.2 | loop fusion | flops 270336 | bytes 270336 | tf_op jit(solution)/shard_map/concatenate | solution.py:206
  4.2 1.4 %collective-permute-start.2 = (bf16[24,2816]{1,0:T(8,128)(2,1)S(1)}, bf16[24,2816]{1,0:T(8,128)(2,1)S(1)}, u32[]{:S(2)}, u32[]{:S(2)}) collective-permute-start(bf16[24,2816]{1,0:T(8,128)(2,1)S(1)} %pad_maximum_fusion.own), channel_id=1, source_target_pairs={{0,4},{1,17},{2,6},{3,19},{4,0},{5,21},{6,2},{7,23},{8,12},{9,25},... | collective-permute-start | bytes 405512 | tf_op jit(solution)/shard_map/ppermute | solution.py:51
  5.5 0.8 %collective-permute-start.1 = (bf16[24,2816]{1,0:T(8,128)(2,1)S(1)}, bf16[24,2816]{1,0:T(8,128)(2,1)S(1)}, u32[]{:S(2)}, u32[]{:S(2)}) collective-permute-start(bf16[24,2816]{1,0:T(8,128)(2,1)S(1)} %pad_maximum_fusion.own), channel_id=1, source_target_pairs={{0,6},{1,25},{2,0},{3,27},{4,2},{5,29},{6,4},{7,31},{8,14},{9,1},{... | collective-permute-start | bytes 405512 | tf_op jit(solution)/shard_map/ppermute | solution.py:51
  6.3 0.7 %collective-permute-start = (bf16[24,2816]{1,0:T(8,128)(2,1)S(1)}, bf16[24,2816]{1,0:T(8,128)(2,1)S(1)}, u32[]{:S(2)}, u32[]{:S(2)}) collective-permute-start(bf16[24,2816]{1,0:T(8,128)(2,1)S(1)} %pad_maximum_fusion.own), channel_id=1, source_target_pairs={{0,2},{1,9},{2,4},{3,11},{4,6},{5,13},{6,0},{7,15},{8,10},{9,17},{... | collective-permute-start | bytes 405512 | tf_op jit(solution)/shard_map/ppermute | solution.py:51
  7.0 3.1 %multiply_reduce_fusion = f32[1024]{0:T(1024)S(1)} fusion(bf16[1,1024,2048]{2,1,0:T(8,128)(2,1)} %param.6), kind=kLoop, calls=%fused_computation | loop fusion | flops 6290432 | bytes 4198400 | tf_op jit(solution)/shard_map/reduce_sum | solution.py:209
  10.1 0.4 multiply_reduce_fusion.1
  10.5 1.2 %collective-permute-done.before = bf16[24,2816]{1,0:T(8,128)(2,1)S(1)} collective-permute-done((bf16[24,2816]{1,0:T(8,128)(2,1)S(1)}, bf16[24,2816]{1,0:T(8,128)(2,1)S(1)}, u32[]{:S(2)}, u32[]{:S(2)}) %collective-permute-start) | collective-permute-done | bytes 135200 | tf_op jit(solution)/shard_map/ppermute | solution.py:51
  11.7 2.5 %collective-permute-start.5 = (bf16[96,2816]{1,0:T(8,128)(2,1)S(1)}, bf16[96,2816]{1,0:T(8,128)(2,1)S(1)}, u32[]{:S(2)}, u32[]{:S(2)}) collective-permute-start(bf16[96,2816]{1,0:T(8,128)(2,1)S(1)} %line.1.w0), channel_id=1, source_target_pairs={{0,16},{1,5},{2,18},{3,7},{4,20},{5,1},{6,22},{7,3},{8,24},{9,13},... | collective-permute-start | bytes 1622024 | tf_op jit(solution)/shard_map/ppermute | solution.py:51
  14.3 0.9 %collective-permute-start.4 = (bf16[96,2816]{1,0:T(8,128)(2,1)S(1)}, bf16[96,2816]{1,0:T(8,128)(2,1)S(1)}, u32[]{:S(2)}, u32[]{:S(2)}) collective-permute-start(bf16[96,2816]{1,0:T(8,128)(2,1)S(1)} %line.1.w0), channel_id=1, source_target_pairs={{0,24},{1,7},{2,26},{3,1},{4,28},{5,3},{6,30},{7,5},{8,0},{9,15},{... | collective-permute-start | bytes 1622024 | tf_op jit(solution)/shard_map/ppermute | solution.py:51
  15.1 0.6 %collective-permute-start.3 = (bf16[96,2816]{1,0:T(8,128)(2,1)S(1)}, bf16[96,2816]{1,0:T(8,128)(2,1)S(1)}, u32[]{:S(2)}, u32[]{:S(2)}) collective-permute-start(bf16[96,2816]{1,0:T(8,128)(2,1)S(1)} %line.1.w0), channel_id=1, source_target_pairs={{0,8},{1,3},{2,10},{3,5},{4,12},{5,7},{6,14},{7,1},{8,16},{9,11},{... | collective-permute-start | bytes 1622024 | tf_op jit(solution)/shard_map/ppermute | solution.py:51
  16.4 1.4 %owners.1 = (bf16[2048,1024]{1,0:T(8,128)(2,1)S(1)}, f32[1,2048]{1,0:T(1,128)S(1)}, bf16[24,192]{1,0:T(8,128)(2,1)S(1)}, bf16[24,192]{1,0:T(8,128)(2,1)S(1)}) custom-call(s32[1,1024]{1,0:T(1,128)S(1)} %compare_select_fusion.tokens, f32[1,1024]{1,0:T(1,128)S(1)} %bitcast.26), custom_call_target="tpu_custom_call" | custom-call | flops 536870912 | bytes 8388608 | tf_op jit(solution)/shard_map/owners/pallas_call | solution.py:155
  17.8 4.1 %collective-permute-done.5.w1 = bf16[96,2816]{1,0:T(8,128)(2,1)S(1)} collective-permute-done((bf16[96,2816]{1,0:T(8,128)(2,1)S(1)}, bf16[96,2816]{1,0:T(8,128)(2,1)S(1)}, u32[]{:S(2)}, u32[]{:S(2)}) %collective-permute-start.5) | collective-permute-done | bytes 540704 | tf_op jit(solution)/shard_map/ppermute | solution.py:51
  21.9 2.2 %early_scores.2.rest_0_ = f32[24,1024]{1,0:T(8,128)S(1)} custom-call(bf16[1024,2048]{1,0:T(8,128)(2,1)S(1)} %bitcast.21, bf16[1024,768]{1,0:T(8,128)(2,1)S(1)} %bitcast.24, bf16[96,2816]{1,0:T(8,128)(2,1)S(1)} %line.1.w0, bf16[96,2816]{1,0:T(8,128)(2,1)S(1)} %collective-permute-done.5.w1, bf16[24,192]{1,0:T(8,128)(2,1)S(1)} %get-tuple-element.18.grouping), custom_call_target="tpu_custom_call" | custom-call | flops 1107296256 | bytes 7340032 | tf_op jit(solution)/shard_map/early_scores/pallas_call | solution.py:121
  24.1 0.0 collective-permute-done.6.acts
  24.1 2.2 %early_scores.3.rest_0_ = f32[24,1024]{1,0:T(8,128)S(1)} custom-call(bf16[1024,2048]{1,0:T(8,128)(2,1)S(1)} %collective-permute-done.6.acts, bf16[1024,768]{1,0:T(8,128)(2,1)S(1)} %collective-permute-done.7.grads, bf16[96,2816]{1,0:T(8,128)(2,1)S(1)} %line.1.w0, bf16[96,2816]{1,0:T(8,128)(2,1)S(1)} %collective-permute-done.5.w1, ...), custom_call_target="tpu_custom_call" | custom-call | flops 1107296256 | bytes 7340032 | tf_op jit(solution)/shard_map/early_scores/pallas_call | solution.py:121
  26.3 1.1 %collective-permute-done.4.w1 = bf16[96,2816]{1,0:T(8,128)(2,1)S(1)} collective-permute-done((bf16[96,2816]{1,0:T(8,128)(2,1)S(1)}, bf16[96,2816]{1,0:T(8,128)(2,1)S(1)}, u32[]{:S(2)}, u32[]{:S(2)}) %collective-permute-start.4) | collective-permute-done | bytes 540704 | tf_op jit(solution)/shard_map/ppermute | solution.py:51
  27.5 0.2 collective-permute-done.3.w0
  27.6 2.2 %late_scores.3 = f32[24,1024]{1,0:T(8,128)S(1)} custom-call(bf16[1024,2048]{1,0:T(8,128)(2,1)S(1)} %collective-permute-done.6.acts, bf16[1024,768]{1,0:T(8,128)(2,1)S(1)} %collective-permute-done.7.grads, bf16[96,2816]{1,0:T(8,128)(2,1)S(1)} %collective-permute-done.3.w0, bf16[96,2816]{1,0:T(8,128)(2,1)S(1)} %collective-permute-done.4.w1, ...), custom_call_target="tpu_custom_call" | custom-call | flops 1107296256 | bytes 7340032 | tf_op jit(solution)/shard_map/late_scores/pallas_call | solution.py:121
  29.8 3.2 %collective-permute-start.8 = (f32[24,1024]{1,0:T(8,128)S(1)}, f32[24,1024]{1,0:T(8,128)S(1)}, u32[]{:S(2)}, u32[]{:S(2)}) collective-permute-start(f32[24,1024]{1,0:T(8,128)S(1)} %late_scores.3), channel_id=1, source_target_pairs={{0,1},{1,0},{2,3},{3,2},{4,5},{5,4},{6,7},{7,6},{8,9},{9,8},{10,11... | collective-permute-start | bytes 294920 | tf_op jit(solution)/shard_map/ppermute | solution.py:51
  33.1 2.2 %late_scores.2.mine = f32[24,1024]{1,0:T(8,128)S(1)} custom-call(bf16[1024,2048]{1,0:T(8,128)(2,1)S(1)} %bitcast.22, bf16[1024,768]{1,0:T(8,128)(2,1)S(1)} %bitcast.25, bf16[96,2816]{1,0:T(8,128)(2,1)S(1)} %collective-permute-done.3.w0, bf16[96,2816]{1,0:T(8,128)(2,1)S(1)} %collective-permute-done.4.w1, bf16[24,192]{1,0:T(8,128)(2,1)S(1)} %get-tuple-element.17.grouping, ...), custom_call_target="tpu_custom_call" | custom-call | flops 1107296256 | bytes 7340032 | tf_op jit(solution)/shard_map/late_scores/pallas_call | solution.py:121
  35.3 1.4 %scatter.1 = f32[8,50,128]{2,1,0:T(8,128)S(1)} custom-call(f32[24,1024]{1,0:T(8,128)S(1)} %late_scores.2.mine, f32[24,1024]{1,0:T(8,128)S(1)} %collective-permute-done.8.theirs, bf16[2048,1024]{1,0:T(8,128)(2,1)S(1)} %get-tuple-element.19.onehot, f32[1,2048]{1,0:T(1,128)S(1)} %get-tuple-element.20.dense_norm), custom_call_target="tpu_custom_call" | custom-call | tf_op jit(solution)/shard_map/scatter/pallas_call | solution.py:191
  36.7 19.6 %all_to_all.5 = f32[8,50,128]{2,1,0:T(8,128)S(1)} all-to-all(f32[8,50,128]{2,1,0:T(8,128)S(1)} %scatter.1), channel_id=1, replica_groups=mesh['expert'=8,'dp'=32] {'expert'}, dimensions={0} | all-to-all | bytes 409600 | tf_op jit(solution)/shard_map/all_to_all | solution.py:230
  56.4 0.6 %copy_bitcast_fusion = f32[256,24]{0,1:T(8,128)} fusion(f32[2,24,128]{2,1,0:T(8,128)S(1)} %bitcast.28, f32[2,128]{1,0:T(2,128)S(1)} %fusion.2), kind=kLoop, calls=%fused_computation.3 | loop fusion | flops 6144 | bytes 50176 | tf_op jit(solution)/shard_map/reshape | solution.py:233
  (17 shorter events, 0.1 us)
Async XLA Ops:
  0.0 10.1 %copy-start.1 = (bf16[1,1024,768]{2,1,0:T(8,128)(2,1)S(1)}, bf16[1,1024,768]{2,1,0:T(8,128)(2,1)}, u32[]{:S(2)}) copy-start(bf16[1,1024,768]{2,1,0:T(8,128)(2,1)} %param.7) | copy-start | bytes 4718596
  0.0 16.4 %copy-start.2 = (s32[1,1024]{1,0:T(1,128)S(1)}, s32[1,1024]{1,0:T(1,128)}, u32[]{:S(2)}) copy-start(s32[1,1024]{1,0:T(1,128)} %param.11) | copy-start | bytes 12292
  0.0 24.1 %collective-permute-start.6 = (bf16[1024,2048]{1,0:T(8,128)(2,1)}, bf16[1024,2048]{1,0:T(8,128)(2,1)S(1)}, u32[]{:S(2)}, u32[]{:S(2)}) collective-permute-start(bf16[1024,2048]{1,0:T(8,128)(2,1)} %bitcast.20), channel_id=1, source_target_pairs={{0,1},{1,0},{2,3},{3,2},{4,5},{5,4},{6,7},{7,6},{8,9},{9,8},{10,11... | collective-permute-start | bytes 12582920 | tf_op jit(solution)/shard_map/ppermute | solution.py:51
  3.2 20.8 %collective-permute-start.7 = (bf16[1024,768]{1,0:T(8,128)(2,1)}, bf16[1024,768]{1,0:T(8,128)(2,1)S(1)}, u32[]{:S(2)}, u32[]{:S(2)}) collective-permute-start(bf16[1024,768]{1,0:T(8,128)(2,1)} %bitcast.23), channel_id=1, source_target_pairs={{0,1},{1,0},{2,3},{3,2},{4,5},{5,4},{6,7},{7,6},{8,9},{9,8},{10,11... | collective-permute-start | bytes 4718600 | tf_op jit(solution)/shard_map/ppermute | solution.py:51
  4.2 17.7 %copy-start = (bf16[1,1024,2048]{2,1,0:T(8,128)(2,1)S(1)}, bf16[1,1024,2048]{2,1,0:T(8,128)(2,1)}, u32[]{:S(2)}) copy-start(bf16[1,1024,2048]{2,1,0:T(8,128)(2,1)} %param.6) | copy-start | bytes 12582916
  4.2 6.3 %collective-permute-start.2 = (bf16[24,2816]{1,0:T(8,128)(2,1)S(1)}, bf16[24,2816]{1,0:T(8,128)(2,1)S(1)}, u32[]{:S(2)}, u32[]{:S(2)}) collective-permute-start(bf16[24,2816]{1,0:T(8,128)(2,1)S(1)} %pad_maximum_fusion.own), channel_id=1, source_target_pairs={{0,4},{1,17},{2,6},{3,19},{4,0},{5,21},{6,2},{7,23},{8,12},{9,25},... | collective-permute-start | bytes 405512 | tf_op jit(solution)/shard_map/ppermute | solution.py:51
  5.5 5.0 %collective-permute-start.1 = (bf16[24,2816]{1,0:T(8,128)(2,1)S(1)}, bf16[24,2816]{1,0:T(8,128)(2,1)S(1)}, u32[]{:S(2)}, u32[]{:S(2)}) collective-permute-start(bf16[24,2816]{1,0:T(8,128)(2,1)S(1)} %pad_maximum_fusion.own), channel_id=1, source_target_pairs={{0,6},{1,25},{2,0},{3,27},{4,2},{5,29},{6,4},{7,31},{8,14},{9,1},{... | collective-permute-start | bytes 405512 | tf_op jit(solution)/shard_map/ppermute | solution.py:51
  6.3 5.4 %collective-permute-start = (bf16[24,2816]{1,0:T(8,128)(2,1)S(1)}, bf16[24,2816]{1,0:T(8,128)(2,1)S(1)}, u32[]{:S(2)}, u32[]{:S(2)}) collective-permute-start(bf16[24,2816]{1,0:T(8,128)(2,1)S(1)} %pad_maximum_fusion.own), channel_id=1, source_target_pairs={{0,2},{1,9},{2,4},{3,11},{4,6},{5,13},{6,0},{7,15},{8,10},{9,17},{... | collective-permute-start | bytes 405512 | tf_op jit(solution)/shard_map/ppermute | solution.py:51
  11.7 10.1 %collective-permute-start.5 = (bf16[96,2816]{1,0:T(8,128)(2,1)S(1)}, bf16[96,2816]{1,0:T(8,128)(2,1)S(1)}, u32[]{:S(2)}, u32[]{:S(2)}) collective-permute-start(bf16[96,2816]{1,0:T(8,128)(2,1)S(1)} %line.1.w0), channel_id=1, source_target_pairs={{0,16},{1,5},{2,18},{3,7},{4,20},{5,1},{6,22},{7,3},{8,24},{9,13},... | collective-permute-start | bytes 1622024 | tf_op jit(solution)/shard_map/ppermute | solution.py:51
  14.3 13.2 %collective-permute-start.4 = (bf16[96,2816]{1,0:T(8,128)(2,1)S(1)}, bf16[96,2816]{1,0:T(8,128)(2,1)S(1)}, u32[]{:S(2)}, u32[]{:S(2)}) collective-permute-start(bf16[96,2816]{1,0:T(8,128)(2,1)S(1)} %line.1.w0), channel_id=1, source_target_pairs={{0,24},{1,7},{2,26},{3,1},{4,28},{5,3},{6,30},{7,5},{8,0},{9,15},{... | collective-permute-start | bytes 1622024 | tf_op jit(solution)/shard_map/ppermute | solution.py:51
  15.1 12.5 %collective-permute-start.3 = (bf16[96,2816]{1,0:T(8,128)(2,1)S(1)}, bf16[96,2816]{1,0:T(8,128)(2,1)S(1)}, u32[]{:S(2)}, u32[]{:S(2)}) collective-permute-start(bf16[96,2816]{1,0:T(8,128)(2,1)S(1)} %line.1.w0), channel_id=1, source_target_pairs={{0,8},{1,3},{2,10},{3,5},{4,12},{5,7},{6,14},{7,1},{8,16},{9,11},{... | collective-permute-start | bytes 1622024 | tf_op jit(solution)/shard_map/ppermute | solution.py:51
  29.8 5.5 %collective-permute-start.8 = (f32[24,1024]{1,0:T(8,128)S(1)}, f32[24,1024]{1,0:T(8,128)S(1)}, u32[]{:S(2)}, u32[]{:S(2)}) collective-permute-start(f32[24,1024]{1,0:T(8,128)S(1)} %late_scores.3), channel_id=1, source_target_pairs={{0,1},{1,0},{2,3},{3,2},{4,5},{5,4},{6,7},{7,6},{8,9},{9,8},{10,11... | collective-permute-start | bytes 294920 | tf_op jit(solution)/shard_map/ppermute | solution.py:51

commit v5 on v4

--- a/solution.py
+++ b/solution.py
@@ -19,7 +19,6 @@
 
 epsilon = 1e-06
 
-CONTRACT_LAST = (((1,), (1,)), ((), ()))
 VMEM = pl.BlockSpec(memory_space=pltpu.VMEM)
 
 
@@ -99,24 +98,38 @@
     )(*shards)
 
 
+def turn_kernel(acts, grads, acts_out, grads_out):
+    for rows, turned in ((acts, acts_out), (grads, grads_out)):
+        for start in range(0, rows.shape[1], TOK_DEV):
+            turned[start : start + TOK_DEV, :] = rows[:, start : start + TOK_DEV].T
+
+
+def turn(acts, grads):
+    return pl.pallas_call(
+        turn_kernel,
+        out_shape=tuple(jax.ShapeDtypeStruct(x.shape[::-1], x.dtype) for x in (acts, grads)),
+        in_specs=[VMEM, VMEM],
+        out_specs=(VMEM, VMEM),
+        compiler_params=pltpu.CompilerParams(vmem_limit_bytes=2 << 20),
+        cost_estimate=pl.CostEstimate(flops=0, bytes_accessed=6 << 20, transcendentals=0),
+        name="turn",
+    )(acts, grads)
+
+
 def scores_kernel(acts, grads, w0, w1, grouping, *rest):
     *base, out, factors = rest
     width = w0.shape[0]
     factors[:width, :] = w0[...]
     factors[width:, :] = w1[...]
-    dot = functools.partial(
-        lax.dot_general, dimension_numbers=CONTRACT_LAST, preferred_element_type=jnp.float32
-    )
+    dot = functools.partial(jnp.dot, preferred_element_type=jnp.float32)
     product = dot(factors[:, :MODEL], acts[...]) * dot(factors[:, MODEL:], grads[...])
     high, low = split(product, 2)
-    scores = jnp.dot(grouping[...], high, preferred_element_type=jnp.float32) + jnp.dot(
-        grouping[...], low, preferred_element_type=jnp.float32
-    )
+    scores = dot(grouping[...], high) + dot(grouping[...], low)
     out[...] = scores + base[0][...] if base else scores
 
 
 def row_scores(acts, grads, pieces, grouping, *base):
-    rows = acts.shape[0]
+    rows = acts.shape[1]
     slots = 2 * pieces[0].shape[0]
     return pl.pallas_call(
         scores_kernel,
@@ -137,17 +150,17 @@
         queries = slot_queries(grouping.shape, 2 * i)
         query_ids = lax.broadcasted_iota(jnp.int32, grouping.shape, 0)
         grouping[...] = (query_ids == queries).astype(jnp.float32).astype(jnp.bfloat16)
-    owner = lax.broadcasted_iota(jnp.int32, (TOK_DEV, tokens.shape[1]), 0)
-    row = lax.broadcasted_iota(jnp.int32, (8, tokens.shape[1]), 0)
+    rows = tokens.shape[1]
+    token = jnp.broadcast_to(tokens[...], (HALF, rows)).T
+    owner = lax.broadcasted_iota(jnp.int32, (rows, HALF), 1)
+    for start in range(0, onehot.shape[1], HALF):
+        hot = (token == owner + start).astype(jnp.float32).astype(jnp.bfloat16)
+        onehot[:, start : start + HALF] = hot
+    row = lax.broadcasted_iota(jnp.int32, (8, rows), 0)
     high, middle, low = split(norms[...], 3)
     terms = jnp.where(row == 0, high, jnp.where(row == 1, middle, low))
-    for start in range(0, onehot.shape[0], TOK_DEV):
-        hot = (owner + start == tokens[...]).astype(jnp.float32).astype(jnp.bfloat16)
-        onehot[start : start + TOK_DEV, :] = hot
-        part = lax.dot_general(
-            terms, hot, CONTRACT_LAST, preferred_element_type=jnp.float32
-        )
-        dense[:, start : start + TOK_DEV] = part[:1] + part[1:2] + part[2:3]
+    part = jnp.dot(terms, onehot[...], preferred_element_type=jnp.float32)
+    dense[...] = part[:1] + part[1:2] + part[2:3]
 
 
 def owners(tokens, norms, shard_tokens, slots):
@@ -155,7 +168,7 @@
     return pl.pallas_call(
         owners_kernel,
         out_shape=(
-            jax.ShapeDtypeStruct((shard_tokens, rows), jnp.bfloat16),
+            jax.ShapeDtypeStruct((rows, shard_tokens), jnp.bfloat16),
             jax.ShapeDtypeStruct((1, shard_tokens), jnp.float32),
             jax.ShapeDtypeStruct((QUERIES, slots // 2), jnp.bfloat16),
             jax.ShapeDtypeStruct((QUERIES, slots // 2), jnp.bfloat16),
@@ -172,22 +185,18 @@
 
 def scatter_kernel(mine, theirs, onehot, dense_norm, out):
     table = jnp.concatenate(split(mine[...] + theirs[...], 3), 0)
+    part = jnp.dot(table, onehot[...], preferred_element_type=jnp.float32)
+    part = part[:QUERIES] + part[QUERIES : 2 * QUERIES] + part[2 * QUERIES :]
     for i in range(out.shape[0]):
-        owned = slice(i * TOK_DEV, (i + 1) * TOK_DEV)
-        part = lax.dot_general(
-            table, onehot[owned, :], CONTRACT_LAST, preferred_element_type=jnp.float32
-        )
-        part = part[:QUERIES] + part[QUERIES : 2 * QUERIES] + part[2 * QUERIES :]
         for half in range(2):
-            lanes = slice(half * HALF, (half + 1) * HALF)
-            out[i, half * QUERIES : (half + 1) * QUERIES, :] = part[:, lanes]
-            out[i, 2 * QUERIES + half : 2 * QUERIES + half + 1, :] = dense_norm[
-                :, i * TOK_DEV + half * HALF : i * TOK_DEV + (half + 1) * HALF
-            ]
+            start = i * TOK_DEV + half * HALF
+            owned = slice(start, start + HALF)
+            out[i, half * QUERIES : (half + 1) * QUERIES, :] = part[:, owned]
+            out[i, 2 * QUERIES + half : 2 * QUERIES + half + 1, :] = dense_norm[:, owned]
 
 
 def scatter(mine, theirs, onehot, dense_norm):
-    shard_tokens = onehot.shape[0]
+    shard_tokens = onehot.shape[1]
     return pl.pallas_call(
         scatter_kernel,
         out_shape=jax.ShapeDtypeStruct(
@@ -206,26 +215,29 @@
     shard = jnp.concatenate([value_factor[0].T, grad_factor[0].T], 1)
     line = [shard] + [send(shard, first_axis(-d)) for d in FIRST[1:]]
     their_acts, their_grads = send(acts, SIBLING), send(grads, SIBLING)
-    norms = jnp.sum(jnp.square(acts.astype(jnp.float32)), 1) * jnp.sum(
-        jnp.square(grads.astype(jnp.float32)), 1
-    )
-    line[-1], norms = lax.optimization_barrier((line[-1], norms))
+    acts_norm = jnp.sum(jnp.square(acts.astype(jnp.float32)), 1)
+    line[-1], acts_norm = lax.optimization_barrier((line[-1], acts_norm))
     line = join(line)
-    line, tokens = lax.optimization_barrier((line, row_token))
+    line, acts, grads = lax.optimization_barrier((line, acts, grads))
     pieces = [line] + [send(line, second_axis(-d)) for d in SECOND[1:]]
     slots = acts.shape[0]
     live = lax.broadcasted_iota(jnp.int32, (1, slots), 1) < counts[0, 0]
+    norms = acts_norm * jnp.sum(jnp.square(grads.astype(jnp.float32)), 1)
+    their_rows = turn(their_acts, their_grads)
+    my_rows = turn(acts, grads)
+    norms, *their_rows = lax.optimization_barrier((norms, *their_rows))
     onehot, dense_norm, early, late = owners(
-        jnp.where(live, tokens, -1),
+        jnp.where(live, row_token, -1),
         norms[None, :],
         TOK_DEV * experts,
         SIDE * SIDE * shard.shape[0],
     )
-    for_them = row_scores(their_acts, their_grads, pieces[:2], early)
-    mine = row_scores(acts, grads, pieces[:2], early)
-    for_them = row_scores(their_acts, their_grads, pieces[2:], late, for_them)
+    for_them = row_scores(*their_rows, pieces[:2], early)
+    mine = row_scores(*my_rows, pieces[:2], early)
+    for_them, mine = lax.optimization_barrier((for_them, mine))
+    for_them = row_scores(*their_rows, pieces[2:], late, for_them)
     theirs = send(for_them, SIBLING)
-    mine = row_scores(acts, grads, pieces[2:], late, mine)
+    mine = row_scores(*my_rows, pieces[2:], late, mine)
     dense = scatter(mine, theirs, onehot, dense_norm)
     summed = lax.all_to_all(dense, "expert", 0, 0).sum(0)
     totals, norm_sum = summed[: 2 * QUERIES].reshape(2, QUERIES, HALF), summed[2 * QUERIES :]

time: 57.2 us -> 54.3 us (0.949)
  waiting for transfers between devices: 6.6 us -> 0.05 us
  starting transfers between devices: 13.3 us -> 15.1 us
  local copies, waits for them, and re-layouts: 0.02 us -> 1.42 us
    ppermute x9, waiting for transfers between devices: 6.6 us -> 0.05 us  [send(): return lax.ppermute(value, 'dp', table)]
    pallas_call x1 -> x3, Pallas kernels: 1.39 us -> 5.19 us  [the longest x2 3.33 us: turn(): pl.pallas_call(turn_kernel, out_shape=tuple((jax.ShapeDtypeStruct(x.shape...]
    pallas_call x4, Pallas kernels: 8.83 us -> 6.03 us  [row_scores(): pl.pallas_call(scores_kernel, out_shape=jax.ShapeDtypeStruct((QUERIES, ro...]
    ppermute x9, starting transfers between devices: 13.3 us -> 15.1 us  [send(): return lax.ppermute(value, 'dp', table)]
    unnamed x6 -> x8, local copies, waits for them, and re-layouts: 0.01 us -> 1.41 us
  transfers between devices with their start and end apart: 9 -> 9, of which waited for: 4 -> 0; matrix products, arithmetic and copies ran while one was open for 8% -> 8% of each run, Pallas kernels for 14% -> 18%
where the time goes in v5:
time: 54.3 us; the launch traced here: 54.1 us
  blocking collectives  19.6 us (36%)
  starting transfers between devices  15.1 us (28%)
  Pallas kernels  12.1 us (22%)
  other arithmetic  5.02 us (9%)
  local copies, waits for them, and re-layouts  1.42 us (3%)
  between operations  0.83 us (2%)
    all_to_all x1, blocking collectives, local(): summed = lax.all_to_all(dense, 'expert', 0, 0).sum(0)  19.6 us
    ppermute x9, starting transfers between devices, send(): return lax.ppermute(value, 'dp', table)  15.1 us
    pallas_call x4, Pallas kernels, row_scores(): pl.pallas_call(scores_kernel, out_shape=jax.ShapeDtypeStruct((QUERIES, ro...  6.03 us
    pallas_call x2, Pallas kernels, turn(): pl.pallas_call(turn_kernel, out_shape=tuple((jax.ShapeDtypeStruct(x.shape...  3.33 us
    reduce_sum x1, other arithmetic, local(): acts_norm = jnp.sum(jnp.square(acts.astype(jnp.float32)), 1)  3.07 us
    pallas_call x1, Pallas kernels, owners(): pl.pallas_call(owners_kernel, out_shape=(jax.ShapeDtypeStruct((rows, shar...  1.85 us
    unnamed x8, local copies, waits for them, and re-layouts  1.41 us
  transfers between devices with their start and end apart: 9, of which 0 were waited for; matrix products, arithmetic and copies ran while one was open for 8% of the time, Pallas kernels for 18%

profile of v5, /device:TPU:1, one launch (start us, length us, event | category | flops | bytes accessed | tf_op | source)
XLA Modules:
  0.0 54.1 jit_solution(14698597783263406198)
XLA Ops:
  0.0 3.2 %collective-permute-start.5 = (bf16[1024,2048]{1,0:T(8,128)(2,1)}, bf16[1024,2048]{1,0:T(8,128)(2,1)S(1)}, u32[]{:S(2)}, u32[]{:S(2)}) collective-permute-start(bf16[1024,2048]{1,0:T(8,128)(2,1)} %bitcast.19), channel_id=1, source_target_pairs={{0,1},{1,0},{2,3},{3,2},{4,5},{5,4},{6,7},{7,6},{8,9},{9,8},{10,11... | collective-permute-start | bytes 12582920 | tf_op jit(solution)/shard_map/ppermute | solution.py:50
  3.2 0.9 %pad_maximum_fusion.own = bf16[24,2816]{1,0:T(8,128)(2,1)S(1)} fusion(bf16[24,768]{1,0:T(8,128)(2,1)} %bitcast.27, bf16[24,2048]{1,0:T(8,128)(2,1)} %bitcast.25), kind=kLoop, calls=%fused_computation.2 | loop fusion | flops 270336 | bytes 270336 | tf_op jit(solution)/shard_map/concatenate | solution.py:215
  4.2 1.5 %collective-permute-start.2 = (bf16[24,2816]{1,0:T(8,128)(2,1)S(1)}, bf16[24,2816]{1,0:T(8,128)(2,1)S(1)}, u32[]{:S(2)}, u32[]{:S(2)}) collective-permute-start(bf16[24,2816]{1,0:T(8,128)(2,1)S(1)} %pad_maximum_fusion.own), channel_id=1, source_target_pairs={{0,4},{1,17},{2,6},{3,19},{4,0},{5,21},{6,2},{7,23},{8,12},{9,25},... | collective-permute-start | bytes 405512 | tf_op jit(solution)/shard_map/ppermute | solution.py:50
  5.7 0.4 collective-permute-start
  6.1 2.3 %collective-permute-start.1 = (bf16[24,2816]{1,0:T(8,128)(2,1)S(1)}, bf16[24,2816]{1,0:T(8,128)(2,1)S(1)}, u32[]{:S(2)}, u32[]{:S(2)}) collective-permute-start(bf16[24,2816]{1,0:T(8,128)(2,1)S(1)} %pad_maximum_fusion.own), channel_id=1, source_target_pairs={{0,6},{1,25},{2,0},{3,27},{4,2},{5,29},{6,4},{7,31},{8,14},{9,1},{... | collective-permute-start | bytes 405512 | tf_op jit(solution)/shard_map/ppermute | solution.py:50
  8.4 3.1 %multiply_reduce_fusion = f32[1024]{0:T(1024)S(1)} fusion(bf16[1,1024,2048]{2,1,0:T(8,128)(2,1)} %param.6), kind=kLoop, calls=%fused_computation | loop fusion | flops 6290432 | bytes 4198400 | tf_op jit(solution)/shard_map/reduce_sum | solution.py:218
  11.5 2.8 %collective-permute-start.7 = (bf16[96,2816]{1,0:T(8,128)(2,1)S(1)}, bf16[96,2816]{1,0:T(8,128)(2,1)S(1)}, u32[]{:S(2)}, u32[]{:S(2)}) collective-permute-start(bf16[96,2816]{1,0:T(8,128)(2,1)S(1)} %line.1.w0), channel_id=1, source_target_pairs={{0,16},{1,5},{2,18},{3,7},{4,20},{5,1},{6,22},{7,3},{8,24},{9,13},... | collective-permute-start | bytes 1622024 | tf_op jit(solution)/shard_map/ppermute | solution.py:50
  15.0 0.4 collective-permute-start.3
  15.4 2.4 %collective-permute-start.4 = (bf16[96,2816]{1,0:T(8,128)(2,1)S(1)}, bf16[96,2816]{1,0:T(8,128)(2,1)S(1)}, u32[]{:S(2)}, u32[]{:S(2)}) collective-permute-start(bf16[96,2816]{1,0:T(8,128)(2,1)S(1)} %line.1.w0), channel_id=1, source_target_pairs={{0,24},{1,7},{2,26},{3,1},{4,28},{5,3},{6,30},{7,5},{8,0},{9,15},{... | collective-permute-start | bytes 1622024 | tf_op jit(solution)/shard_map/ppermute | solution.py:50
  17.8 1.4 %copy-done.1 = bf16[1,1024,768]{2,1,0:T(8,128)(2,1)S(1)} copy-done((bf16[1,1024,768]{2,1,0:T(8,128)(2,1)S(1)}, bf16[1,1024,768]{2,1,0:T(8,128)(2,1)}, u32[]{:S(2)}) %copy-start.1) | copy-done | bytes 1572888
  19.2 1.7 %turn.2 = (bf16[2048,1024]{1,0:T(8,128)(2,1)S(1)}, bf16[768,1024]{1,0:T(8,128)(2,1)S(1)}) custom-call(bf16[1024,2048]{1,0:T(8,128)(2,1)S(1)} %bitcast.20, bf16[1024,768]{1,0:T(8,128)(2,1)S(1)} %bitcast.22), custom_call_target="tpu_custom_call" | custom-call | bytes 6291456 | tf_op jit(solution)/shard_map/turn/pallas_call | solution.py:108
  20.9 0.4 multiply_reduce_fusion.1
  21.3 1.7 %turn.3 = (bf16[2048,1024]{1,0:T(8,128)(2,1)S(1)}, bf16[768,1024]{1,0:T(8,128)(2,1)S(1)}) custom-call(bf16[1024,2048]{1,0:T(8,128)(2,1)S(1)} %collective-permute-done.5.acts, bf16[1024,768]{1,0:T(8,128)(2,1)S(1)} %collective-permute-done.6.grads), custom_call_target="tpu_custom_call" | custom-call | bytes 6291456 | tf_op jit(solution)/shard_map/turn/pallas_call | solution.py:108
  23.0 1.9 %owners.1 = (bf16[1024,2048]{1,0:T(8,128)(2,1)S(1)}, f32[1,2048]{1,0:T(1,128)S(1)}, bf16[24,192]{1,0:T(8,128)(2,1)S(1)}, bf16[24,192]{1,0:T(8,128)(2,1)S(1)}) custom-call(s32[1,1024]{1,0:T(1,128)S(1)} %compare_select_fusion.tokens, f32[1,1024]{1,0:T(1,128)S(1)} %bitcast.24), custom_call_target="tpu_custom_call" | custom-call | flops 536870912 | bytes 8388608 | tf_op jit(solution)/shard_map/owners/pallas_call | solution.py:168
  24.8 1.5 %early_scores.3.rest_0_ = f32[24,1024]{1,0:T(8,128)S(1)} custom-call(bf16[2048,1024]{1,0:T(8,128)(2,1)S(1)} %get-tuple-element.26.acts, bf16[768,1024]{1,0:T(8,128)(2,1)S(1)} %get-tuple-element.27.grads, bf16[96,2816]{1,0:T(8,128)(2,1)S(1)} %line.1.w0, bf16[96,2816]{1,0:T(8,128)(2,1)S(1)} %collective-permute-done.7.w1, ...), custom_call_target="tpu_custom_call" | custom-call | flops 1107296256 | bytes 7340032 | tf_op jit(solution)/shard_map/early_scores/pallas_call | solution.py:134
  26.3 1.5 %early_scores.2.rest_0_ = f32[24,1024]{1,0:T(8,128)S(1)} custom-call(bf16[2048,1024]{1,0:T(8,128)(2,1)S(1)} %get-tuple-element.34.acts, bf16[768,1024]{1,0:T(8,128)(2,1)S(1)} %get-tuple-element.35.grads, bf16[96,2816]{1,0:T(8,128)(2,1)S(1)} %line.1.w0, bf16[96,2816]{1,0:T(8,128)(2,1)S(1)} %collective-permute-done.7.w1, ...), custom_call_target="tpu_custom_call" | custom-call | flops 1107296256 | bytes 7340032 | tf_op jit(solution)/shard_map/early_scores/pallas_call | solution.py:134
  27.9 0.0 collective-permute-done.4.w1
  27.9 1.5 %late_scores.3 = f32[24,1024]{1,0:T(8,128)S(1)} custom-call(bf16[2048,1024]{1,0:T(8,128)(2,1)S(1)} %get-tuple-element.34.acts, bf16[768,1024]{1,0:T(8,128)(2,1)S(1)} %get-tuple-element.35.grads, bf16[96,2816]{1,0:T(8,128)(2,1)S(1)} %collective-permute-done.3.w0, bf16[96,2816]{1,0:T(8,128)(2,1)S(1)} %collective-permute-done.4.w1, ...), custom_call_target="tpu_custom_call" | custom-call | flops 1107296256 | bytes 7340032 | tf_op jit(solution)/shard_map/late_scores/pallas_call | solution.py:134
  29.4 2.0 %collective-permute-start.8 = (f32[24,1024]{1,0:T(8,128)S(1)}, f32[24,1024]{1,0:T(8,128)S(1)}, u32[]{:S(2)}, u32[]{:S(2)}) collective-permute-start(f32[24,1024]{1,0:T(8,128)S(1)} %late_scores.3), channel_id=1, source_target_pairs={{0,1},{1,0},{2,3},{3,2},{4,5},{5,4},{6,7},{7,6},{8,9},{9,8},{10,11... | collective-permute-start | bytes 294920 | tf_op jit(solution)/shard_map/ppermute | solution.py:50
  31.4 1.5 %late_scores.2.mine = f32[24,1024]{1,0:T(8,128)S(1)} custom-call(bf16[2048,1024]{1,0:T(8,128)(2,1)S(1)} %get-tuple-element.26.acts, bf16[768,1024]{1,0:T(8,128)(2,1)S(1)} %get-tuple-element.27.grads, bf16[96,2816]{1,0:T(8,128)(2,1)S(1)} %collective-permute-done.3.w0, bf16[96,2816]{1,0:T(8,128)(2,1)S(1)} %collective-permute-done.4.w1, ...), custom_call_target="tpu_custom_call" | custom-call | flops 1107296256 | bytes 7340032 | tf_op jit(solution)/shard_map/late_scores/pallas_call | solution.py:134
  32.9 0.0 collective-permute-done.8.theirs
  33.0 0.8 %scatter.1 = f32[8,50,128]{2,1,0:T(8,128)S(1)} custom-call(f32[24,1024]{1,0:T(8,128)S(1)} %late_scores.2.mine, f32[24,1024]{1,0:T(8,128)S(1)} %collective-permute-done.8.theirs, bf16[1024,2048]{1,0:T(8,128)(2,1)S(1)} %get-tuple-element.39.onehot, f32[1,2048]{1,0:T(1,128)S(1)} %get-tuple-element.40.dense_norm), custom_call_target="tpu_custom_call" | custom-call | tf_op jit(solution)/shard_map/scatter/pallas_call | solution.py:200
  33.8 19.6 %all_to_all.5 = f32[8,50,128]{2,1,0:T(8,128)S(1)} all-to-all(f32[8,50,128]{2,1,0:T(8,128)S(1)} %scatter.1), channel_id=1, replica_groups=mesh['expert'=8,'dp'=32] {'expert'}, dimensions={0} | all-to-all | bytes 409600 | tf_op jit(solution)/shard_map/all_to_all | solution.py:242
  53.5 0.6 %copy_bitcast_fusion = f32[256,24]{0,1:T(8,128)} fusion(f32[2,24,128]{2,1,0:T(8,128)S(1)} %bitcast.26, f32[2,128]{1,0:T(2,128)S(1)} %fusion.2), kind=kLoop, calls=%fused_computation.3 | loop fusion | flops 6144 | bytes 50176 | tf_op jit(solution)/shard_map/reshape | solution.py:245
  (21 shorter events, 0.1 us)
Async XLA Ops:
  0.0 17.8 %copy-start = (bf16[1,1024,2048]{2,1,0:T(8,128)(2,1)S(1)}, bf16[1,1024,2048]{2,1,0:T(8,128)(2,1)}, u32[]{:S(2)}) copy-start(bf16[1,1024,2048]{2,1,0:T(8,128)(2,1)} %param.6) | copy-start | bytes 12582916
  0.0 17.7 %copy-start.3 = (s32[1,1024]{1,0:T(1,128)S(1)}, s32[1,1024]{1,0:T(1,128)}, u32[]{:S(2)}) copy-start(s32[1,1024]{1,0:T(1,128)} %param.11) | copy-start | bytes 12292
  0.0 21.3 %collective-permute-start.5 = (bf16[1024,2048]{1,0:T(8,128)(2,1)}, bf16[1024,2048]{1,0:T(8,128)(2,1)S(1)}, u32[]{:S(2)}, u32[]{:S(2)}) collective-permute-start(bf16[1024,2048]{1,0:T(8,128)(2,1)} %bitcast.19), channel_id=1, source_target_pairs={{0,1},{1,0},{2,3},{3,2},{4,5},{5,4},{6,7},{7,6},{8,9},{9,8},{10,11... | collective-permute-start | bytes 12582920 | tf_op jit(solution)/shard_map/ppermute | solution.py:50
  3.2 18.0 %collective-permute-start.6 = (bf16[1024,768]{1,0:T(8,128)(2,1)}, bf16[1024,768]{1,0:T(8,128)(2,1)S(1)}, u32[]{:S(2)}, u32[]{:S(2)}) collective-permute-start(bf16[1024,768]{1,0:T(8,128)(2,1)} %bitcast.21), channel_id=1, source_target_pairs={{0,1},{1,0},{2,3},{3,2},{4,5},{5,4},{6,7},{7,6},{8,9},{9,8},{10,11... | collective-permute-start | bytes 4718600 | tf_op jit(solution)/shard_map/ppermute | solution.py:50
  4.2 7.3 %collective-permute-start.2 = (bf16[24,2816]{1,0:T(8,128)(2,1)S(1)}, bf16[24,2816]{1,0:T(8,128)(2,1)S(1)}, u32[]{:S(2)}, u32[]{:S(2)}) collective-permute-start(bf16[24,2816]{1,0:T(8,128)(2,1)S(1)} %pad_maximum_fusion.own), channel_id=1, source_target_pairs={{0,4},{1,17},{2,6},{3,19},{4,0},{5,21},{6,2},{7,23},{8,12},{9,25},... | collective-permute-start | bytes 405512 | tf_op jit(solution)/shard_map/ppermute | solution.py:50
  5.7 5.8 %collective-permute-start = (bf16[24,2816]{1,0:T(8,128)(2,1)S(1)}, bf16[24,2816]{1,0:T(8,128)(2,1)S(1)}, u32[]{:S(2)}, u32[]{:S(2)}) collective-permute-start(bf16[24,2816]{1,0:T(8,128)(2,1)S(1)} %pad_maximum_fusion.own), channel_id=1, source_target_pairs={{0,2},{1,9},{2,4},{3,11},{4,6},{5,13},{6,0},{7,15},{8,10},{9,17},{... | collective-permute-start | bytes 405512 | tf_op jit(solution)/shard_map/ppermute | solution.py:50
  6.1 5.4 %collective-permute-start.1 = (bf16[24,2816]{1,0:T(8,128)(2,1)S(1)}, bf16[24,2816]{1,0:T(8,128)(2,1)S(1)}, u32[]{:S(2)}, u32[]{:S(2)}) collective-permute-start(bf16[24,2816]{1,0:T(8,128)(2,1)S(1)} %pad_maximum_fusion.own), channel_id=1, source_target_pairs={{0,6},{1,25},{2,0},{3,27},{4,2},{5,29},{6,4},{7,31},{8,14},{9,1},{... | collective-permute-start | bytes 405512 | tf_op jit(solution)/shard_map/ppermute | solution.py:50
  11.5 13.3 %collective-permute-start.7 = (bf16[96,2816]{1,0:T(8,128)(2,1)S(1)}, bf16[96,2816]{1,0:T(8,128)(2,1)S(1)}, u32[]{:S(2)}, u32[]{:S(2)}) collective-permute-start(bf16[96,2816]{1,0:T(8,128)(2,1)S(1)} %line.1.w0), channel_id=1, source_target_pairs={{0,16},{1,5},{2,18},{3,7},{4,20},{5,1},{6,22},{7,3},{8,24},{9,13},... | collective-permute-start | bytes 1622024 | tf_op jit(solution)/shard_map/ppermute | solution.py:50
  15.0 12.9 %collective-permute-start.3 = (bf16[96,2816]{1,0:T(8,128)(2,1)S(1)}, bf16[96,2816]{1,0:T(8,128)(2,1)S(1)}, u32[]{:S(2)}, u32[]{:S(2)}) collective-permute-start(bf16[96,2816]{1,0:T(8,128)(2,1)S(1)} %line.1.w0), channel_id=1, source_target_pairs={{0,8},{1,3},{2,10},{3,5},{4,12},{5,7},{6,14},{7,1},{8,16},{9,11},{... | collective-permute-start | bytes 1622024 | tf_op jit(solution)/shard_map/ppermute | solution.py:50
  15.4 12.5 %collective-permute-start.4 = (bf16[96,2816]{1,0:T(8,128)(2,1)S(1)}, bf16[96,2816]{1,0:T(8,128)(2,1)S(1)}, u32[]{:S(2)}, u32[]{:S(2)}) collective-permute-start(bf16[96,2816]{1,0:T(8,128)(2,1)S(1)} %line.1.w0), channel_id=1, source_target_pairs={{0,24},{1,7},{2,26},{3,1},{4,28},{5,3},{6,30},{7,5},{8,0},{9,15},{... | collective-permute-start | bytes 1622024 | tf_op jit(solution)/shard_map/ppermute | solution.py:50
  17.8 1.4 %copy-start.1 = (bf16[1,1024,768]{2,1,0:T(8,128)(2,1)S(1)}, bf16[1,1024,768]{2,1,0:T(8,128)(2,1)}, u32[]{:S(2)}) copy-start(bf16[1,1024,768]{2,1,0:T(8,128)(2,1)} %param.7) | copy-start | bytes 4718596
  19.2 1.7 %copy-start.2 = (bf16[1,1024,768]{2,1,0:T(8,128)(2,1)S(1)}, bf16[1,1024,768]{2,1,0:T(8,128)(2,1)}, u32[]{:S(2)}) copy-start(bf16[1,1024,768]{2,1,0:T(8,128)(2,1)} %param.7) | copy-start | bytes 4718596
  29.4 3.6 %collective-permute-start.8 = (f32[24,1024]{1,0:T(8,128)S(1)}, f32[24,1024]{1,0:T(8,128)S(1)}, u32[]{:S(2)}, u32[]{:S(2)}) collective-permute-start(f32[24,1024]{1,0:T(8,128)S(1)} %late_scores.3), channel_id=1, source_target_pairs={{0,1},{1,0},{2,3},{3,2},{4,5},{5,4},{6,7},{7,6},{8,9},{9,8},{10,11... | collective-permute-start | bytes 294920 | tf_op jit(solution)/shard_map/ppermute | solution.py:50

commit v6 on v5

--- a/solution.py
+++ b/solution.py
@@ -15,6 +15,7 @@
 SIDE = 4
 FIRST = (0, -1, 1, 2)
 SECOND = (0, 2, -1, 1)
+STEPS = (3, 2, 1)
 HALF = TOK_DEV // 2
 
 epsilon = 1e-06
@@ -183,30 +184,68 @@
     )(tokens, norms)
 
 
-def scatter_kernel(mine, theirs, onehot, dense_norm, out):
+def scatter_kernel(mine, theirs, onehot, dense_norm, *rest):
+    *outs, dense = rest
     table = jnp.concatenate(split(mine[...] + theirs[...], 3), 0)
     part = jnp.dot(table, onehot[...], preferred_element_type=jnp.float32)
     part = part[:QUERIES] + part[QUERIES : 2 * QUERIES] + part[2 * QUERIES :]
-    for i in range(out.shape[0]):
+    experts = dense.shape[0]
+    for i in range(experts):
         for half in range(2):
             start = i * TOK_DEV + half * HALF
             owned = slice(start, start + HALF)
-            out[i, half * QUERIES : (half + 1) * QUERIES, :] = part[:, owned]
-            out[i, 2 * QUERIES + half : 2 * QUERIES + half + 1, :] = dense_norm[:, owned]
+            dense[i, half * QUERIES : (half + 1) * QUERIES, :] = part[:, owned]
+            dense[i, 2 * QUERIES + half : 2 * QUERIES + half + 1, :] = dense_norm[:, owned]
+    pair = lax.axis_index("expert") >> 1
+    for out, step in zip(outs, (0, *STEPS)):
+        first = ((pair + step) & (experts // 2 - 1)) * 2
+        out[...] = dense[pl.ds(first, 2)]
 
 
 def scatter(mine, theirs, onehot, dense_norm):
-    shard_tokens = onehot.shape[1]
+    block = (2 * QUERIES + 2, HALF)
+    experts = onehot.shape[1] // TOK_DEV
     return pl.pallas_call(
         scatter_kernel,
-        out_shape=jax.ShapeDtypeStruct(
-            (shard_tokens // TOK_DEV, 2 * QUERIES + 2, HALF), jnp.float32
-        ),
+        out_shape=(jax.ShapeDtypeStruct((2, *block), jnp.float32),) * (1 + len(STEPS)),
         in_specs=[VMEM] * 4,
-        out_specs=VMEM,
+        out_specs=(VMEM,) * (1 + len(STEPS)),
+        scratch_shapes=[pltpu.VMEM((experts, *block), jnp.float32)],
         compiler_params=pltpu.CompilerParams(vmem_limit_bytes=2 << 20),
         name="scatter",
     )(mine, theirs, onehot, dense_norm)
+
+
+def combine_kernel(own, *rest):
+    *others, keep, give, total = rest
+    total[...] = own[...]
+    for other in others:
+        total[...] += other[...]
+    parity = lax.axis_index("expert") & 1
+    keep[...] = total[parity]
+    give[...] = total[1 - parity]
+
+
+def combine(blocks):
+    shape = blocks[0].shape
+    return pl.pallas_call(
+        combine_kernel,
+        out_shape=(jax.ShapeDtypeStruct(shape[1:], jnp.float32),) * 2,
+        in_specs=[VMEM] * len(blocks),
+        out_specs=(VMEM, VMEM),
+        scratch_shapes=[pltpu.VMEM(shape, jnp.float32)],
+        compiler_params=pltpu.CompilerParams(vmem_limit_bytes=1 << 20),
+        name="combine",
+    )(*blocks)
+
+
+def exchange(blocks, experts):
+    parts = [blocks[0]]
+    for block, step in zip(blocks[1:], STEPS):
+        table = [(z, (z + 2 * step) % experts) for z in range(experts)]
+        parts.append(lax.ppermute(block, "expert", table))
+    keep, give = combine(parts)
+    return keep + lax.ppermute(give, "expert", [(z, z ^ 1) for z in range(experts)])
 
 
 def local(row_acts, row_grads, grad_factor, value_factor, counts, row_token):
@@ -238,8 +277,7 @@
     for_them = row_scores(*their_rows, pieces[2:], late, for_them)
     theirs = send(for_them, SIBLING)
     mine = row_scores(*my_rows, pieces[2:], late, mine)
-    dense = scatter(mine, theirs, onehot, dense_norm)
-    summed = lax.all_to_all(dense, "expert", 0, 0).sum(0)
+    summed = exchange(scatter(mine, theirs, onehot, dense_norm), experts)
     totals, norm_sum = summed[: 2 * QUERIES].reshape(2, QUERIES, HALF), summed[2 * QUERIES :]
     factor = lax.rsqrt(norm_sum / (MODEL * MOE_FF) + epsilon) / jnp.sqrt(jnp.float32(RANK))
     return (totals * factor[:, None, :]).transpose(0, 2, 1).reshape(TOK_DEV, QUERIES)

time: 54.3 us -> 52.1 us (0.959)
  the two profiles are of different devices: /device:TPU:1 before, /device:TPU:6 now
where the time goes in v6:
time: 52.1 us; the launch traced here: 52 us
  starting transfers between devices  23.4 us (45%)
  Pallas kernels  12.1 us (23%)
  waiting for transfers between devices  9.11 us (17%)
  other arithmetic  5.03 us (10%)
  local copies, waits for them, and re-layouts  1.42 us (3%)
  between operations  0.82 us (2%)
    ppermute x3, starting transfers between devices, exchange(): parts.append(lax.ppermute(block, 'expert', table))  11.4 us
    ppermute x9, starting transfers between devices, send(): return lax.ppermute(value, 'dp', table)  10.8 us
    pallas_call x4, Pallas kernels, row_scores(): pl.pallas_call(scores_kernel, out_shape=jax.ShapeDtypeStruct((QUERIES, ro...  6.01 us
    pallas_call x2, Pallas kernels, turn(): pl.pallas_call(turn_kernel, out_shape=tuple((jax.ShapeDtypeStruct(x.shape...  3.33 us
    ppermute x3, waiting for transfers between devices, exchange(): parts.append(lax.ppermute(block, 'expert', table))  3.22 us
    ppermute x9, waiting for transfers between devices, send(): return lax.ppermute(value, 'dp', table)  3.18 us
    reduce_sum x1, other arithmetic, local(): acts_norm = jnp.sum(jnp.square(acts.astype(jnp.float32)), 1)  3.07 us
    ppermute x1, waiting for transfers between devices, exchange(): lax.ppermute(give, 'expert', [(z, z ^ 1) for z in range(experts)])  2.71 us
  transfers between devices with their start and end apart: 13, of which 5 were waited for; matrix products, arithmetic and copies ran while one was open for 8% of the time, Pallas kernels for 19%

profile of v6, /device:TPU:6, one launch (start us, length us, event | category | flops | bytes accessed | tf_op | source)
XLA Modules:
  0.0 52.0 jit_solution(7227084230837174851)
XLA Ops:
  0.5 0.9 %pad_maximum_fusion.own = bf16[24,2816]{1,0:T(8,128)(2,1)S(1)} fusion(bf16[24,768]{1,0:T(8,128)(2,1)} %bitcast.27, bf16[24,2048]{1,0:T(8,128)(2,1)} %bitcast.25), kind=kLoop, calls=%fused_computation.2 | loop fusion | flops 270336 | bytes 270336 | tf_op jit(solution)/shard_map/concatenate | solution.py:254
  1.5 1.5 %collective-permute-start.2 = (bf16[24,2816]{1,0:T(8,128)(2,1)S(1)}, bf16[24,2816]{1,0:T(8,128)(2,1)S(1)}, u32[]{:S(2)}, u32[]{:S(2)}) collective-permute-start(bf16[24,2816]{1,0:T(8,128)(2,1)S(1)} %pad_maximum_fusion.own), channel_id=1, source_target_pairs={{0,4},{1,17},{2,6},{3,19},{4,0},{5,21},{6,2},{7,23},{8,12},{9,25},... | collective-permute-start | bytes 405512 | tf_op jit(solution)/shard_map/ppermute | solution.py:51
  3.0 2.1 %collective-permute-start = (bf16[24,2816]{1,0:T(8,128)(2,1)S(1)}, bf16[24,2816]{1,0:T(8,128)(2,1)S(1)}, u32[]{:S(2)}, u32[]{:S(2)}) collective-permute-start(bf16[24,2816]{1,0:T(8,128)(2,1)S(1)} %pad_maximum_fusion.own), channel_id=1, source_target_pairs={{0,2},{1,9},{2,4},{3,11},{4,6},{5,13},{6,0},{7,15},{8,10},{9,17},{... | collective-permute-start | bytes 405512 | tf_op jit(solution)/shard_map/ppermute | solution.py:51
  5.1 3.1 %multiply_reduce_fusion = f32[1024]{0:T(1024)S(1)} fusion(bf16[1,1024,2048]{2,1,0:T(8,128)(2,1)} %param.6), kind=kLoop, calls=%fused_computation | loop fusion | flops 6290432 | bytes 4198400 | tf_op jit(solution)/shard_map/reduce_sum | solution.py:257
  8.1 0.9 %collective-permute-done.before = bf16[24,2816]{1,0:T(8,128)(2,1)S(1)} collective-permute-done((bf16[24,2816]{1,0:T(8,128)(2,1)S(1)}, bf16[24,2816]{1,0:T(8,128)(2,1)S(1)}, u32[]{:S(2)}, u32[]{:S(2)}) %collective-permute-start) | collective-permute-done | bytes 135200 | tf_op jit(solution)/shard_map/ppermute | solution.py:51
  9.1 2.2 %collective-permute-done.1.after = bf16[24,2816]{1,0:T(8,128)(2,1)S(1)} collective-permute-done((bf16[24,2816]{1,0:T(8,128)(2,1)S(1)}, bf16[24,2816]{1,0:T(8,128)(2,1)S(1)}, u32[]{:S(2)}, u32[]{:S(2)}) %collective-permute-start.1) | collective-permute-done | bytes 135200 | tf_op jit(solution)/shard_map/ppermute | solution.py:51
  11.3 3.3 %collective-permute-start.7 = (bf16[96,2816]{1,0:T(8,128)(2,1)S(1)}, bf16[96,2816]{1,0:T(8,128)(2,1)S(1)}, u32[]{:S(2)}, u32[]{:S(2)}) collective-permute-start(bf16[96,2816]{1,0:T(8,128)(2,1)S(1)} %line.1.w0), channel_id=1, source_target_pairs={{0,16},{1,5},{2,18},{3,7},{4,20},{5,1},{6,22},{7,3},{8,24},{9,13},... | collective-permute-start | bytes 1622024 | tf_op jit(solution)/shard_map/ppermute | solution.py:51
  16.0 2.6 %collective-permute-start.4 = (bf16[96,2816]{1,0:T(8,128)(2,1)S(1)}, bf16[96,2816]{1,0:T(8,128)(2,1)S(1)}, u32[]{:S(2)}, u32[]{:S(2)}) collective-permute-start(bf16[96,2816]{1,0:T(8,128)(2,1)S(1)} %line.1.w0), channel_id=1, source_target_pairs={{0,24},{1,7},{2,26},{3,1},{4,28},{5,3},{6,30},{7,5},{8,0},{9,15},{... | collective-permute-start | bytes 1622024 | tf_op jit(solution)/shard_map/ppermute | solution.py:51
  18.6 1.4 %copy-done.1 = bf16[1,1024,768]{2,1,0:T(8,128)(2,1)S(1)} copy-done((bf16[1,1024,768]{2,1,0:T(8,128)(2,1)S(1)}, bf16[1,1024,768]{2,1,0:T(8,128)(2,1)}, u32[]{:S(2)}) %copy-start.1) | copy-done | bytes 1572888
  20.0 1.7 %turn.2 = (bf16[2048,1024]{1,0:T(8,128)(2,1)S(1)}, bf16[768,1024]{1,0:T(8,128)(2,1)S(1)}) custom-call(bf16[1024,2048]{1,0:T(8,128)(2,1)S(1)} %bitcast.20, bf16[1024,768]{1,0:T(8,128)(2,1)S(1)} %bitcast.22), custom_call_target="tpu_custom_call" | custom-call | bytes 6291456 | tf_op jit(solution)/shard_map/turn/pallas_call | solution.py:109
  22.1 1.7 %turn.3 = (bf16[2048,1024]{1,0:T(8,128)(2,1)S(1)}, bf16[768,1024]{1,0:T(8,128)(2,1)S(1)}) custom-call(bf16[1024,2048]{1,0:T(8,128)(2,1)S(1)} %collective-permute-done.5.acts, bf16[1024,768]{1,0:T(8,128)(2,1)S(1)} %collective-permute-done.6.grads), custom_call_target="tpu_custom_call" | custom-call | bytes 6291456 | tf_op jit(solution)/shard_map/turn/pallas_call | solution.py:109
  23.8 1.9 %owners.1 = (bf16[1024,2048]{1,0:T(8,128)(2,1)S(1)}, f32[1,2048]{1,0:T(1,128)S(1)}, bf16[24,192]{1,0:T(8,128)(2,1)S(1)}, bf16[24,192]{1,0:T(8,128)(2,1)S(1)}) custom-call(s32[1,1024]{1,0:T(1,128)S(1)} %compare_select_fusion.tokens, f32[1,1024]{1,0:T(1,128)S(1)} %bitcast.24), custom_call_target="tpu_custom_call" | custom-call | flops 536870912 | bytes 8388608 | tf_op jit(solution)/shard_map/owners/pallas_call | solution.py:169
  25.6 1.5 %early_scores.3.rest_0_ = f32[24,1024]{1,0:T(8,128)S(1)} custom-call(bf16[2048,1024]{1,0:T(8,128)(2,1)S(1)} %get-tuple-element.32.acts, bf16[768,1024]{1,0:T(8,128)(2,1)S(1)} %get-tuple-element.33.grads, bf16[96,2816]{1,0:T(8,128)(2,1)S(1)} %line.1.w0, bf16[96,2816]{1,0:T(8,128)(2,1)S(1)} %collective-permute-done.7.w1, ...), custom_call_target="tpu_custom_call" | custom-call | flops 1107296256 | bytes 7340032 | tf_op jit(solution)/shard_map/early_scores/pallas_call | solution.py:135
  27.2 1.5 %early_scores.2.rest_0_ = f32[24,1024]{1,0:T(8,128)S(1)} custom-call(bf16[2048,1024]{1,0:T(8,128)(2,1)S(1)} %get-tuple-element.40.acts, bf16[768,1024]{1,0:T(8,128)(2,1)S(1)} %get-tuple-element.41.grads, bf16[96,2816]{1,0:T(8,128)(2,1)S(1)} %line.1.w0, bf16[96,2816]{1,0:T(8,128)(2,1)S(1)} %collective-permute-done.7.w1, ...), custom_call_target="tpu_custom_call" | custom-call | flops 1107296256 | bytes 7340032 | tf_op jit(solution)/shard_map/early_scores/pallas_call | solution.py:135
  28.7 1.5 %late_scores.3 = f32[24,1024]{1,0:T(8,128)S(1)} custom-call(bf16[2048,1024]{1,0:T(8,128)(2,1)S(1)} %get-tuple-element.40.acts, bf16[768,1024]{1,0:T(8,128)(2,1)S(1)} %get-tuple-element.41.grads, bf16[96,2816]{1,0:T(8,128)(2,1)S(1)} %collective-permute-done.3.w0, bf16[96,2816]{1,0:T(8,128)(2,1)S(1)} %collective-permute-done.4.w1, ...), custom_call_target="tpu_custom_call" | custom-call | flops 1107296256 | bytes 7340032 | tf_op jit(solution)/shard_map/late_scores/pallas_call | solution.py:135
  30.3 1.5 %late_scores.2.mine = f32[24,1024]{1,0:T(8,128)S(1)} custom-call(bf16[2048,1024]{1,0:T(8,128)(2,1)S(1)} %get-tuple-element.32.acts, bf16[768,1024]{1,0:T(8,128)(2,1)S(1)} %get-tuple-element.33.grads, bf16[96,2816]{1,0:T(8,128)(2,1)S(1)} %collective-permute-done.3.w0, bf16[96,2816]{1,0:T(8,128)(2,1)S(1)} %collective-permute-done.4.w1, ...), custom_call_target="tpu_custom_call" | custom-call | flops 1107296256 | bytes 7340032 | tf_op jit(solution)/shard_map/late_scores/pallas_call | solution.py:135
  31.8 0.9 %scatter.1 = (f32[2,50,128]{2,1,0:T(8,128)S(1)}, f32[2,50,128]{2,1,0:T(8,128)S(1)}, f32[2,50,128]{2,1,0:T(8,128)S(1)}, f32[2,50,128]{2,1,0:T(8,128)S(1)}) custom-call(f32[24,1024]{1,0:T(8,128)S(1)} %late_scores.2.mine, f32[24,1024]{1,0:T(8,128)S(1)} %collective-permute-done.8.theirs, bf16[1024,2048]{1,0:T(8,128)(2,1)S(1)} %get-tuple-element.45.onehot, ...), custom_call_target="tpu_custom_call" | custom-call | tf_op jit(solution)/shard_map/scatter/pallas_call | solution.py:208
  32.7 7.3 %collective-permute-start.10 = (f32[2,50,128]{2,1,0:T(8,128)S(1)}, f32[2,50,128]{2,1,0:T(8,128)S(1)}, u32[]{:S(2)}, u32[]{:S(2)}) collective-permute-start(f32[2,50,128]{2,1,0:T(8,128)S(1)} %get-tuple-element.49), channel_id=1, source_target_pairs={{0,128},{32,160},{64,192},{96,224},{128,0},{160,32},{192,64},{224,... | collective-permute-start | bytes 153608 | tf_op jit(solution)/shard_map/ppermute | solution.py:246
  40.0 1.5 %collective-permute-start.11 = (f32[2,50,128]{2,1,0:T(8,128)S(1)}, f32[2,50,128]{2,1,0:T(8,128)S(1)}, u32[]{:S(2)}, u32[]{:S(2)}) collective-permute-start(f32[2,50,128]{2,1,0:T(8,128)S(1)} %get-tuple-element.50), channel_id=1, source_target_pairs={{0,64},{32,96},{64,128},{96,160},{128,192},{160,224},{192,0},{224,... | collective-permute-start | bytes 153608 | tf_op jit(solution)/shard_map/ppermute | solution.py:246
  41.5 2.7 %collective-permute-start.9 = (f32[2,50,128]{2,1,0:T(8,128)S(1)}, f32[2,50,128]{2,1,0:T(8,128)S(1)}, u32[]{:S(2)}, u32[]{:S(2)}) collective-permute-start(f32[2,50,128]{2,1,0:T(8,128)S(1)} %get-tuple-element.48), channel_id=1, source_target_pairs={{0,192},{32,224},{64,0},{96,32},{128,64},{160,96},{192,128},{224,1... | collective-permute-start | bytes 153608 | tf_op jit(solution)/shard_map/ppermute | solution.py:246
  44.1 2.4 %collective-permute-done.11.rest_2_ = f32[2,50,128]{2,1,0:T(8,128)S(1)} collective-permute-done((f32[2,50,128]{2,1,0:T(8,128)S(1)}, f32[2,50,128]{2,1,0:T(8,128)S(1)}, u32[]{:S(2)}, u32[]{:S(2)}) %collective-permute-start.11) | collective-permute-done | bytes 51232 | tf_op jit(solution)/shard_map/ppermute | solution.py:246
  46.6 0.8 %collective-permute-done.9.rest_0_ = f32[2,50,128]{2,1,0:T(8,128)S(1)} collective-permute-done((f32[2,50,128]{2,1,0:T(8,128)S(1)}, f32[2,50,128]{2,1,0:T(8,128)S(1)}, u32[]{:S(2)}, u32[]{:S(2)}) %collective-permute-start.9) | collective-permute-done | bytes 51232 | tf_op jit(solution)/shard_map/ppermute | solution.py:246
  47.4 1.2 %collective-permute-start.12 = (f32[50,128]{1,0:T(8,128)S(1)}, f32[50,128]{1,0:T(8,128)S(1)}, u32[]{:S(2)}, u32[]{:S(2)}) collective-permute-start(f32[50,128]{1,0:T(8,128)S(1)} %get-tuple-element.52), channel_id=1, source_target_pairs={{0,32},{32,0},{64,96},{96,64},{128,160},{160,128},{192,224},{224,1... | collective-permute-start | bytes 76808 | tf_op jit(solution)/shard_map/ppermute | solution.py:248
  48.6 2.7 %collective-permute-done.12 = f32[50,128]{1,0:T(8,128)S(1)} collective-permute-done((f32[50,128]{1,0:T(8,128)S(1)}, f32[50,128]{1,0:T(8,128)S(1)}, u32[]{:S(2)}, u32[]{:S(2)}) %collective-permute-start.12) | collective-permute-done | bytes 25632 | tf_op jit(solution)/shard_map/ppermute | solution.py:248
  (29 shorter events, 2.5 us)
Async XLA Ops:
  0.0 18.6 %copy-start = (bf16[1,1024,2048]{2,1,0:T(8,128)(2,1)S(1)}, bf16[1,1024,2048]{2,1,0:T(8,128)(2,1)}, u32[]{:S(2)}) copy-start(bf16[1,1024,2048]{2,1,0:T(8,128)(2,1)} %param.6) | copy-start | bytes 12582916
  0.0 18.6 %copy-start.3 = (s32[1,1024]{1,0:T(1,128)S(1)}, s32[1,1024]{1,0:T(1,128)}, u32[]{:S(2)}) copy-start(s32[1,1024]{1,0:T(1,128)} %param.11) | copy-start | bytes 12292
  0.0 22.1 %collective-permute-start.5 = (bf16[1024,2048]{1,0:T(8,128)(2,1)}, bf16[1024,2048]{1,0:T(8,128)(2,1)S(1)}, u32[]{:S(2)}, u32[]{:S(2)}) collective-permute-start(bf16[1024,2048]{1,0:T(8,128)(2,1)} %bitcast.19), channel_id=1, source_target_pairs={{0,1},{1,0},{2,3},{3,2},{4,5},{5,4},{6,7},{7,6},{8,9},{9,8},{10,11... | collective-permute-start | bytes 12582920 | tf_op jit(solution)/shard_map/ppermute | solution.py:51
  0.0 22.1 %collective-permute-start.6 = (bf16[1024,768]{1,0:T(8,128)(2,1)}, bf16[1024,768]{1,0:T(8,128)(2,1)S(1)}, u32[]{:S(2)}, u32[]{:S(2)}) collective-permute-start(bf16[1024,768]{1,0:T(8,128)(2,1)} %bitcast.21), channel_id=1, source_target_pairs={{0,1},{1,0},{2,3},{3,2},{4,5},{5,4},{6,7},{7,6},{8,9},{9,8},{10,11... | collective-permute-start | bytes 4718600 | tf_op jit(solution)/shard_map/ppermute | solution.py:51
  1.5 6.7 %collective-permute-start.2 = (bf16[24,2816]{1,0:T(8,128)(2,1)S(1)}, bf16[24,2816]{1,0:T(8,128)(2,1)S(1)}, u32[]{:S(2)}, u32[]{:S(2)}) collective-permute-start(bf16[24,2816]{1,0:T(8,128)(2,1)S(1)} %pad_maximum_fusion.own), channel_id=1, source_target_pairs={{0,4},{1,17},{2,6},{3,19},{4,0},{5,21},{6,2},{7,23},{8,12},{9,25},... | collective-permute-start | bytes 405512 | tf_op jit(solution)/shard_map/ppermute | solution.py:51
  3.0 6.1 %collective-permute-start = (bf16[24,2816]{1,0:T(8,128)(2,1)S(1)}, bf16[24,2816]{1,0:T(8,128)(2,1)S(1)}, u32[]{:S(2)}, u32[]{:S(2)}) collective-permute-start(bf16[24,2816]{1,0:T(8,128)(2,1)S(1)} %pad_maximum_fusion.own), channel_id=1, source_target_pairs={{0,2},{1,9},{2,4},{3,11},{4,6},{5,13},{6,0},{7,15},{8,10},{9,17},{... | collective-permute-start | bytes 405512 | tf_op jit(solution)/shard_map/ppermute | solution.py:51
  5.1 6.2 %collective-permute-start.1 = (bf16[24,2816]{1,0:T(8,128)(2,1)S(1)}, bf16[24,2816]{1,0:T(8,128)(2,1)S(1)}, u32[]{:S(2)}, u32[]{:S(2)}) collective-permute-start(bf16[24,2816]{1,0:T(8,128)(2,1)S(1)} %pad_maximum_fusion.own), channel_id=1, source_target_pairs={{0,6},{1,25},{2,0},{3,27},{4,2},{5,29},{6,4},{7,31},{8,14},{9,1},{... | collective-permute-start | bytes 405512 | tf_op jit(solution)/shard_map/ppermute | solution.py:51
  11.3 14.3 %collective-permute-start.7 = (bf16[96,2816]{1,0:T(8,128)(2,1)S(1)}, bf16[96,2816]{1,0:T(8,128)(2,1)S(1)}, u32[]{:S(2)}, u32[]{:S(2)}) collective-permute-start(bf16[96,2816]{1,0:T(8,128)(2,1)S(1)} %line.1.w0), channel_id=1, source_target_pairs={{0,16},{1,5},{2,18},{3,7},{4,20},{5,1},{6,22},{7,3},{8,24},{9,13},... | collective-permute-start | bytes 1622024 | tf_op jit(solution)/shard_map/ppermute | solution.py:51
  15.3 13.4 %collective-permute-start.3 = (bf16[96,2816]{1,0:T(8,128)(2,1)S(1)}, bf16[96,2816]{1,0:T(8,128)(2,1)S(1)}, u32[]{:S(2)}, u32[]{:S(2)}) collective-permute-start(bf16[96,2816]{1,0:T(8,128)(2,1)S(1)} %line.1.w0), channel_id=1, source_target_pairs={{0,8},{1,3},{2,10},{3,5},{4,12},{5,7},{6,14},{7,1},{8,16},{9,11},{... | collective-permute-start | bytes 1622024 | tf_op jit(solution)/shard_map/ppermute | solution.py:51
  16.0 12.7 %collective-permute-start.4 = (bf16[96,2816]{1,0:T(8,128)(2,1)S(1)}, bf16[96,2816]{1,0:T(8,128)(2,1)S(1)}, u32[]{:S(2)}, u32[]{:S(2)}) collective-permute-start(bf16[96,2816]{1,0:T(8,128)(2,1)S(1)} %line.1.w0), channel_id=1, source_target_pairs={{0,24},{1,7},{2,26},{3,1},{4,28},{5,3},{6,30},{7,5},{8,0},{9,15},{... | collective-permute-start | bytes 1622024 | tf_op jit(solution)/shard_map/ppermute | solution.py:51
  18.6 1.4 %copy-start.1 = (bf16[1,1024,768]{2,1,0:T(8,128)(2,1)S(1)}, bf16[1,1024,768]{2,1,0:T(8,128)(2,1)}, u32[]{:S(2)}) copy-start(bf16[1,1024,768]{2,1,0:T(8,128)(2,1)} %param.7) | copy-start | bytes 4718596
  20.0 1.7 %copy-start.2 = (bf16[1,1024,768]{2,1,0:T(8,128)(2,1)S(1)}, bf16[1,1024,768]{2,1,0:T(8,128)(2,1)}, u32[]{:S(2)}) copy-start(bf16[1,1024,768]{2,1,0:T(8,128)(2,1)} %param.7) | copy-start | bytes 4718596
  30.2 1.6 %collective-permute-start.8 = (f32[24,1024]{1,0:T(8,128)S(1)}, f32[24,1024]{1,0:T(8,128)S(1)}, u32[]{:S(2)}, u32[]{:S(2)}) collective-permute-start(f32[24,1024]{1,0:T(8,128)S(1)} %late_scores.3), channel_id=1, source_target_pairs={{0,1},{1,0},{2,3},{3,2},{4,5},{5,4},{6,7},{7,6},{8,9},{9,8},{10,11... | collective-permute-start | bytes 294920 | tf_op jit(solution)/shard_map/ppermute | solution.py:51
  32.7 11.4 %collective-permute-start.10 = (f32[2,50,128]{2,1,0:T(8,128)S(1)}, f32[2,50,128]{2,1,0:T(8,128)S(1)}, u32[]{:S(2)}, u32[]{:S(2)}) collective-permute-start(f32[2,50,128]{2,1,0:T(8,128)S(1)} %get-tuple-element.49), channel_id=1, source_target_pairs={{0,128},{32,160},{64,192},{96,224},{128,0},{160,32},{192,64},{224,... | collective-permute-start | bytes 153608 | tf_op jit(solution)/shard_map/ppermute | solution.py:246
  40.0 6.6 %collective-permute-start.11 = (f32[2,50,128]{2,1,0:T(8,128)S(1)}, f32[2,50,128]{2,1,0:T(8,128)S(1)}, u32[]{:S(2)}, u32[]{:S(2)}) collective-permute-start(f32[2,50,128]{2,1,0:T(8,128)S(1)} %get-tuple-element.50), channel_id=1, source_target_pairs={{0,64},{32,96},{64,128},{96,160},{128,192},{160,224},{192,0},{224,... | collective-permute-start | bytes 153608 | tf_op jit(solution)/shard_map/ppermute | solution.py:246
  41.5 5.9 %collective-permute-start.9 = (f32[2,50,128]{2,1,0:T(8,128)S(1)}, f32[2,50,128]{2,1,0:T(8,128)S(1)}, u32[]{:S(2)}, u32[]{:S(2)}) collective-permute-start(f32[2,50,128]{2,1,0:T(8,128)S(1)} %get-tuple-element.48), channel_id=1, source_target_pairs={{0,192},{32,224},{64,0},{96,32},{128,64},{160,96},{192,128},{224,1... | collective-permute-start | bytes 153608 | tf_op jit(solution)/shard_map/ppermute | solution.py:246
  47.4 4.0 %collective-permute-start.12 = (f32[50,128]{1,0:T(8,128)S(1)}, f32[50,128]{1,0:T(8,128)S(1)}, u32[]{:S(2)}, u32[]{:S(2)}) collective-permute-start(f32[50,128]{1,0:T(8,128)S(1)} %get-tuple-element.52), channel_id=1, source_target_pairs={{0,32},{32,0},{64,96},{96,64},{128,160},{160,128},{192,224},{224,1... | collective-permute-start | bytes 76808 | tf_op jit(solution)/shard_map/ppermute | solution.py:248

commit v7 on v6

--- a/solution.py
+++ b/solution.py
@@ -21,6 +21,7 @@
 epsilon = 1e-06
 
 VMEM = pl.BlockSpec(memory_space=pltpu.VMEM)
+SMEM = pl.BlockSpec(memory_space=pltpu.SMEM)
 
 
 def place(y, x, core):
@@ -146,13 +147,14 @@
     )(acts, grads, *pieces, grouping, *base)
 
 
-def owners_kernel(tokens, norms, onehot, dense, early, late):
+def owners_kernel(counts, tokens, norms, onehot, dense, early, late):
     for i, grouping in enumerate((early, late)):
         queries = slot_queries(grouping.shape, 2 * i)
         query_ids = lax.broadcasted_iota(jnp.int32, grouping.shape, 0)
         grouping[...] = (query_ids == queries).astype(jnp.float32).astype(jnp.bfloat16)
     rows = tokens.shape[1]
-    token = jnp.broadcast_to(tokens[...], (HALF, rows)).T
+    live = lax.broadcasted_iota(jnp.int32, (1, rows), 1) < counts[0, 0]
+    token = jnp.broadcast_to(jnp.where(live, tokens[...], -1), (HALF, rows)).T
     owner = lax.broadcasted_iota(jnp.int32, (rows, HALF), 1)
     for start in range(0, onehot.shape[1], HALF):
         hot = (token == owner + start).astype(jnp.float32).astype(jnp.bfloat16)
@@ -164,7 +166,7 @@
     dense[...] = part[:1] + part[1:2] + part[2:3]
 
 
-def owners(tokens, norms, shard_tokens, slots):
+def owners(counts, tokens, norms, shard_tokens, slots):
     rows = tokens.shape[1]
     return pl.pallas_call(
         owners_kernel,
@@ -174,14 +176,14 @@
             jax.ShapeDtypeStruct((QUERIES, slots // 2), jnp.bfloat16),
             jax.ShapeDtypeStruct((QUERIES, slots // 2), jnp.bfloat16),
         ),
-        in_specs=[VMEM] * 2,
+        in_specs=[SMEM, VMEM, VMEM],
         out_specs=(VMEM,) * 4,
         compiler_params=pltpu.CompilerParams(vmem_limit_bytes=3 << 20),
         cost_estimate=pl.CostEstimate(
             flops=2 * rows * shard_tokens * 128, bytes_accessed=8 << 20, transcendentals=0
         ),
         name="owners",
-    )(tokens, norms)
+    )(counts, tokens, norms)
 
 
 def scatter_kernel(mine, theirs, onehot, dense_norm, *rest):
@@ -259,14 +261,13 @@
     line = join(line)
     line, acts, grads = lax.optimization_barrier((line, acts, grads))
     pieces = [line] + [send(line, second_axis(-d)) for d in SECOND[1:]]
-    slots = acts.shape[0]
-    live = lax.broadcasted_iota(jnp.int32, (1, slots), 1) < counts[0, 0]
     norms = acts_norm * jnp.sum(jnp.square(grads.astype(jnp.float32)), 1)
     their_rows = turn(their_acts, their_grads)
     my_rows = turn(acts, grads)
     norms, *their_rows = lax.optimization_barrier((norms, *their_rows))
     onehot, dense_norm, early, late = owners(
-        jnp.where(live, row_token, -1),
+        counts,
+        row_token,
         norms[None, :],
         TOK_DEV * experts,
         SIDE * SIDE * shard.shape[0],

time: 52.1 us -> 52.3 us (level)
  transfers between devices with their start and end apart: 13 -> 13, of which waited for: 5 -> 5; matrix products, arithmetic and copies ran while one was open for 8% -> 9% of each run, Pallas kernels for 19% -> 19%
where the time goes in v7:
time: 52.3 us; the launch traced here: 52.2 us
  starting transfers between devices  23.3 us (45%)
  Pallas kernels  12.2 us (23%)
  waiting for transfers between devices  9.17 us (18%)
  other arithmetic  5.25 us (10%)
  local copies, waits for them, and re-layouts  1.42 us (3%)
  between operations  0.83 us (2%)
    ppermute x3, starting transfers between devices, exchange(): parts.append(lax.ppermute(block, 'expert', table))  11.4 us
    ppermute x9, starting transfers between devices, send(): return lax.ppermute(value, 'dp', table)  10.7 us
    pallas_call x4, Pallas kernels, row_scores(): pl.pallas_call(scores_kernel, out_shape=jax.ShapeDtypeStruct((QUERIES, ro...  6.01 us
    pallas_call x2, Pallas kernels, turn(): pl.pallas_call(turn_kernel, out_shape=tuple((jax.ShapeDtypeStruct(x.shape...  3.33 us
    ppermute x3, waiting for transfers between devices, exchange(): parts.append(lax.ppermute(block, 'expert', table))  3.25 us
    ppermute x9, waiting for transfers between devices, send(): return lax.ppermute(value, 'dp', table)  3.18 us
    reduce_sum x1, other arithmetic, local(): acts_norm = jnp.sum(jnp.square(acts.astype(jnp.float32)), 1)  3.07 us
    ppermute x1, waiting for transfers between devices, exchange(): lax.ppermute(give, 'expert', [(z, z ^ 1) for z in range(experts)])  2.74 us
  transfers between devices with their start and end apart: 13, of which 5 were waited for; matrix products, arithmetic and copies ran while one was open for 9% of the time, Pallas kernels for 19%

profile of v7, /device:TPU:6, one launch (start us, length us, event | category | flops | bytes accessed | tf_op | source)
XLA Modules:
  0.0 52.2 jit_solution(10904255955063209549)
XLA Ops:
  0.5 1.2 %pad_maximum_fusion.own = bf16[24,2816]{1,0:T(8,128)(2,1)S(1)} fusion(bf16[24,768]{1,0:T(8,128)(2,1)} %bitcast.25, bf16[24,2048]{1,0:T(8,128)(2,1)} %bitcast.23), kind=kLoop, calls=%fused_computation.2 | loop fusion | flops 270336 | bytes 270336 | tf_op jit(solution)/shard_map/concatenate | solution.py:256
  1.7 1.5 %collective-permute-start.2 = (bf16[24,2816]{1,0:T(8,128)(2,1)S(1)}, bf16[24,2816]{1,0:T(8,128)(2,1)S(1)}, u32[]{:S(2)}, u32[]{:S(2)}) collective-permute-start(bf16[24,2816]{1,0:T(8,128)(2,1)S(1)} %pad_maximum_fusion.own), channel_id=1, source_target_pairs={{0,4},{1,17},{2,6},{3,19},{4,0},{5,21},{6,2},{7,23},{8,12},{9,25},... | collective-permute-start | bytes 405512 | tf_op jit(solution)/shard_map/ppermute | solution.py:52
  3.2 2.1 %collective-permute-start = (bf16[24,2816]{1,0:T(8,128)(2,1)S(1)}, bf16[24,2816]{1,0:T(8,128)(2,1)S(1)}, u32[]{:S(2)}, u32[]{:S(2)}) collective-permute-start(bf16[24,2816]{1,0:T(8,128)(2,1)S(1)} %pad_maximum_fusion.own), channel_id=1, source_target_pairs={{0,2},{1,9},{2,4},{3,11},{4,6},{5,13},{6,0},{7,15},{8,10},{9,17},{... | collective-permute-start | bytes 405512 | tf_op jit(solution)/shard_map/ppermute | solution.py:52
  5.3 3.1 %multiply_reduce_fusion = f32[1024]{0:T(1024)S(1)} fusion(bf16[1,1024,2048]{2,1,0:T(8,128)(2,1)} %param.6), kind=kLoop, calls=%fused_computation | loop fusion | flops 6290432 | bytes 4198400 | tf_op jit(solution)/shard_map/reduce_sum | solution.py:259
  8.4 0.9 %collective-permute-done.before = bf16[24,2816]{1,0:T(8,128)(2,1)S(1)} collective-permute-done((bf16[24,2816]{1,0:T(8,128)(2,1)S(1)}, bf16[24,2816]{1,0:T(8,128)(2,1)S(1)}, u32[]{:S(2)}, u32[]{:S(2)}) %collective-permute-start) | collective-permute-done | bytes 135200 | tf_op jit(solution)/shard_map/ppermute | solution.py:52
  9.3 2.2 %collective-permute-done.1.after = bf16[24,2816]{1,0:T(8,128)(2,1)S(1)} collective-permute-done((bf16[24,2816]{1,0:T(8,128)(2,1)S(1)}, bf16[24,2816]{1,0:T(8,128)(2,1)S(1)}, u32[]{:S(2)}, u32[]{:S(2)}) %collective-permute-start.1) | collective-permute-done | bytes 135200 | tf_op jit(solution)/shard_map/ppermute | solution.py:52
  11.5 3.3 %collective-permute-start.7 = (bf16[96,2816]{1,0:T(8,128)(2,1)S(1)}, bf16[96,2816]{1,0:T(8,128)(2,1)S(1)}, u32[]{:S(2)}, u32[]{:S(2)}) collective-permute-start(bf16[96,2816]{1,0:T(8,128)(2,1)S(1)} %line.1.w0), channel_id=1, source_target_pairs={{0,16},{1,5},{2,18},{3,7},{4,20},{5,1},{6,22},{7,3},{8,24},{9,13},... | collective-permute-start | bytes 1622024 | tf_op jit(solution)/shard_map/ppermute | solution.py:52
  15.5 2.6 %collective-permute-start.4 = (bf16[96,2816]{1,0:T(8,128)(2,1)S(1)}, bf16[96,2816]{1,0:T(8,128)(2,1)S(1)}, u32[]{:S(2)}, u32[]{:S(2)}) collective-permute-start(bf16[96,2816]{1,0:T(8,128)(2,1)S(1)} %line.1.w0), channel_id=1, source_target_pairs={{0,24},{1,7},{2,26},{3,1},{4,28},{5,3},{6,30},{7,5},{8,0},{9,15},{... | collective-permute-start | bytes 1622024 | tf_op jit(solution)/shard_map/ppermute | solution.py:52
  18.7 1.4 %copy-done.1 = bf16[1,1024,768]{2,1,0:T(8,128)(2,1)S(1)} copy-done((bf16[1,1024,768]{2,1,0:T(8,128)(2,1)S(1)}, bf16[1,1024,768]{2,1,0:T(8,128)(2,1)}, u32[]{:S(2)}) %copy-start.1) | copy-done | bytes 1572888
  20.1 1.7 %turn.2 = (bf16[2048,1024]{1,0:T(8,128)(2,1)S(1)}, bf16[768,1024]{1,0:T(8,128)(2,1)S(1)}) custom-call(bf16[1024,2048]{1,0:T(8,128)(2,1)S(1)} %bitcast.18, bf16[1024,768]{1,0:T(8,128)(2,1)S(1)} %bitcast.20), custom_call_target="tpu_custom_call" | custom-call | bytes 6291456 | tf_op jit(solution)/shard_map/turn/pallas_call | solution.py:110
  22.2 1.7 %turn.3 = (bf16[2048,1024]{1,0:T(8,128)(2,1)S(1)}, bf16[768,1024]{1,0:T(8,128)(2,1)S(1)}) custom-call(bf16[1024,2048]{1,0:T(8,128)(2,1)S(1)} %collective-permute-done.5.acts, bf16[1024,768]{1,0:T(8,128)(2,1)S(1)} %collective-permute-done.6.grads), custom_call_target="tpu_custom_call" | custom-call | bytes 6291456 | tf_op jit(solution)/shard_map/turn/pallas_call | solution.py:110
  23.9 1.9 %owners.1 = (bf16[1024,2048]{1,0:T(8,128)(2,1)S(1)}, f32[1,2048]{1,0:T(1,128)S(1)}, bf16[24,192]{1,0:T(8,128)(2,1)S(1)}, bf16[24,192]{1,0:T(8,128)(2,1)S(1)}) custom-call(s32[1,1]{1,0:T(1,128)S(6)} %copy.10.counts, s32[1,1024]{1,0:T(1,128)S(1)} %copy-done.3, f32[1,1024]{1,0:T(1,128)S(1)} %bitcast.22), custom_call_target="tpu_custom_call" | custom-call | flops 536870912 | bytes 8388608 | tf_op jit(solution)/shard_map/owners/pallas_call | solution.py:171
  25.8 1.5 %early_scores.3.rest_0_ = f32[24,1024]{1,0:T(8,128)S(1)} custom-call(bf16[2048,1024]{1,0:T(8,128)(2,1)S(1)} %get-tuple-element.32.acts, bf16[768,1024]{1,0:T(8,128)(2,1)S(1)} %get-tuple-element.33.grads, bf16[96,2816]{1,0:T(8,128)(2,1)S(1)} %line.1.w0, bf16[96,2816]{1,0:T(8,128)(2,1)S(1)} %collective-permute-done.7.w1, ...), custom_call_target="tpu_custom_call" | custom-call | flops 1107296256 | bytes 7340032 | tf_op jit(solution)/shard_map/early_scores/pallas_call | solution.py:136
  27.3 1.5 %early_scores.2.rest_0_ = f32[24,1024]{1,0:T(8,128)S(1)} custom-call(bf16[2048,1024]{1,0:T(8,128)(2,1)S(1)} %get-tuple-element.40.acts, bf16[768,1024]{1,0:T(8,128)(2,1)S(1)} %get-tuple-element.41.grads, bf16[96,2816]{1,0:T(8,128)(2,1)S(1)} %line.1.w0, bf16[96,2816]{1,0:T(8,128)(2,1)S(1)} %collective-permute-done.7.w1, ...), custom_call_target="tpu_custom_call" | custom-call | flops 1107296256 | bytes 7340032 | tf_op jit(solution)/shard_map/early_scores/pallas_call | solution.py:136
  28.9 1.5 %late_scores.3 = f32[24,1024]{1,0:T(8,128)S(1)} custom-call(bf16[2048,1024]{1,0:T(8,128)(2,1)S(1)} %get-tuple-element.40.acts, bf16[768,1024]{1,0:T(8,128)(2,1)S(1)} %get-tuple-element.41.grads, bf16[96,2816]{1,0:T(8,128)(2,1)S(1)} %collective-permute-done.3.w0, bf16[96,2816]{1,0:T(8,128)(2,1)S(1)} %collective-permute-done.4.w1, ...), custom_call_target="tpu_custom_call" | custom-call | flops 1107296256 | bytes 7340032 | tf_op jit(solution)/shard_map/late_scores/pallas_call | solution.py:136
  30.5 1.5 %late_scores.2.mine = f32[24,1024]{1,0:T(8,128)S(1)} custom-call(bf16[2048,1024]{1,0:T(8,128)(2,1)S(1)} %get-tuple-element.32.acts, bf16[768,1024]{1,0:T(8,128)(2,1)S(1)} %get-tuple-element.33.grads, bf16[96,2816]{1,0:T(8,128)(2,1)S(1)} %collective-permute-done.3.w0, bf16[96,2816]{1,0:T(8,128)(2,1)S(1)} %collective-permute-done.4.w1, ...), custom_call_target="tpu_custom_call" | custom-call | flops 1107296256 | bytes 7340032 | tf_op jit(solution)/shard_map/late_scores/pallas_call | solution.py:136
  32.0 0.9 %scatter.1 = (f32[2,50,128]{2,1,0:T(8,128)S(1)}, f32[2,50,128]{2,1,0:T(8,128)S(1)}, f32[2,50,128]{2,1,0:T(8,128)S(1)}, f32[2,50,128]{2,1,0:T(8,128)S(1)}) custom-call(f32[24,1024]{1,0:T(8,128)S(1)} %late_scores.2.mine, f32[24,1024]{1,0:T(8,128)S(1)} %collective-permute-done.8.theirs, bf16[1024,2048]{1,0:T(8,128)(2,1)S(1)} %get-tuple-element.45.onehot, ...), custom_call_target="tpu_custom_call" | custom-call | tf_op jit(solution)/shard_map/scatter/pallas_call | solution.py:210
  32.9 7.3 %collective-permute-start.10 = (f32[2,50,128]{2,1,0:T(8,128)S(1)}, f32[2,50,128]{2,1,0:T(8,128)S(1)}, u32[]{:S(2)}, u32[]{:S(2)}) collective-permute-start(f32[2,50,128]{2,1,0:T(8,128)S(1)} %get-tuple-element.49), channel_id=1, source_target_pairs={{0,128},{32,160},{64,192},{96,224},{128,0},{160,32},{192,64},{224,... | collective-permute-start | bytes 153608 | tf_op jit(solution)/shard_map/ppermute | solution.py:248
  40.2 1.5 %collective-permute-start.11 = (f32[2,50,128]{2,1,0:T(8,128)S(1)}, f32[2,50,128]{2,1,0:T(8,128)S(1)}, u32[]{:S(2)}, u32[]{:S(2)}) collective-permute-start(f32[2,50,128]{2,1,0:T(8,128)S(1)} %get-tuple-element.50), channel_id=1, source_target_pairs={{0,64},{32,96},{64,128},{96,160},{128,192},{160,224},{192,0},{224,... | collective-permute-start | bytes 153608 | tf_op jit(solution)/shard_map/ppermute | solution.py:248
  41.7 2.6 %collective-permute-start.9 = (f32[2,50,128]{2,1,0:T(8,128)S(1)}, f32[2,50,128]{2,1,0:T(8,128)S(1)}, u32[]{:S(2)}, u32[]{:S(2)}) collective-permute-start(f32[2,50,128]{2,1,0:T(8,128)S(1)} %get-tuple-element.48), channel_id=1, source_target_pairs={{0,192},{32,224},{64,0},{96,32},{128,64},{160,96},{192,128},{224,1... | collective-permute-start | bytes 153608 | tf_op jit(solution)/shard_map/ppermute | solution.py:248
  44.3 2.5 %collective-permute-done.11.rest_2_ = f32[2,50,128]{2,1,0:T(8,128)S(1)} collective-permute-done((f32[2,50,128]{2,1,0:T(8,128)S(1)}, f32[2,50,128]{2,1,0:T(8,128)S(1)}, u32[]{:S(2)}, u32[]{:S(2)}) %collective-permute-start.11) | collective-permute-done | bytes 51232 | tf_op jit(solution)/shard_map/ppermute | solution.py:248
  46.8 0.8 %collective-permute-done.9.rest_0_ = f32[2,50,128]{2,1,0:T(8,128)S(1)} collective-permute-done((f32[2,50,128]{2,1,0:T(8,128)S(1)}, f32[2,50,128]{2,1,0:T(8,128)S(1)}, u32[]{:S(2)}, u32[]{:S(2)}) %collective-permute-start.9) | collective-permute-done | bytes 51232 | tf_op jit(solution)/shard_map/ppermute | solution.py:248
  47.6 1.2 %collective-permute-start.12 = (f32[50,128]{1,0:T(8,128)S(1)}, f32[50,128]{1,0:T(8,128)S(1)}, u32[]{:S(2)}, u32[]{:S(2)}) collective-permute-start(f32[50,128]{1,0:T(8,128)S(1)} %get-tuple-element.52), channel_id=1, source_target_pairs={{0,32},{32,0},{64,96},{96,64},{128,160},{160,128},{192,224},{224,1... | collective-permute-start | bytes 76808 | tf_op jit(solution)/shard_map/ppermute | solution.py:250
  48.8 2.7 %collective-permute-done.12 = f32[50,128]{1,0:T(8,128)S(1)} collective-permute-done((f32[50,128]{1,0:T(8,128)S(1)}, f32[50,128]{1,0:T(8,128)S(1)}, u32[]{:S(2)}, u32[]{:S(2)}) %collective-permute-start.12) | collective-permute-done | bytes 25632 | tf_op jit(solution)/shard_map/ppermute | solution.py:250
  (28 shorter events, 2.4 us)
Async XLA Ops:
  0.0 18.7 %copy-start = (bf16[1,1024,2048]{2,1,0:T(8,128)(2,1)S(1)}, bf16[1,1024,2048]{2,1,0:T(8,128)(2,1)}, u32[]{:S(2)}) copy-start(bf16[1,1024,2048]{2,1,0:T(8,128)(2,1)} %param.6) | copy-start | bytes 12582916
  0.0 22.2 %collective-permute-start.5 = (bf16[1024,2048]{1,0:T(8,128)(2,1)}, bf16[1024,2048]{1,0:T(8,128)(2,1)S(1)}, u32[]{:S(2)}, u32[]{:S(2)}) collective-permute-start(bf16[1024,2048]{1,0:T(8,128)(2,1)} %bitcast.17), channel_id=1, source_target_pairs={{0,1},{1,0},{2,3},{3,2},{4,5},{5,4},{6,7},{7,6},{8,9},{9,8},{10,11... | collective-permute-start | bytes 12582920 | tf_op jit(solution)/shard_map/ppermute | solution.py:52
  0.0 22.2 %collective-permute-start.6 = (bf16[1024,768]{1,0:T(8,128)(2,1)}, bf16[1024,768]{1,0:T(8,128)(2,1)S(1)}, u32[]{:S(2)}, u32[]{:S(2)}) collective-permute-start(bf16[1024,768]{1,0:T(8,128)(2,1)} %bitcast.19), channel_id=1, source_target_pairs={{0,1},{1,0},{2,3},{3,2},{4,5},{5,4},{6,7},{7,6},{8,9},{9,8},{10,11... | collective-permute-start | bytes 4718600 | tf_op jit(solution)/shard_map/ppermute | solution.py:52
  1.7 6.7 %collective-permute-start.2 = (bf16[24,2816]{1,0:T(8,128)(2,1)S(1)}, bf16[24,2816]{1,0:T(8,128)(2,1)S(1)}, u32[]{:S(2)}, u32[]{:S(2)}) collective-permute-start(bf16[24,2816]{1,0:T(8,128)(2,1)S(1)} %pad_maximum_fusion.own), channel_id=1, source_target_pairs={{0,4},{1,17},{2,6},{3,19},{4,0},{5,21},{6,2},{7,23},{8,12},{9,25},... | collective-permute-start | bytes 405512 | tf_op jit(solution)/shard_map/ppermute | solution.py:52
  3.2 6.1 %collective-permute-start = (bf16[24,2816]{1,0:T(8,128)(2,1)S(1)}, bf16[24,2816]{1,0:T(8,128)(2,1)S(1)}, u32[]{:S(2)}, u32[]{:S(2)}) collective-permute-start(bf16[24,2816]{1,0:T(8,128)(2,1)S(1)} %pad_maximum_fusion.own), channel_id=1, source_target_pairs={{0,2},{1,9},{2,4},{3,11},{4,6},{5,13},{6,0},{7,15},{8,10},{9,17},{... | collective-permute-start | bytes 405512 | tf_op jit(solution)/shard_map/ppermute | solution.py:52
  5.3 6.2 %collective-permute-start.1 = (bf16[24,2816]{1,0:T(8,128)(2,1)S(1)}, bf16[24,2816]{1,0:T(8,128)(2,1)S(1)}, u32[]{:S(2)}, u32[]{:S(2)}) collective-permute-start(bf16[24,2816]{1,0:T(8,128)(2,1)S(1)} %pad_maximum_fusion.own), channel_id=1, source_target_pairs={{0,6},{1,25},{2,0},{3,27},{4,2},{5,29},{6,4},{7,31},{8,14},{9,1},{... | collective-permute-start | bytes 405512 | tf_op jit(solution)/shard_map/ppermute | solution.py:52
  11.5 14.3 %collective-permute-start.7 = (bf16[96,2816]{1,0:T(8,128)(2,1)S(1)}, bf16[96,2816]{1,0:T(8,128)(2,1)S(1)}, u32[]{:S(2)}, u32[]{:S(2)}) collective-permute-start(bf16[96,2816]{1,0:T(8,128)(2,1)S(1)} %line.1.w0), channel_id=1, source_target_pairs={{0,16},{1,5},{2,18},{3,7},{4,20},{5,1},{6,22},{7,3},{8,24},{9,13},... | collective-permute-start | bytes 1622024 | tf_op jit(solution)/shard_map/ppermute | solution.py:52
  14.8 14.0 %collective-permute-start.3 = (bf16[96,2816]{1,0:T(8,128)(2,1)S(1)}, bf16[96,2816]{1,0:T(8,128)(2,1)S(1)}, u32[]{:S(2)}, u32[]{:S(2)}) collective-permute-start(bf16[96,2816]{1,0:T(8,128)(2,1)S(1)} %line.1.w0), channel_id=1, source_target_pairs={{0,8},{1,3},{2,10},{3,5},{4,12},{5,7},{6,14},{7,1},{8,16},{9,11},{... | collective-permute-start | bytes 1622024 | tf_op jit(solution)/shard_map/ppermute | solution.py:52
  15.5 13.4 %collective-permute-start.4 = (bf16[96,2816]{1,0:T(8,128)(2,1)S(1)}, bf16[96,2816]{1,0:T(8,128)(2,1)S(1)}, u32[]{:S(2)}, u32[]{:S(2)}) collective-permute-start(bf16[96,2816]{1,0:T(8,128)(2,1)S(1)} %line.1.w0), channel_id=1, source_target_pairs={{0,24},{1,7},{2,26},{3,1},{4,28},{5,3},{6,30},{7,5},{8,0},{9,15},{... | collective-permute-start | bytes 1622024 | tf_op jit(solution)/shard_map/ppermute | solution.py:52
  18.7 1.4 %copy-start.1 = (bf16[1,1024,768]{2,1,0:T(8,128)(2,1)S(1)}, bf16[1,1024,768]{2,1,0:T(8,128)(2,1)}, u32[]{:S(2)}) copy-start(bf16[1,1024,768]{2,1,0:T(8,128)(2,1)} %param.7) | copy-start | bytes 4718596
  20.1 1.7 %copy-start.2 = (bf16[1,1024,768]{2,1,0:T(8,128)(2,1)S(1)}, bf16[1,1024,768]{2,1,0:T(8,128)(2,1)}, u32[]{:S(2)}) copy-start(bf16[1,1024,768]{2,1,0:T(8,128)(2,1)} %param.7) | copy-start | bytes 4718596
  21.8 2.1 %copy-start.3 = (s32[1,1024]{1,0:T(1,128)S(1)}, s32[1,1024]{1,0:T(1,128)}, u32[]{:S(2)}) copy-start(s32[1,1024]{1,0:T(1,128)} %tokens.1) | copy-start | bytes 12292
  30.4 1.6 %collective-permute-start.8 = (f32[24,1024]{1,0:T(8,128)S(1)}, f32[24,1024]{1,0:T(8,128)S(1)}, u32[]{:S(2)}, u32[]{:S(2)}) collective-permute-start(f32[24,1024]{1,0:T(8,128)S(1)} %late_scores.3), channel_id=1, source_target_pairs={{0,1},{1,0},{2,3},{3,2},{4,5},{5,4},{6,7},{7,6},{8,9},{9,8},{10,11... | collective-permute-start | bytes 294920 | tf_op jit(solution)/shard_map/ppermute | solution.py:52
  32.9 11.4 %collective-permute-start.10 = (f32[2,50,128]{2,1,0:T(8,128)S(1)}, f32[2,50,128]{2,1,0:T(8,128)S(1)}, u32[]{:S(2)}, u32[]{:S(2)}) collective-permute-start(f32[2,50,128]{2,1,0:T(8,128)S(1)} %get-tuple-element.49), channel_id=1, source_target_pairs={{0,128},{32,160},{64,192},{96,224},{128,0},{160,32},{192,64},{224,... | collective-permute-start | bytes 153608 | tf_op jit(solution)/shard_map/ppermute | solution.py:248
  40.2 6.6 %collective-permute-start.11 = (f32[2,50,128]{2,1,0:T(8,128)S(1)}, f32[2,50,128]{2,1,0:T(8,128)S(1)}, u32[]{:S(2)}, u32[]{:S(2)}) collective-permute-start(f32[2,50,128]{2,1,0:T(8,128)S(1)} %get-tuple-element.50), channel_id=1, source_target_pairs={{0,64},{32,96},{64,128},{96,160},{128,192},{160,224},{192,0},{224,... | collective-permute-start | bytes 153608 | tf_op jit(solution)/shard_map/ppermute | solution.py:248
  41.7 5.9 %collective-permute-start.9 = (f32[2,50,128]{2,1,0:T(8,128)S(1)}, f32[2,50,128]{2,1,0:T(8,128)S(1)}, u32[]{:S(2)}, u32[]{:S(2)}) collective-permute-start(f32[2,50,128]{2,1,0:T(8,128)S(1)} %get-tuple-element.48), channel_id=1, source_target_pairs={{0,192},{32,224},{64,0},{96,32},{128,64},{160,96},{192,128},{224,1... | collective-permute-start | bytes 153608 | tf_op jit(solution)/shard_map/ppermute | solution.py:248
  47.6 4.0 %collective-permute-start.12 = (f32[50,128]{1,0:T(8,128)S(1)}, f32[50,128]{1,0:T(8,128)S(1)}, u32[]{:S(2)}, u32[]{:S(2)}) collective-permute-start(f32[50,128]{1,0:T(8,128)S(1)} %get-tuple-element.52), channel_id=1, source_target_pairs={{0,32},{32,0},{64,96},{96,64},{128,160},{160,128},{192,224},{224,1... | collective-permute-start | bytes 76808 | tf_op jit(solution)/shard_map/ppermute | solution.py:250

commit v8 on v7

--- a/solution.py
+++ b/solution.py
@@ -100,22 +100,23 @@
     )(*shards)
 
 
-def turn_kernel(acts, grads, acts_out, grads_out):
-    for rows, turned in ((acts, acts_out), (grads, grads_out)):
-        for start in range(0, rows.shape[1], TOK_DEV):
-            turned[start : start + TOK_DEV, :] = rows[:, start : start + TOK_DEV].T
-
-
-def turn(acts, grads):
+def turn_kernel(rows, turned):
+    for start in range(0, rows.shape[1], TOK_DEV):
+        turned[start : start + TOK_DEV, :] = rows[:, start : start + TOK_DEV].T
+
+
+def turn(rows):
     return pl.pallas_call(
         turn_kernel,
-        out_shape=tuple(jax.ShapeDtypeStruct(x.shape[::-1], x.dtype) for x in (acts, grads)),
-        in_specs=[VMEM, VMEM],
-        out_specs=(VMEM, VMEM),
+        out_shape=jax.ShapeDtypeStruct(rows.shape[::-1], rows.dtype),
+        in_specs=[VMEM],
+        out_specs=VMEM,
         compiler_params=pltpu.CompilerParams(vmem_limit_bytes=2 << 20),
-        cost_estimate=pl.CostEstimate(flops=0, bytes_accessed=6 << 20, transcendentals=0),
+        cost_estimate=pl.CostEstimate(
+            flops=0, bytes_accessed=4 * rows.size, transcendentals=0
+        ),
         name="turn",
-    )(acts, grads)
+    )(rows)
 
 
 def scores_kernel(acts, grads, w0, w1, grouping, *rest):
@@ -262,8 +263,8 @@
     line, acts, grads = lax.optimization_barrier((line, acts, grads))
     pieces = [line] + [send(line, second_axis(-d)) for d in SECOND[1:]]
     norms = acts_norm * jnp.sum(jnp.square(grads.astype(jnp.float32)), 1)
-    their_rows = turn(their_acts, their_grads)
-    my_rows = turn(acts, grads)
+    their_rows = turn(their_acts), turn(their_grads)
+    my_rows = turn(acts), turn(grads)
     norms, *their_rows = lax.optimization_barrier((norms, *their_rows))
     onehot, dense_norm, early, late = owners(
         counts,

time: 52.3 us -> 51.9 us (level)
  local copies, waits for them, and re-layouts: 1.42 us -> 0.02 us
  waiting for transfers between devices: 9.17 us -> 10.2 us
    unnamed x8 -> x6, local copies, waits for them, and re-layouts: 1.42 us -> 0.02 us
    ppermute x9, waiting for transfers between devices: 3.18 us -> 4.29 us  [send(): return lax.ppermute(value, 'dp', table)]
    pallas_call x2 -> x4, Pallas kernels: 3.33 us -> 3.43 us  [turn(): pl.pallas_call(turn_kernel, out_shape=jax.ShapeDtypeStruct(rows.shape[::-...]
  transfers between devices with their start and end apart: 13 -> 13, of which waited for: 5 -> 7; matrix products, arithmetic and copies ran while one was open for 9% -> 8% of each run, Pallas kernels for 19% -> 19%
where the time goes in v8:
time: 51.9 us; the launch traced here: 51.7 us
  starting transfers between devices  23.4 us (45%)
  Pallas kernels  12.3 us (24%)
  waiting for transfers between devices  10.2 us (20%)
  other arithmetic  5 us (10%)
  between operations  0.83 us (2%)
    ppermute x3, starting transfers between devices, exchange(): parts.append(lax.ppermute(block, 'expert', table))  11.4 us
    ppermute x9, starting transfers between devices, send(): return lax.ppermute(value, 'dp', table)  10.7 us
    pallas_call x4, Pallas kernels, row_scores(): pl.pallas_call(scores_kernel, out_shape=jax.ShapeDtypeStruct((QUERIES, ro...  6.02 us
    ppermute x9, waiting for transfers between devices, send(): return lax.ppermute(value, 'dp', table)  4.29 us
    pallas_call x4, Pallas kernels, turn(): pl.pallas_call(turn_kernel, out_shape=jax.ShapeDtypeStruct(rows.shape[::-...  3.43 us
    ppermute x3, waiting for transfers between devices, exchange(): parts.append(lax.ppermute(block, 'expert', table))  3.22 us
    reduce_sum x1, other arithmetic, local(): acts_norm = jnp.sum(jnp.square(acts.astype(jnp.float32)), 1)  3.07 us
    ppermute x1, waiting for transfers between devices, exchange(): lax.ppermute(give, 'expert', [(z, z ^ 1) for z in range(experts)])  2.72 us
  transfers between devices with their start and end apart: 13, of which 7 were waited for; matrix products, arithmetic and copies ran while one was open for 8% of the time, Pallas kernels for 19%

profile of v8, /device:TPU:6, one launch (start us, length us, event | category | flops | bytes accessed | tf_op | source)
XLA Modules:
  0.0 51.7 jit_solution(2740184103770141893)
XLA Ops:
  0.5 0.9 %pad_maximum_fusion.own = bf16[24,2816]{1,0:T(8,128)(2,1)S(1)} fusion(bf16[24,768]{1,0:T(8,128)(2,1)} %bitcast.25, bf16[24,2048]{1,0:T(8,128)(2,1)} %bitcast.23), kind=kLoop, calls=%fused_computation.2 | loop fusion | flops 270336 | bytes 270336 | tf_op jit(solution)/shard_map/concatenate | solution.py:257
  1.5 1.5 %collective-permute-start.2 = (bf16[24,2816]{1,0:T(8,128)(2,1)S(1)}, bf16[24,2816]{1,0:T(8,128)(2,1)S(1)}, u32[]{:S(2)}, u32[]{:S(2)}) collective-permute-start(bf16[24,2816]{1,0:T(8,128)(2,1)S(1)} %pad_maximum_fusion.own), channel_id=1, source_target_pairs={{0,4},{1,17},{2,6},{3,19},{4,0},{5,21},{6,2},{7,23},{8,12},{9,25},... | collective-permute-start | bytes 405512 | tf_op jit(solution)/shard_map/ppermute | solution.py:52
  2.9 2.1 %collective-permute-start = (bf16[24,2816]{1,0:T(8,128)(2,1)S(1)}, bf16[24,2816]{1,0:T(8,128)(2,1)S(1)}, u32[]{:S(2)}, u32[]{:S(2)}) collective-permute-start(bf16[24,2816]{1,0:T(8,128)(2,1)S(1)} %pad_maximum_fusion.own), channel_id=1, source_target_pairs={{0,2},{1,9},{2,4},{3,11},{4,6},{5,13},{6,0},{7,15},{8,10},{9,17},{... | collective-permute-start | bytes 405512 | tf_op jit(solution)/shard_map/ppermute | solution.py:52
  5.0 3.1 %multiply_reduce_fusion = f32[1024]{0:T(1024)S(1)} fusion(bf16[1,1024,2048]{2,1,0:T(8,128)(2,1)} %param.6), kind=kLoop, calls=%fused_computation | loop fusion | flops 6290432 | bytes 4198400 | tf_op jit(solution)/shard_map/reduce_sum | solution.py:260
  8.1 0.9 %collective-permute-done.before = bf16[24,2816]{1,0:T(8,128)(2,1)S(1)} collective-permute-done((bf16[24,2816]{1,0:T(8,128)(2,1)S(1)}, bf16[24,2816]{1,0:T(8,128)(2,1)S(1)}, u32[]{:S(2)}, u32[]{:S(2)}) %collective-permute-start) | collective-permute-done | bytes 135200 | tf_op jit(solution)/shard_map/ppermute | solution.py:52
  9.0 2.2 %collective-permute-done.1.after = bf16[24,2816]{1,0:T(8,128)(2,1)S(1)} collective-permute-done((bf16[24,2816]{1,0:T(8,128)(2,1)S(1)}, bf16[24,2816]{1,0:T(8,128)(2,1)S(1)}, u32[]{:S(2)}, u32[]{:S(2)}) %collective-permute-start.1) | collective-permute-done | bytes 135200 | tf_op jit(solution)/shard_map/ppermute | solution.py:52
  11.3 3.3 %collective-permute-start.7 = (bf16[96,2816]{1,0:T(8,128)(2,1)S(1)}, bf16[96,2816]{1,0:T(8,128)(2,1)S(1)}, u32[]{:S(2)}, u32[]{:S(2)}) collective-permute-start(bf16[96,2816]{1,0:T(8,128)(2,1)S(1)} %line.1.w0), channel_id=1, source_target_pairs={{0,16},{1,5},{2,18},{3,7},{4,20},{5,1},{6,22},{7,3},{8,24},{9,13},... | collective-permute-start | bytes 1622024 | tf_op jit(solution)/shard_map/ppermute | solution.py:52
  15.3 2.6 %collective-permute-start.4 = (bf16[96,2816]{1,0:T(8,128)(2,1)S(1)}, bf16[96,2816]{1,0:T(8,128)(2,1)S(1)}, u32[]{:S(2)}, u32[]{:S(2)}) collective-permute-start(bf16[96,2816]{1,0:T(8,128)(2,1)S(1)} %line.1.w0), channel_id=1, source_target_pairs={{0,24},{1,7},{2,26},{3,1},{4,28},{5,3},{6,30},{7,5},{8,0},{9,15},{... | collective-permute-start | bytes 1622024 | tf_op jit(solution)/shard_map/ppermute | solution.py:52
  19.0 1.2 %turn.4.acts = bf16[2048,1024]{1,0:T(8,128)(2,1)S(1)} custom-call(bf16[1024,2048]{1,0:T(8,128)(2,1)S(1)} %bitcast.18), custom_call_target="tpu_custom_call" | custom-call | bytes 8388608 | tf_op jit(solution)/shard_map/turn/pallas_call | solution.py:109
  21.1 1.2 %turn.6.acts = bf16[2048,1024]{1,0:T(8,128)(2,1)S(1)} custom-call(bf16[1024,2048]{1,0:T(8,128)(2,1)S(1)} %collective-permute-done.5.rows), custom_call_target="tpu_custom_call" | custom-call | bytes 8388608 | tf_op jit(solution)/shard_map/turn/pallas_call | solution.py:109
  22.4 1.9 %owners.1 = (bf16[1024,2048]{1,0:T(8,128)(2,1)S(1)}, f32[1,2048]{1,0:T(1,128)S(1)}, bf16[24,192]{1,0:T(8,128)(2,1)S(1)}, bf16[24,192]{1,0:T(8,128)(2,1)S(1)}) custom-call(s32[1,1]{1,0:T(1,128)S(6)} %copy.10.counts, s32[1,1024]{1,0:T(1,128)S(1)} %copy-done.2, f32[1,1024]{1,0:T(1,128)S(1)} %bitcast.22), custom_call_target="tpu_custom_call" | custom-call | flops 536870912 | bytes 8388608 | tf_op jit(solution)/shard_map/owners/pallas_call | solution.py:172
  24.3 1.5 %early_scores.3.rest_0_ = f32[24,1024]{1,0:T(8,128)S(1)} custom-call(bf16[2048,1024]{1,0:T(8,128)(2,1)S(1)} %turn.4.acts, bf16[768,1024]{1,0:T(8,128)(2,1)S(1)} %turn.5.grads, bf16[96,2816]{1,0:T(8,128)(2,1)S(1)} %line.1.w0, bf16[96,2816]{1,0:T(8,128)(2,1)S(1)} %collective-permute-done.7.w1, bf16[24,192]{1,0:T(8,128)(2,1)S(1)} %get-tuple-element.34.grouping), custom_call_target="tpu_custom_call" | custom-call | flops 1107296256 | bytes 7340032 | tf_op jit(solution)/shard_map/early_scores/pallas_call | solution.py:137
  25.8 1.5 %early_scores.2.rest_0_ = f32[24,1024]{1,0:T(8,128)S(1)} custom-call(bf16[2048,1024]{1,0:T(8,128)(2,1)S(1)} %turn.6.acts, bf16[768,1024]{1,0:T(8,128)(2,1)S(1)} %turn.7.grads, bf16[96,2816]{1,0:T(8,128)(2,1)S(1)} %line.1.w0, bf16[96,2816]{1,0:T(8,128)(2,1)S(1)} %collective-permute-done.7.w1, bf16[24,192]{1,0:T(8,128)(2,1)S(1)} %get-tuple-element.34.grouping), custom_call_target="tpu_custom_call" | custom-call | flops 1107296256 | bytes 7340032 | tf_op jit(solution)/shard_map/early_scores/pallas_call | solution.py:137
  27.3 0.7 %collective-permute-done.3.w0 = bf16[96,2816]{1,0:T(8,128)(2,1)S(1)} collective-permute-done((bf16[96,2816]{1,0:T(8,128)(2,1)S(1)}, bf16[96,2816]{1,0:T(8,128)(2,1)S(1)}, u32[]{:S(2)}, u32[]{:S(2)}) %collective-permute-start.3) | collective-permute-done | bytes 540704 | tf_op jit(solution)/shard_map/ppermute | solution.py:52
  28.4 1.5 %late_scores.3 = f32[24,1024]{1,0:T(8,128)S(1)} custom-call(bf16[2048,1024]{1,0:T(8,128)(2,1)S(1)} %turn.6.acts, bf16[768,1024]{1,0:T(8,128)(2,1)S(1)} %turn.7.grads, bf16[96,2816]{1,0:T(8,128)(2,1)S(1)} %collective-permute-done.3.w0, bf16[96,2816]{1,0:T(8,128)(2,1)S(1)} %collective-permute-done.4.w1, bf16[24,192]{1,0:T(8,128)(2,1)S(1)} %get-tuple-element.31.grouping, ...), custom_call_target="tpu_custom_call" | custom-call | flops 1107296256 | bytes 7340032 | tf_op jit(solution)/shard_map/late_scores/pallas_call | solution.py:137
  30.0 1.5 %late_scores.2.mine = f32[24,1024]{1,0:T(8,128)S(1)} custom-call(bf16[2048,1024]{1,0:T(8,128)(2,1)S(1)} %turn.4.acts, bf16[768,1024]{1,0:T(8,128)(2,1)S(1)} %turn.5.grads, bf16[96,2816]{1,0:T(8,128)(2,1)S(1)} %collective-permute-done.3.w0, bf16[96,2816]{1,0:T(8,128)(2,1)S(1)} %collective-permute-done.4.w1, bf16[24,192]{1,0:T(8,128)(2,1)S(1)} %get-tuple-element.31.grouping, ...), custom_call_target="tpu_custom_call" | custom-call | flops 1107296256 | bytes 7340032 | tf_op jit(solution)/shard_map/late_scores/pallas_call | solution.py:137
  31.6 0.9 %scatter.1 = (f32[2,50,128]{2,1,0:T(8,128)S(1)}, f32[2,50,128]{2,1,0:T(8,128)S(1)}, f32[2,50,128]{2,1,0:T(8,128)S(1)}, f32[2,50,128]{2,1,0:T(8,128)S(1)}) custom-call(f32[24,1024]{1,0:T(8,128)S(1)} %late_scores.2.mine, f32[24,1024]{1,0:T(8,128)S(1)} %collective-permute-done.8.theirs, bf16[1024,2048]{1,0:T(8,128)(2,1)S(1)} %get-tuple-element.37.onehot, ...), custom_call_target="tpu_custom_call" | custom-call | tf_op jit(solution)/shard_map/scatter/pallas_call | solution.py:211
  32.5 7.3 %collective-permute-start.10 = (f32[2,50,128]{2,1,0:T(8,128)S(1)}, f32[2,50,128]{2,1,0:T(8,128)S(1)}, u32[]{:S(2)}, u32[]{:S(2)}) collective-permute-start(f32[2,50,128]{2,1,0:T(8,128)S(1)} %get-tuple-element.41), channel_id=1, source_target_pairs={{0,128},{32,160},{64,192},{96,224},{128,0},{160,32},{192,64},{224,... | collective-permute-start | bytes 153608 | tf_op jit(solution)/shard_map/ppermute | solution.py:249
  39.7 1.5 %collective-permute-start.11 = (f32[2,50,128]{2,1,0:T(8,128)S(1)}, f32[2,50,128]{2,1,0:T(8,128)S(1)}, u32[]{:S(2)}, u32[]{:S(2)}) collective-permute-start(f32[2,50,128]{2,1,0:T(8,128)S(1)} %get-tuple-element.42), channel_id=1, source_target_pairs={{0,64},{32,96},{64,128},{96,160},{128,192},{160,224},{192,0},{224,... | collective-permute-start | bytes 153608 | tf_op jit(solution)/shard_map/ppermute | solution.py:249
  41.2 2.7 %collective-permute-start.9 = (f32[2,50,128]{2,1,0:T(8,128)S(1)}, f32[2,50,128]{2,1,0:T(8,128)S(1)}, u32[]{:S(2)}, u32[]{:S(2)}) collective-permute-start(f32[2,50,128]{2,1,0:T(8,128)S(1)} %get-tuple-element.40), channel_id=1, source_target_pairs={{0,192},{32,224},{64,0},{96,32},{128,64},{160,96},{192,128},{224,1... | collective-permute-start | bytes 153608 | tf_op jit(solution)/shard_map/ppermute | solution.py:249
  43.9 2.4 %collective-permute-done.11.rest_2_ = f32[2,50,128]{2,1,0:T(8,128)S(1)} collective-permute-done((f32[2,50,128]{2,1,0:T(8,128)S(1)}, f32[2,50,128]{2,1,0:T(8,128)S(1)}, u32[]{:S(2)}, u32[]{:S(2)}) %collective-permute-start.11) | collective-permute-done | bytes 51232 | tf_op jit(solution)/shard_map/ppermute | solution.py:249
  46.3 0.8 %collective-permute-done.9.rest_0_ = f32[2,50,128]{2,1,0:T(8,128)S(1)} collective-permute-done((f32[2,50,128]{2,1,0:T(8,128)S(1)}, f32[2,50,128]{2,1,0:T(8,128)S(1)}, u32[]{:S(2)}, u32[]{:S(2)}) %collective-permute-start.9) | collective-permute-done | bytes 51232 | tf_op jit(solution)/shard_map/ppermute | solution.py:249
  47.1 1.2 %collective-permute-start.12 = (f32[50,128]{1,0:T(8,128)S(1)}, f32[50,128]{1,0:T(8,128)S(1)}, u32[]{:S(2)}, u32[]{:S(2)}) collective-permute-start(f32[50,128]{1,0:T(8,128)S(1)} %get-tuple-element.44), channel_id=1, source_target_pairs={{0,32},{32,0},{64,96},{96,64},{128,160},{160,128},{192,224},{224,1... | collective-permute-start | bytes 76808 | tf_op jit(solution)/shard_map/ppermute | solution.py:251
  48.4 2.7 %collective-permute-done.12 = f32[50,128]{1,0:T(8,128)S(1)} collective-permute-done((f32[50,128]{1,0:T(8,128)S(1)}, f32[50,128]{1,0:T(8,128)S(1)}, u32[]{:S(2)}, u32[]{:S(2)}) %collective-permute-start.12) | collective-permute-done | bytes 25632 | tf_op jit(solution)/shard_map/ppermute | solution.py:251
  (28 shorter events, 3.8 us)
Async XLA Ops:
  0.0 18.5 %copy-start.1 = (bf16[1,1024,768]{2,1,0:T(8,128)(2,1)S(1)}, bf16[1,1024,768]{2,1,0:T(8,128)(2,1)}, u32[]{:S(2)}) copy-start(bf16[1,1024,768]{2,1,0:T(8,128)(2,1)} %param.7) | copy-start | bytes 4718596
  0.0 21.1 %collective-permute-start.5 = (bf16[1024,2048]{1,0:T(8,128)(2,1)}, bf16[1024,2048]{1,0:T(8,128)(2,1)S(1)}, u32[]{:S(2)}, u32[]{:S(2)}) collective-permute-start(bf16[1024,2048]{1,0:T(8,128)(2,1)} %bitcast.17), channel_id=1, source_target_pairs={{0,1},{1,0},{2,3},{3,2},{4,5},{5,4},{6,7},{7,6},{8,9},{9,8},{10,11... | collective-permute-start | bytes 12582920 | tf_op jit(solution)/shard_map/ppermute | solution.py:52
  0.0 20.6 %collective-permute-start.6 = (bf16[1024,768]{1,0:T(8,128)(2,1)}, bf16[1024,768]{1,0:T(8,128)(2,1)S(1)}, u32[]{:S(2)}, u32[]{:S(2)}) collective-permute-start(bf16[1024,768]{1,0:T(8,128)(2,1)} %bitcast.19), channel_id=1, source_target_pairs={{0,1},{1,0},{2,3},{3,2},{4,5},{5,4},{6,7},{7,6},{8,9},{9,8},{10,11... | collective-permute-start | bytes 4718600 | tf_op jit(solution)/shard_map/ppermute | solution.py:52
  1.4 17.5 %copy-start = (bf16[1,1024,2048]{2,1,0:T(8,128)(2,1)S(1)}, bf16[1,1024,2048]{2,1,0:T(8,128)(2,1)}, u32[]{:S(2)}) copy-start(bf16[1,1024,2048]{2,1,0:T(8,128)(2,1)} %param.6) | copy-start | bytes 12582916
  1.5 6.7 %collective-permute-start.2 = (bf16[24,2816]{1,0:T(8,128)(2,1)S(1)}, bf16[24,2816]{1,0:T(8,128)(2,1)S(1)}, u32[]{:S(2)}, u32[]{:S(2)}) collective-permute-start(bf16[24,2816]{1,0:T(8,128)(2,1)S(1)} %pad_maximum_fusion.own), channel_id=1, source_target_pairs={{0,4},{1,17},{2,6},{3,19},{4,0},{5,21},{6,2},{7,23},{8,12},{9,25},... | collective-permute-start | bytes 405512 | tf_op jit(solution)/shard_map/ppermute | solution.py:52
  2.9 6.1 %collective-permute-start = (bf16[24,2816]{1,0:T(8,128)(2,1)S(1)}, bf16[24,2816]{1,0:T(8,128)(2,1)S(1)}, u32[]{:S(2)}, u32[]{:S(2)}) collective-permute-start(bf16[24,2816]{1,0:T(8,128)(2,1)S(1)} %pad_maximum_fusion.own), channel_id=1, source_target_pairs={{0,2},{1,9},{2,4},{3,11},{4,6},{5,13},{6,0},{7,15},{8,10},{9,17},{... | collective-permute-start | bytes 405512 | tf_op jit(solution)/shard_map/ppermute | solution.py:52
  5.0 6.2 %collective-permute-start.1 = (bf16[24,2816]{1,0:T(8,128)(2,1)S(1)}, bf16[24,2816]{1,0:T(8,128)(2,1)S(1)}, u32[]{:S(2)}, u32[]{:S(2)}) collective-permute-start(bf16[24,2816]{1,0:T(8,128)(2,1)S(1)} %pad_maximum_fusion.own), channel_id=1, source_target_pairs={{0,6},{1,25},{2,0},{3,27},{4,2},{5,29},{6,4},{7,31},{8,14},{9,1},{... | collective-permute-start | bytes 405512 | tf_op jit(solution)/shard_map/ppermute | solution.py:52
  11.3 13.0 %collective-permute-start.7 = (bf16[96,2816]{1,0:T(8,128)(2,1)S(1)}, bf16[96,2816]{1,0:T(8,128)(2,1)S(1)}, u32[]{:S(2)}, u32[]{:S(2)}) collective-permute-start(bf16[96,2816]{1,0:T(8,128)(2,1)S(1)} %line.1.w0), channel_id=1, source_target_pairs={{0,16},{1,5},{2,18},{3,7},{4,20},{5,1},{6,22},{7,3},{8,24},{9,13},... | collective-permute-start | bytes 1622024 | tf_op jit(solution)/shard_map/ppermute | solution.py:52
  14.6 13.5 %collective-permute-start.3 = (bf16[96,2816]{1,0:T(8,128)(2,1)S(1)}, bf16[96,2816]{1,0:T(8,128)(2,1)S(1)}, u32[]{:S(2)}, u32[]{:S(2)}) collective-permute-start(bf16[96,2816]{1,0:T(8,128)(2,1)S(1)} %line.1.w0), channel_id=1, source_target_pairs={{0,8},{1,3},{2,10},{3,5},{4,12},{5,7},{6,14},{7,1},{8,16},{9,11},{... | collective-permute-start | bytes 1622024 | tf_op jit(solution)/shard_map/ppermute | solution.py:52
  15.3 13.2 %collective-permute-start.4 = (bf16[96,2816]{1,0:T(8,128)(2,1)S(1)}, bf16[96,2816]{1,0:T(8,128)(2,1)S(1)}, u32[]{:S(2)}, u32[]{:S(2)}) collective-permute-start(bf16[96,2816]{1,0:T(8,128)(2,1)S(1)} %line.1.w0), channel_id=1, source_target_pairs={{0,24},{1,7},{2,26},{3,1},{4,28},{5,3},{6,30},{7,5},{8,0},{9,15},{... | collective-permute-start | bytes 1622024 | tf_op jit(solution)/shard_map/ppermute | solution.py:52
  21.1 1.3 %copy-start.2 = (s32[1,1024]{1,0:T(1,128)S(1)}, s32[1,1024]{1,0:T(1,128)}, u32[]{:S(2)}) copy-start(s32[1,1024]{1,0:T(1,128)} %tokens.1) | copy-start | bytes 12292
  29.9 1.6 %collective-permute-start.8 = (f32[24,1024]{1,0:T(8,128)S(1)}, f32[24,1024]{1,0:T(8,128)S(1)}, u32[]{:S(2)}, u32[]{:S(2)}) collective-permute-start(f32[24,1024]{1,0:T(8,128)S(1)} %late_scores.3), channel_id=1, source_target_pairs={{0,1},{1,0},{2,3},{3,2},{4,5},{5,4},{6,7},{7,6},{8,9},{9,8},{10,11... | collective-permute-start | bytes 294920 | tf_op jit(solution)/shard_map/ppermute | solution.py:52
  32.5 11.4 %collective-permute-start.10 = (f32[2,50,128]{2,1,0:T(8,128)S(1)}, f32[2,50,128]{2,1,0:T(8,128)S(1)}, u32[]{:S(2)}, u32[]{:S(2)}) collective-permute-start(f32[2,50,128]{2,1,0:T(8,128)S(1)} %get-tuple-element.41), channel_id=1, source_target_pairs={{0,128},{32,160},{64,192},{96,224},{128,0},{160,32},{192,64},{224,... | collective-permute-start | bytes 153608 | tf_op jit(solution)/shard_map/ppermute | solution.py:249
  39.7 6.6 %collective-permute-start.11 = (f32[2,50,128]{2,1,0:T(8,128)S(1)}, f32[2,50,128]{2,1,0:T(8,128)S(1)}, u32[]{:S(2)}, u32[]{:S(2)}) collective-permute-start(f32[2,50,128]{2,1,0:T(8,128)S(1)} %get-tuple-element.42), channel_id=1, source_target_pairs={{0,64},{32,96},{64,128},{96,160},{128,192},{160,224},{192,0},{224,... | collective-permute-start | bytes 153608 | tf_op jit(solution)/shard_map/ppermute | solution.py:249
  41.2 5.9 %collective-permute-start.9 = (f32[2,50,128]{2,1,0:T(8,128)S(1)}, f32[2,50,128]{2,1,0:T(8,128)S(1)}, u32[]{:S(2)}, u32[]{:S(2)}) collective-permute-start(f32[2,50,128]{2,1,0:T(8,128)S(1)} %get-tuple-element.40), channel_id=1, source_target_pairs={{0,192},{32,224},{64,0},{96,32},{128,64},{160,96},{192,128},{224,1... | collective-permute-start | bytes 153608 | tf_op jit(solution)/shard_map/ppermute | solution.py:249
  47.1 4.0 %collective-permute-start.12 = (f32[50,128]{1,0:T(8,128)S(1)}, f32[50,128]{1,0:T(8,128)S(1)}, u32[]{:S(2)}, u32[]{:S(2)}) collective-permute-start(f32[50,128]{1,0:T(8,128)S(1)} %get-tuple-element.44), channel_id=1, source_target_pairs={{0,32},{32,0},{64,96},{96,64},{128,160},{160,128},{192,224},{224,1... | collective-permute-start | bytes 76808 | tf_op jit(solution)/shard_map/ppermute | solution.py:251
